TPU v7x, 256 devices: a whole 4x4x8 slice. The times are simulated.
256 devices in a mesh: tx: 4 (over x), ty: 8 (over y, core), pos: 8 (over z).
Axes of the slice: x: 4, y: 4, z: 8, core: 2. Of those that a mesh axis runs over, the one named last changes fastest.
Arguments:
- obj: float32 [2, 3072, 6144], P(None, 'tx', 'ty'), may hold values from -5 to 5
- probe: float32 [4, 2, 128, 128], replicated, may hold values from -6 to 6
- measured: bfloat16 [4096, 128, 128], P(('tx', 'ty', 'pos')), may hold values from 0 to 4
- tile_of: int32 [4096, 1], replicated, may hold values from 0 to 31; in each aligned block of 16 rows (0 to 15, 16 to 31, ...) at most 2 rows name the same one
- inner: int32 [4096, 2], replicated, may hold values from 0 to 640
Outputs:
- obj_grad: float32 [2, 3072, 6144], P(None, ('tx', 'pos'), 'ty')
- probe_grad: float32 [4, 2, 128, 128], replicated
- misfit: float32 [4096], P(('tx', 'ty', 'pos'))
Inputs may be any that keep to these rules, and one draw needn't show every extreme that they name: `tile_of`: tile number: tile row index times the number of tile columns plus tile column index; among the 16 positions of one device no tile is named more than 2 times.
All inputs are finite; a program needn't handle non-finite values.
Results may differ from a plain program's by a relative error of at most 0.00075.
The roundings to bfloat16 on the way count: a program that leaves them out, or rounds other values in their place, can miss the bound.
Values may be sent and summed in bfloat16 or wider, within the bound.
No kernel may reach another device: no remote copies, remote signals or barrier semaphores. Data moves between devices by JAX's collectives and lax.ppermute only.
A program may use at most 128 MiB of HBM per device.

v0:
```python
import jax
import jax.numpy as jnp
from jax import lax
from jax.sharding import PartitionSpec as P

CAP = 2


def dft_tables(width):
    counter = jnp.arange(width, dtype=jnp.int32)
    product = counter[:, None] * counter[None, :] % width
    angles = product.astype(jnp.float32) * (2.0 * jnp.pi / width)
    factor = 1.0 / jnp.sqrt(jnp.float32(width))
    return (
        (jnp.cos(angles) * factor).astype(jnp.bfloat16),
        (-jnp.sin(angles) * factor).astype(jnp.bfloat16),
    )


def right_product(field, table):
    return jnp.einsum("...jk,kl->...jl", field, table, preferred_element_type=jnp.float32)


def left_product(table, field):
    return jnp.einsum("ij,...jl->...il", table, field, preferred_element_type=jnp.float32)


def transform(real_part, imag_part, table_real_values, table_imaginary):
    half_real = (
        right_product(real_part, table_real_values) - right_product(imag_part, table_imaginary)
    ).astype(jnp.bfloat16)
    half_imag = (
        right_product(real_part, table_imaginary) + right_product(imag_part, table_real_values)
    ).astype(jnp.bfloat16)
    whole_real = left_product(table_real_values, half_real) - left_product(
        table_imaginary, half_imag
    )
    whole_imag = left_product(table_real_values, half_imag) + left_product(
        table_imaginary, half_real
    )
    return (whole_real, whole_imag)


def position_contributions(patch_stack, probe, measured, table_real_values, table_imaginary):
    obj_real = patch_stack[:, 0].astype(jnp.float32)[:, None]
    obj_imag = patch_stack[:, 1].astype(jnp.float32)[:, None]
    probe_real = probe[:, 0][None]
    probe_imag = probe[:, 1][None]
    wave_real = (probe_real * obj_real - probe_imag * obj_imag).astype(jnp.bfloat16)
    wave_imag = (probe_real * obj_imag + probe_imag * obj_real).astype(jnp.bfloat16)
    far_real, far_imag = transform(wave_real, wave_imag, table_real_values, table_imaginary)
    intensity = jnp.sum(far_real * far_real + far_imag * far_imag, axis=1)
    model_amp = jnp.sqrt(intensity + 1.0)
    data_amp = measured.astype(jnp.float32)
    misfit = jnp.mean((model_amp - data_amp) * (model_amp - data_amp), axis=(1, 2))
    factor = (1.0 - data_amp / model_amp)[:, None]
    resid_real = (far_real * factor).astype(jnp.bfloat16)
    resid_imag = (far_imag * factor).astype(jnp.bfloat16)
    back_real, back_imag = transform(resid_real, resid_imag, table_real_values, -table_imaginary)
    object_share = jnp.stack(
        [
            jnp.sum(probe_real * back_real + probe_imag * back_imag, axis=1),
            jnp.sum(probe_real * back_imag - probe_imag * back_real, axis=1),
        ],
        axis=1,
    )
    probe_share = jnp.stack(
        [
            jnp.sum(obj_real * back_real + obj_imag * back_imag, axis=0),
            jnp.sum(obj_real * back_imag - obj_imag * back_real, axis=0),
        ],
        axis=1,
    )
    return (object_share, probe_share, misfit)


def column_table(start, width, tile_width, dtype):
    window_cols = jnp.arange(width, dtype=jnp.int32)
    tile_cols = jnp.arange(tile_width, dtype=jnp.int32)
    return (tile_cols[None, :] == window_cols[:, None] + start).astype(dtype)


def local(obj, probe, measured, tile_of, inner):
    rows_along = lax.axis_size("tx")
    cols_along = lax.axis_size("ty")
    depth = lax.axis_size("pos")
    groups = rows_along * cols_along
    width = probe.shape[-1]
    tile_width = obj.shape[-1]
    per_device = measured.shape[0]
    index_row = lax.axis_index("tx")
    index_col = lax.axis_index("ty")
    index_depth = lax.axis_index("pos")
    my_tile = index_row * cols_along + index_col
    anchor = jnp.zeros((), jnp.int32)
    table_real_values, table_imaginary = dft_tables(width)
    tile_ids = tile_of[:, 0].reshape(groups, depth, per_device)
    offsets = inner.reshape(groups, depth, per_device, 2)
    slice_ids = lax.dynamic_index_in_dim(tile_ids, index_depth, 1, keepdims=False)
    slice_offsets = lax.dynamic_index_in_dim(offsets, index_depth, 1, keepdims=False)
    matches = (slice_ids == my_tile).astype(jnp.int32)
    ranks = jnp.cumsum(matches, axis=1) - 1
    slot_numbers = jnp.arange(CAP, dtype=jnp.int32)
    select = matches[:, :, None] * (ranks[:, :, None] == slot_numbers[None, None, :]).astype(
        jnp.int32
    )
    slot_rows = jnp.sum(select * slice_offsets[:, :, None, 0], axis=1).reshape(-1)
    slot_cols = jnp.sum(select * slice_offsets[:, :, None, 1], axis=1).reshape(-1)
    slot_live = jnp.sum(select, axis=1).reshape(-1)
    local_tile = obj.astype(jnp.bfloat16)

    def cut(row, col):
        band = lax.dynamic_slice(local_tile, (anchor, row, anchor), (2, width, tile_width))
        picker = column_table(col, width, tile_width, jnp.bfloat16)
        return jnp.einsum("arc,wc->arw", band, picker, preferred_element_type=jnp.float32).astype(
            jnp.bfloat16
        )

    windows = jax.vmap(cut)(slot_rows, slot_cols)
    windows = windows * slot_live[:, None, None, None].astype(jnp.bfloat16)
    outgoing = windows.reshape(groups, CAP, 2, width, width)
    arrived = lax.all_to_all(outgoing, ("tx", "ty"), split_axis=0, concat_axis=0, tiled=True)
    arrived = arrived.reshape(groups * CAP, 2, width, width)
    own_start = (my_tile * depth + index_depth) * per_device
    own_ids = lax.dynamic_slice_in_dim(tile_of[:, 0], own_start, per_device)
    counter = jnp.arange(per_device, dtype=jnp.int32)
    earlier = (counter[:, None] > counter[None, :]) & (own_ids[:, None] == own_ids[None, :])
    own_slot = jnp.sum(earlier.astype(jnp.int32), axis=1)
    lookup = own_ids * CAP + own_slot
    patch_stack = jnp.take(arrived, lookup, axis=0)
    object_share, probe_share, misfit = position_contributions(
        patch_stack, probe, measured, table_real_values, table_imaginary
    )
    returning = jnp.zeros((groups * CAP, 2, width, width), jnp.float32).at[lookup].set(object_share)
    returned = lax.all_to_all(
        returning.reshape(groups, CAP, 2, width, width),
        ("tx", "ty"),
        split_axis=0,
        concat_axis=0,
        tiled=True,
    )
    returned = returned.reshape(groups * CAP, 2, width, width)

    def add_slot(item, accum):
        placer = column_table(slot_cols[item], width, tile_width, jnp.float32)
        spread = jnp.einsum(
            "arw,wc->arc",
            returned[item],
            placer,
            precision=lax.Precision.HIGHEST,
            preferred_element_type=jnp.float32,
        )
        current = lax.dynamic_slice(
            accum, (anchor, slot_rows[item], anchor), (2, width, tile_width)
        )
        return lax.dynamic_update_slice(accum, current + spread, (anchor, slot_rows[item], anchor))

    tile_grad = lax.fori_loop(0, groups * CAP, add_slot, jnp.zeros(obj.shape, jnp.float32))
    shares = lax.psum_scatter(tile_grad, "pos", scatter_dimension=1, tiled=True)
    probe_total = lax.psum(probe_share, ("tx", "ty", "pos"))
    total_positions = per_device * groups * depth
    return (shares, probe_total / total_positions, misfit)


def solution(mesh):
    return jax.shard_map(
        local,
        mesh=mesh,
        in_specs=(P(None, "tx", "ty"), P(), P(("tx", "ty", "pos"), None, None), P(), P()),
        out_specs=(P(None, ("tx", "pos"), "ty"), P(), P(("tx", "ty", "pos"))),
        check_vma=False,
    )
```

profile of v0, /device:TPU:1, one launch (start us, length us, event | category | flops | bytes accessed | tf_op | source)
XLA Modules:
  0.0 967.8 jit_solution(12493036927163727315)
XLA Ops:
  11.6 6.0 copy.221
  18.1 53.4 %gather_fusion = bf16[64,2,128,768]{3,1,2,0:T(2,128)(2,1)} fusion(bf16[2,768,768]{2,0,1:T(2,128)(2,1)S(1)} %copy.221, s32[64]{0:T(128)S(1)} %fusion.111), kind=kCustom, calls=%fused_computation | custom fusion | bytes 50332416 | tf_op jit(solution)/shard_map/vmap()/gather | solution.py:113
  71.6 14.2 %convert_multiply_fusion = bf16[64,2,128,128]{3,2,1,0:T(8,128)(2,1)} fusion(s32[64,128]{1,0:T(8,128)S(1)} %iota_add_fusion.1, bf16[64,2,128,768]{3,1,2,0:T(2,128)(2,1)} %gather_fusion, bf16[64]{0:T(256)(128)(2,1)S(1)} %convert_element_type.143), kind=kOutput, calls=%fused_computation.47 | convolution fusion | flops 3231711232 | bytes 29393024 | tf_op jit(solution)/shard_map/vmap(arc,wc->arw)/dot_general | solution.py:115
  85.7 8.2 all-to-all-start
  96.3 49.7 %all-to-all-done = bf16[32,2,2,128,128]{4,3,2,1,0:T(8,128)(2,1)} async-done(((bf16[32,2,2,128,128]{4,3,2,1,0:T(8,128)(2,1)}), bf16[32,2,2,128,128]{4,3,2,1,0:T(8,128)(2,1)}, u32[]{:S(2)}, u32[]{:S(2)}) %all-to-all-start) | async-done | bytes 4194336 | tf_op jit(solution)/shard_map/all_to_all | solution.py:122
  169.3 3.7 fusion.16
  176.6 4.3 broadcast_in_dim.16
  180.8 3.7 scatter_fusion
  184.5 7.2 all-to-all-start.1
  192.7 106.7 %all-to-all-done.1 = f32[32,2,2,128,128]{4,3,2,1,0:T(8,128)} async-done(((f32[32,2,2,128,128]{4,3,2,1,0:T(8,128)}), f32[32,2,2,128,128]{4,3,2,1,0:T(8,128)}, u32[]{:S(2)}, u32[]{:S(2)}) %all-to-all-start.1) | async-done | bytes 8388640 | tf_op jit(solution)/shard_map/all_to_all | solution.py:135
  301.9 579.8 %while.13 = (s32[]{:T(128)}, f32[2,768,768]{2,1,0:T(8,128)}, s32[64]{0:T(128)S(1)}, f32[64,2,128,128]{3,2,1,0:T(8,128)}, s32[64]{0:T(128)S(1)}, /*index=5*/s32[]{:T(128)}, s32[]{:T(128)}, s32[]{:T(128)}) while((s32[]{:T(128)}, f32[2,768,768]{2,1,0:T(8,128)}, s32[64]{0:T(128)S(1)}, f32[64,2,128,128]{3,2,1,0:T(8,128)}, s32[64]{0:T(128)S(1)}, ...), condition=%wide.region_10.11_spmd, body=%wide.region_9.10_spmd.sunk | while | flops 302284928 | bytes 3278491 | solution.py:158
  307.4 3.5 dynamic_update_slice.8
  316.5 3.5 dynamic_update_slice.8
  334.6 3.5 dynamic_update_slice.8
  343.7 3.5 dynamic_update_slice.8
  361.7 3.5 dynamic_update_slice.8
  370.7 3.5 dynamic_update_slice.8
  379.8 3.5 dynamic_update_slice.8
  388.9 3.5 dynamic_update_slice.8
  398.0 3.5 dynamic_update_slice.8
  407.1 3.5 dynamic_update_slice.8
  416.2 3.5 dynamic_update_slice.8
  425.2 3.5 dynamic_update_slice.8
  434.3 3.5 dynamic_update_slice.8
  443.4 3.5 dynamic_update_slice.8
  452.4 3.5 dynamic_update_slice.8
  461.5 3.5 dynamic_update_slice.8
  470.5 3.5 dynamic_update_slice.8
  479.6 3.5 dynamic_update_slice.8
  488.7 3.5 dynamic_update_slice.8
  506.8 3.5 dynamic_update_slice.8
  515.8 3.5 dynamic_update_slice.8
  524.9 3.5 dynamic_update_slice.8
  534.0 3.5 dynamic_update_slice.8
  543.1 3.5 dynamic_update_slice.8
  552.1 3.5 dynamic_update_slice.8
  561.2 3.5 dynamic_update_slice.8
  570.2 3.5 dynamic_update_slice.8
  579.3 3.5 dynamic_update_slice.8
  588.4 3.5 dynamic_update_slice.8
  624.4 3.5 dynamic_update_slice.8
  642.6 3.5 dynamic_update_slice.8
  651.6 3.5 dynamic_update_slice.8
  660.7 3.5 dynamic_update_slice.8
  669.8 3.5 dynamic_update_slice.8
  678.8 3.5 dynamic_update_slice.8
  696.9 3.5 dynamic_update_slice.8
  706.0 3.5 dynamic_update_slice.8
  715.1 3.5 dynamic_update_slice.8
  733.2 3.5 dynamic_update_slice.8
  742.3 3.5 dynamic_update_slice.8
  760.4 3.5 dynamic_update_slice.8
  769.5 3.5 dynamic_update_slice.8
  778.5 3.5 dynamic_update_slice.8
  787.6 3.5 dynamic_update_slice.8
  796.7 3.5 dynamic_update_slice.8
  805.7 3.5 dynamic_update_slice.8
  814.8 3.5 dynamic_update_slice.8
  823.9 3.5 dynamic_update_slice.8
  832.9 3.5 dynamic_update_slice.8
  860.1 3.5 dynamic_update_slice.8
  869.1 3.5 dynamic_update_slice.8
  878.2 3.5 dynamic_update_slice.8
  884.3 76.1 %reduce-scatter.2.cloned.1.call-done = f32[2,96,768]{2,1,0:T(8,128)} async-done(((f32[2,768,768]{2,1,0:T(8,128)}), f32[2,96,768]{2,1,0:T(8,128)}) %reduce-scatter.2.cloned.1.call-update) | async-done | bytes 589840 | tf_op jit(solution)/shard_map/reduce_scatter | solution.py:159
  (336 shorter events, 311.8 us)
Async XLA Ops:
  85.7 8.3 copy-start
  85.7 8.6 copy-start.1
  85.7 60.3 %all-to-all-start = ((bf16[32,2,2,128,128]{4,3,2,1,0:T(8,128)(2,1)}), bf16[32,2,2,128,128]{4,3,2,1,0:T(8,128)(2,1)}, u32[]{:S(2)}, u32[]{:S(2)}) async-start(bf16[32,2,2,128,128]{4,3,2,1,0:T(8,128)(2,1)} %bitcast.167), calls=%async_computation | async-start | bytes 8388608 | tf_op jit(solution)/shard_map/all_to_all | solution.py:122
  184.5 114.9 %all-to-all-start.1 = ((f32[32,2,2,128,128]{4,3,2,1,0:T(8,128)}), f32[32,2,2,128,128]{4,3,2,1,0:T(8,128)}, u32[]{:S(2)}, u32[]{:S(2)}) async-start(f32[32,2,2,128,128]{4,3,2,1,0:T(8,128)} %bitcast.166), calls=%async_computation.1 | async-start | bytes 16777216 | tf_op jit(solution)/shard_map/all_to_all | solution.py:135
  191.7 690.5 %all-reduce.2.cloned.1.call-start = ((), (), s32[]{:S(2)}) async-start(), calls=%async_computation.4 | async-start | bytes 1048576 | tf_op jit(solution)/shard_map/psum | solution.py:160
  192.7 767.7 %reduce-scatter.2.cloned.1.call-start = ((), (), s32[]{:S(2)}) async-start(), calls=%async_computation.3 | async-start | bytes 5308416 | tf_op jit(solution)/shard_map/reduce_scatter | solution.py:159
Sparse Core Ops, SparseCore 0:
  198.6 302.7 all-reduce.1
Sparse Core Ops, SparseCore 1:
  881.8 78.6 reduce-scatter.1
where the time goes:
time: 976 us; the launch traced here: 968 us
  local copies, waits for them, and re-layouts  379 us (39%)
  waiting for transfers between devices  233 us (24%)
  matrix products  149 us (15%)
  loops' own time  125 us (13%)
  other arithmetic  50.3 us (5%)
  between operations  15.8 us (2%)
  starting transfers between devices  15.5 us (2%)
    dynamic_update_slice x64, local copies, waits for them, and re-layouts, add_slot(): lax.dynamic_update_slice(accum, current + spread, (anchor, slot_rows[item...  223 us
    another operation x1, loops' own time, local(): lax.fori_loop(0, groups * CAP, add_slot, jnp.zeros(obj.shape, jnp.float32))  125 us
    dot_general x64, matrix products, add_slot(): jnp.einsum('arw,wc->arc', returned[item], placer, precision=lax.Precision...  115 us
    all_to_all x1, waiting for transfers between devices, local(): lax.all_to_all(returning.reshape(groups, CAP, 2, width, width), ('tx', 't...  107 us
    reduce_scatter x1, waiting for transfers between devices, local(): shares = lax.psum_scatter(tile_grad, 'pos', scatter_dimension=1, tiled=True)  76.1 us
    gather x1, local copies, waits for them, and re-layouts, cut(): lax.dynamic_slice(local_tile, (anchor, row, anchor), (2, width, tile_width))  53.4 us
    all_to_all x1, waiting for transfers between devices, local(): lax.all_to_all(outgoing, ('tx', 'ty'), split_axis=0, concat_axis=0, tiled...  49.7 us
    add x65, other arithmetic, column_table(): return (tile_cols[None, :] == window_cols[:, None] + start).astype(dtype)  41.5 us
  transfers between devices with their start and end apart: 4, of which 3 were waited for; matrix products, arithmetic and copies ran while one was open for 48% of the time, Pallas kernels for 0%

commit v1 on v0

v1 whole, which is shorter than its diff:
```python
import jax
import jax.numpy as jnp
import ml_dtypes
import numpy as np
from jax import lax
from jax.experimental import pallas as pl
from jax.experimental.pallas import tpu as pltpu
from jax.sharding import PartitionSpec as P

CAP = 2
LANES = 128
ROW_BITS = 10
TILE_SHIFT = 2 * ROW_BITS
LOW = (1 << ROW_BITS) - 1


def dft_blocks(width):
    counter = np.arange(width, dtype=np.int32)
    product = counter[:, None] * counter[None, :] % width
    angles = product.astype(np.float32) * np.float32(2.0 * np.pi / width)
    factor = np.float32(1.0) / np.sqrt(np.float32(width))
    c = (np.cos(angles) * factor).astype(ml_dtypes.bfloat16)
    s = (-np.sin(angles) * factor).astype(ml_dtypes.bfloat16)
    return np.block([[c, -s], [s, c]]), np.block([[c, s], [-s, c]])


def send_kernel(groups, depth, per_device, where_ref, packed_ref, measured_ref, out_ref, slot_ref, sems):
    base = (where_ref[0] * depth + where_ref[1]) * per_device
    tiles = [lax.shift_right_logical(packed_ref[base + i], TILE_SHIFT) for i in range(per_device)]
    copies = []
    for i in range(per_device):
        rank = jnp.int32(0)
        for j in range(i):
            rank = rank + (tiles[j] == tiles[i]).astype(jnp.int32)
        slot = tiles[i] * CAP + rank
        slot_ref[i] = slot
        copy = pltpu.make_async_copy(measured_ref.at[i], out_ref.at[slot], sems.at[i])
        copy.start()
        copies.append(copy)
    for copy in copies:
        copy.wait()


def list_kernel(groups, depth, per_device, where_ref, packed_ref, list_ref):
    tile = where_ref[0]
    plane = where_ref[1]

    def one_group(group, count):
        base = (group * depth + plane) * per_device
        rank = jnp.int32(0)
        for i in range(per_device):
            value = packed_ref[base + i]
            hit = (lax.shift_right_logical(value, TILE_SHIFT) == tile).astype(jnp.int32)
            slot = group * CAP + rank
            list_ref[count] = (slot << TILE_SHIFT) | (value & ((1 << TILE_SHIFT) - 1))
            count = count + hit
            rank = rank + hit
        return count

    count = lax.fori_loop(0, groups, one_group, jnp.int32(0))
    list_ref[groups * CAP + 1] = count


def main_kernel(
    modes,
    slots,
    list_ref,
    obj_ref,
    probe_ref,
    arrived_ref,
    x_ref,
    y_ref,
    grad_ref,
    sums_ref,
    tile_s,
    acc_s,
    probe_s,
    meas_s,
    misfit_s,
    sems,
):
    width = LANES
    blocks = tile_s.shape[1]
    copies = []
    for a in range(2):
        for b in range(blocks):
            copies.append(
                pltpu.make_async_copy(
                    obj_ref.at[a, :, pl.ds(b * LANES, LANES)], tile_s.at[a, b], sems.at[a * blocks + b]
                )
            )
    copies.append(pltpu.make_async_copy(arrived_ref, meas_s, sems.at[2 * blocks]))
    for copy in copies:
        copy.start()
    acc_s[...] = jnp.zeros_like(acc_s)
    probe_s[...] = jnp.zeros_like(probe_s)
    misfit_s[...] = jnp.zeros_like(misfit_s)
    for copy in copies:
        copy.wait()
    lane = lax.broadcasted_iota(jnp.int32, (width, LANES), 1)

    def one(item, carry):
        entry = list_ref[item]
        slot = lax.shift_right_logical(entry, TILE_SHIFT)
        row = lax.shift_right_logical(entry, ROW_BITS) & LOW
        col = entry & LOW
        block = jnp.minimum(lax.shift_right_logical(col, 7), blocks - 2)
        shift = col - block * LANES
        back_shift = (LANES - shift) & (LANES - 1)
        own = lane < LANES - shift

        def cut(a):
            left = pltpu.roll(tile_s[a, block, pl.ds(row, width), :], back_shift, 1)
            right = pltpu.roll(tile_s[a, block + 1, pl.ds(row, width), :], back_shift, 1)
            return jnp.where(own, left, right).astype(jnp.bfloat16).astype(jnp.float32)

        obj_r = cut(0)
        obj_i = cut(1)
        waves = []
        for k in range(modes):
            p_r = probe_ref[k, 0]
            p_i = probe_ref[k, 1]
            waves.append(
                jnp.concatenate([p_r * obj_r - p_i * obj_i, p_r * obj_i + p_i * obj_r], axis=1).astype(
                    jnp.bfloat16
                )
            )

        def stack(half):
            return jnp.concatenate(
                [
                    jnp.concatenate(
                        [half[k * width : (k + 1) * width, :width], half[k * width : (k + 1) * width, width:]],
                        axis=0,
                    )
                    for k in range(modes)
                ],
                axis=1,
            )

        half = jnp.dot(jnp.concatenate(waves, axis=0), y_ref[...], preferred_element_type=jnp.float32)
        far = jnp.dot(x_ref[...], stack(half.astype(jnp.bfloat16)), preferred_element_type=jnp.float32)
        intensity = jnp.ones((width, LANES), jnp.float32)
        for k in range(modes):
            f_r = far[:width, k * width : (k + 1) * width]
            f_i = far[width:, k * width : (k + 1) * width]
            intensity = intensity + (f_r * f_r + f_i * f_i)
        data = meas_s[slot].astype(jnp.float32)
        inverse = lax.rsqrt(intensity)
        gap = intensity * inverse - data
        misfit_s[slot] = jnp.sum(gap * gap, axis=0, keepdims=True)
        factor = 1.0 - data * inverse
        residuals = []
        for k in range(modes):
            f_r = far[:width, k * width : (k + 1) * width]
            f_i = far[width:, k * width : (k + 1) * width]
            residuals.append(jnp.concatenate([f_r * factor, f_i * factor], axis=1).astype(jnp.bfloat16))
        half = jnp.dot(jnp.concatenate(residuals, axis=0), x_ref[...], preferred_element_type=jnp.float32)
        back = jnp.dot(y_ref[...], stack(half.astype(jnp.bfloat16)), preferred_element_type=jnp.float32)
        part_r = jnp.zeros((width, LANES), jnp.float32)
        part_i = jnp.zeros((width, LANES), jnp.float32)
        for k in range(modes):
            p_r = probe_ref[k, 0]
            p_i = probe_ref[k, 1]
            b_r = back[:width, k * width : (k + 1) * width]
            b_i = back[width:, k * width : (k + 1) * width]
            part_r = part_r + (p_r * b_r + p_i * b_i)
            part_i = part_i + (p_r * b_i - p_i * b_r)
            probe_s[k, 0] = probe_s[k, 0] + (obj_r * b_r + obj_i * b_i)
            probe_s[k, 1] = probe_s[k, 1] + (obj_r * b_i - obj_i * b_r)
        keep = lane >= shift
        for a, part in ((0, part_r), (1, part_i)):
            turned = pltpu.roll(part, shift & (LANES - 1), 1)
            spot = (a, block, pl.ds(row, width), slice(None))
            acc_s[spot] = acc_s[spot] + jnp.where(keep, turned, 0.0)
            spot = (a, block + 1, pl.ds(row, width), slice(None))
            acc_s[spot] = acc_s[spot] + jnp.where(keep, 0.0, turned)
        return carry

    lax.fori_loop(0, list_ref[slots + 1], one, jnp.int32(0))
    groups = sums_ref.shape[0]
    rows = sums_ref.shape[1] - 8
    copies = []
    for a in range(2):
        for b in range(blocks):
            copies.append(
                pltpu.make_async_copy(
                    acc_s.at[a, b], grad_ref.at[a, :, pl.ds(b * LANES, LANES)], sems.at[a * blocks + b]
                )
            )
    for copy in copies:
        copy.start()
    flat = modes * 2 * width // groups
    per_plane = width // flat
    for g in range(groups):
        plane, part = divmod(g, per_plane)
        sums_ref[g, pl.ds(0, rows), :] = probe_s[plane // 2, plane % 2, pl.ds(part * flat, flat), :]
        for s in range(CAP):
            sums_ref[g, pl.ds(rows + s, 1), :] = misfit_s[g * CAP + s]
        sums_ref[g, pl.ds(rows + CAP, 8 - CAP), :] = jnp.zeros((8 - CAP, LANES), jnp.float32)
    for copy in copies:
        copy.wait()


def receive_kernel(scale, pixels, slot_ref, sums_ref, probe_ref, misfit_ref):
    groups, rows = sums_ref.shape[0], probe_ref.shape[0]
    total = jnp.zeros((rows, LANES), jnp.float32)
    for g in range(groups):
        total = total + sums_ref[g, pl.ds(0, rows), :]
    probe_ref[...] = total * scale
    for i in range(slot_ref.shape[0]):
        slot = slot_ref[i]
        picked = sums_ref[lax.shift_right_logical(slot, 1), pl.ds(rows + (slot & 1), 1), :]
        misfit_ref[i] = jnp.sum(picked) * (1.0 / pixels)


SMEM = pl.BlockSpec(memory_space=pltpu.SMEM)
VMEM = pl.BlockSpec(memory_space=pltpu.VMEM)
ANY = pl.BlockSpec(memory_space=pl.ANY)


def local(obj, probe, measured, tile_of, inner):
    cols_along = lax.axis_size("ty")
    groups = lax.axis_size("tx") * cols_along
    depth = lax.axis_size("pos")
    modes, _, width, _ = probe.shape
    tile_width = obj.shape[-1]
    blocks = tile_width // LANES
    per_device = measured.shape[0]
    positions = per_device * groups * depth
    slots = groups * CAP
    plane = ("tx", "ty")
    my_tile = lax.axis_index("tx") * cols_along + lax.axis_index("ty")
    where = jnp.stack([my_tile, lax.axis_index("pos")]).astype(jnp.int32)
    packed = (tile_of[:, 0] << TILE_SHIFT) | (inner[:, 0] << ROW_BITS) | inner[:, 1]
    sizes = (groups, depth, per_device)

    outgoing, own_slots = pl.pallas_call(
        lambda *refs: send_kernel(*sizes, *refs),
        out_shape=(
            jax.ShapeDtypeStruct((slots, width, width), measured.dtype),
            jax.ShapeDtypeStruct((per_device,), jnp.int32),
        ),
        in_specs=[SMEM, SMEM, ANY],
        out_specs=(ANY, SMEM),
        scratch_shapes=[pltpu.SemaphoreType.DMA((per_device,))],
        name="send_slots",
    )(where, packed, measured)
    arrived = lax.all_to_all(
        outgoing.reshape(groups, CAP, width, width), plane, split_axis=0, concat_axis=0, tiled=True
    ).reshape(slots, width, width)
    listed = pl.pallas_call(
        lambda *refs: list_kernel(*sizes, *refs),
        out_shape=jax.ShapeDtypeStruct((slots + 8,), jnp.int32),
        in_specs=[SMEM, SMEM],
        out_specs=SMEM,
        cost_estimate=pl.CostEstimate(flops=10_000_000, bytes_accessed=10_000_000, transcendentals=0),
        name="list_windows",
    )(where, packed)
    x_table, y_table = dft_blocks(width)
    rows = modes * 2 * width // groups
    tile_grad, sums = pl.pallas_call(
        lambda *refs: main_kernel(modes, slots, *refs),
        out_shape=(
            jax.ShapeDtypeStruct(obj.shape, jnp.float32),
            jax.ShapeDtypeStruct((groups, rows + 8, LANES), jnp.float32),
        ),
        in_specs=[SMEM, ANY, VMEM, ANY, VMEM, VMEM],
        out_specs=(ANY, VMEM),
        scratch_shapes=[
            pltpu.VMEM((2, blocks, tile_width, LANES), jnp.float32),
            pltpu.VMEM((2, blocks, tile_width, LANES), jnp.float32),
            pltpu.VMEM((modes, 2, width, LANES), jnp.float32),
            pltpu.VMEM((slots, width, width), measured.dtype),
            pltpu.VMEM((slots, 1, LANES), jnp.float32),
            pltpu.SemaphoreType.DMA((2 * blocks + 1,)),
        ],
        compiler_params=pltpu.CompilerParams(vmem_limit_bytes=48 << 20),
        name="windows",
    )(listed, obj, probe, arrived, jnp.asarray(x_table), jnp.asarray(y_table))
    shares = lax.psum_scatter(tile_grad, "pos", scatter_dimension=1, tiled=True)
    sums = lax.all_to_all(sums, plane, split_axis=0, concat_axis=0, tiled=True)
    probe_part, misfit = pl.pallas_call(
        lambda *refs: receive_kernel(1.0 / positions, width * width, *refs),
        out_shape=(
            jax.ShapeDtypeStruct((rows, LANES), jnp.float32),
            jax.ShapeDtypeStruct((per_device,), jnp.float32),
        ),
        in_specs=[SMEM, VMEM],
        out_specs=(VMEM, SMEM),
        name="receive_sums",
    )(own_slots, sums)
    probe_part = jnp.sum(lax.all_gather(probe_part, "pos", axis=0), axis=0)
    probe_total = lax.all_gather(probe_part, plane, axis=0, tiled=True)
    return (shares, probe_total.reshape(modes, 2, width, width), misfit)


def solution(mesh):
    return jax.shard_map(
        local,
        mesh=mesh,
        in_specs=(P(None, "tx", "ty"), P(), P(("tx", "ty", "pos"), None, None), P(), P()),
        out_specs=(P(None, ("tx", "pos"), "ty"), P(), P(("tx", "ty", "pos"))),
        check_vma=False,
    )
```

time: 976 us -> 223 us (0.23)
  local copies, waits for them, and re-layouts: 379 us -> 1.46 us
  waiting for transfers between devices: 233 us -> 24.7 us
  matrix products: 149 us -> 0 us
  blocking collectives: 0 us -> 130 us
  loops' own time: 125 us -> 0 us
  other arithmetic: 50.3 us -> 2.07 us
  Pallas kernels: 0 us -> 41.7 us
    dynamic_update_slice x64 -> x0, local copies, waits for them, and re-layouts: 223 us -> none  [add_slot(): lax.dynamic_update_slice(accum, current + spread, (anchor, slot_rows[item...]
    dot_general x81 -> x0, matrix products: 149 us -> none  [the longest x64 115 us: add_slot(): jnp.einsum('arw,wc->arc', returned[item], placer, precision=lax.Precision...]
    all_to_all x2 -> x1, waiting for transfers between devices: 156 us -> 24.7 us  [local(): lax.all_to_all(outgoing.reshape(groups, CAP, width, width), plane, split_...]
    another operation x1 -> x0, loops' own time: 125 us -> none  [local(): lax.fori_loop(0, groups * CAP, add_slot, jnp.zeros(obj.shape, jnp.float32))]
    all_to_all x0 -> x1, blocking collectives: none -> 77 us  [local(): sums = lax.all_to_all(sums, plane, split_axis=0, concat_axis=0, tiled=True)]
    reduce_scatter x1, waiting for transfers between devices: 76.1 us -> 0.01 us  [local(): shares = lax.psum_scatter(tile_grad, 'pos', scatter_dimension=1, tiled=True)]
    dynamic_slice x130 -> x0, local copies, waits for them, and re-layouts: 75 us -> none  [the longest x64 37.7 us: add_slot(): placer = column_table(slot_cols[item], width, tile_width, jnp.float32)]
    gather x2 -> x0, local copies, waits for them, and re-layouts: 56.4 us -> none  [the longest x1 53.4 us: cut(): lax.dynamic_slice(local_tile, (anchor, row, anchor), (2, width, tile_width))]
  transfers between devices with their start and end apart: 4 -> 2, of which waited for: 3 -> 1; matrix products, arithmetic and copies ran while one was open for 48% -> 0% of each run, Pallas kernels for 0% -> 2%
where the time goes in v1:
time: 223 us; the launch traced here: 222 us
  blocking collectives  130 us (58%)
  Pallas kernels  41.7 us (19%)
  waiting for transfers between devices  24.7 us (11%)
  between operations  14.1 us (6%)
  starting transfers between devices  8.64 us (4%)
    all_to_all x1, blocking collectives, local(): sums = lax.all_to_all(sums, plane, split_axis=0, concat_axis=0, tiled=True)  77 us
    all_gather x1, blocking collectives, local(): probe_total = lax.all_gather(probe_part, plane, axis=0, tiled=True)  26.7 us
    all_gather x1, blocking collectives, local(): probe_part = jnp.sum(lax.all_gather(probe_part, 'pos', axis=0), axis=0)  25.9 us
    all_to_all x1, waiting for transfers between devices, local(): lax.all_to_all(outgoing.reshape(groups, CAP, width, width), plane, split_...  24.7 us
    pallas_call x1, Pallas kernels, local(): pl.pallas_call(lambda *refs: send_kernel(*sizes, *refs), out_shape=(jax.S...  18.6 us
    pallas_call x1, Pallas kernels, local(): pl.pallas_call(lambda *refs: main_kernel(modes, slots, *refs), out_shape=...  17.7 us
    all_to_all x1, starting transfers between devices, local(): lax.all_to_all(outgoing.reshape(groups, CAP, width, width), plane, split_...  8.6 us
  transfers between devices with their start and end apart: 2, of which 1 were waited for; matrix products, arithmetic and copies ran while one was open for 0% of the time, Pallas kernels for 2%

profile of v1, /device:TPU:1, one launch (start us, length us, event | category | flops | bytes accessed | tf_op | source)
XLA Modules:
  0.0 222.3 jit_solution(8924205785014936930)
XLA Ops:
  7.2 0.0 copy-start.1
  7.2 0.0 copy-start.2
  7.2 0.0 copy-start
  7.2 0.6 pad_add_fusion.refs_0_
  7.8 1.5 slice_or_fusion
  9.3 18.6 %send_slots.1 = (bf16[64,128,128]{2,1,0:T(8,128)(2,1)}, s32[16]{0:T(128)}) custom-call(s32[2]{0:T(128)} %pad_add_fusion.refs_0_, s32[4096]{0:T(1024)} %bitcast.11, bf16[16,128,128]{2,1,0:T(8,128)(2,1)} %refs_2_.2), custom_call_target="tpu_custom_call" | custom-call | tf_op jit(solution)/shard_map/send_slots/pallas_call | solution.py:238
  27.9 8.6 %all-to-all-start = ((bf16[32,2,128,128]{3,2,1,0:T(8,128)(2,1)}), bf16[32,2,128,128]{3,2,1,0:T(8,128)(2,1)S(1)}, u32[]{:S(2)}, u32[]{:S(2)}) async-start(bf16[32,2,128,128]{3,2,1,0:T(8,128)(2,1)} %bitcast.8), calls=%async_computation | async-start | bytes 4194304 | tf_op jit(solution)/shard_map/all_to_all | solution.py:249
  36.5 0.0 reduce-scatter.2.cloned.1.call-start
  36.5 3.5 %list_windows.1.refs_0_ = s32[72]{0:T(128)} custom-call(s32[2]{0:T(128)} %pad_add_fusion.refs_0_, s32[4096]{0:T(1024)} %bitcast.12), custom_call_target="tpu_custom_call" | custom-call | flops 10000000 | bytes 10000000 | tf_op jit(solution)/shard_map/list_windows/pallas_call | solution.py:252
  40.1 24.7 %all-to-all-done = bf16[32,2,128,128]{3,2,1,0:T(8,128)(2,1)S(1)} async-done(((bf16[32,2,128,128]{3,2,1,0:T(8,128)(2,1)}), bf16[32,2,128,128]{3,2,1,0:T(8,128)(2,1)S(1)}, u32[]{:S(2)}, u32[]{:S(2)}) %all-to-all-start) | async-done | bytes 2097184 | tf_op jit(solution)/shard_map/all_to_all | solution.py:249
  64.8 0.0 copy-done.1
  64.8 0.0 copy-done.2
  64.8 0.0 copy-done
  64.8 0.0 copy-start.3
  64.8 0.6 copy-done.3
  65.4 17.7 %windows.1 = (f32[2,768,768]{2,1,0:T(8,128)}, f32[32,40,128]{2,1,0:T(8,128)S(1)}) custom-call(s32[72]{0:T(128)S(1)} %copy-done.3, f32[2,768,768]{2,1,0:T(8,128)} %refs_1_.1, f32[4,2,128,128]{3,2,1,0:T(8,128)S(1)} %copy-done, bf16[64,128,128]{2,1,0:T(8,128)(2,1)S(1)} %bitcast.7, bf16[256,256]{1,0:T(8,128)(2,1)S(1)} %copy-done.2, bf16[256,256]{1,0:T(8,128)(2,1)S(1)} %copy-done.1), custom_call_target="tpu_custom_call" | custom-call | tf_op jit(solution)/shard_map/windows/pallas_call | solution.py:262
  83.2 0.0 reduce-scatter.2.cloned.1.call-update
  83.2 77.0 %all_to_all.10.refs_1_ = f32[32,40,128]{2,1,0:T(8,128)} all-to-all(f32[32,40,128]{2,1,0:T(8,128)S(1)} %get-tuple-element.12), channel_id=1, replica_groups=mesh['tx'=4,'ty'=8,'pos'=8] {'tx','ty'}, dimensions={0} | all-to-all | bytes 1310720 | tf_op jit(solution)/shard_map/all_to_all | solution.py:282
  160.3 1.8 receive_sums.1
  162.1 25.9 %all-gather = f32[256,128]{1,0:T(8,128)S(1)} all-gather(f32[32,128]{1,0:T(8,128)} %get-tuple-element.13), channel_id=2, replica_groups=mesh['tx'=4,'ty'=8,'pos'=8] {'pos'}, dimensions={0}, use_global_device_ids=true | all-gather | bytes 147456 | tf_op jit(solution)/shard_map/all_gather | solution.py:293
  188.0 26.7 %all_gather.11 = f32[1024,128]{1,0:T(8,128)S(1)} all-gather(f32[32,128]{1,0:T(8,128)S(1)} %reduce_sum.9), channel_id=1, replica_groups=mesh['tx'=4,'ty'=8,'pos'=8] {'tx','ty'}, dimensions={0}, use_global_device_ids=true | all-gather | bytes 540672 | tf_op jit(solution)/shard_map/all_gather | solution.py:294
  214.7 0.0 reduce-scatter.2.cloned.1.call-done
  214.7 0.8 copy.11
  (1 shorter events, 0.0 us)
Async XLA Ops:
  7.2 57.6 %copy-start.1 = (bf16[256,256]{1,0:T(8,128)(2,1)S(1)}, bf16[256,256]{1,0:T(8,128)(2,1)}, u32[]{:S(2)}) copy-start(bf16[256,256]{1,0:T(8,128)(2,1)} %constant.25.clone.refs_5_) | copy-start | bytes 393220
  7.2 57.6 %copy-start.2 = (bf16[256,256]{1,0:T(8,128)(2,1)S(1)}, bf16[256,256]{1,0:T(8,128)(2,1)}, u32[]{:S(2)}) copy-start(bf16[256,256]{1,0:T(8,128)(2,1)} %constant.24.clone.refs_4_) | copy-start | bytes 393220
  7.2 57.6 %copy-start = (f32[4,2,128,128]{3,2,1,0:T(8,128)S(1)}, f32[4,2,128,128]{3,2,1,0:T(8,128)}, u32[]{:S(2)}) copy-start(f32[4,2,128,128]{3,2,1,0:T(8,128)} %refs_2_.3) | copy-start | bytes 1572868
  27.9 36.9 %all-to-all-start = ((bf16[32,2,128,128]{3,2,1,0:T(8,128)(2,1)}), bf16[32,2,128,128]{3,2,1,0:T(8,128)(2,1)S(1)}, u32[]{:S(2)}, u32[]{:S(2)}) async-start(bf16[32,2,128,128]{3,2,1,0:T(8,128)(2,1)} %bitcast.8), calls=%async_computation | async-start | bytes 4194304 | tf_op jit(solution)/shard_map/all_to_all | solution.py:249
  36.5 178.2 %reduce-scatter.2.cloned.1.call-start = ((), (), s32[]{:S(2)}) async-start(), calls=%async_computation.3 | async-start | bytes 5308416 | tf_op jit(solution)/shard_map/reduce_scatter | solution.py:281
  64.8 0.7 copy-start.3
Sparse Core Ops, SparseCore 0:
  83.3 120.9 reduce-scatter.1

commit v2 on v1

v2 whole, which is shorter than its diff:
```python
import jax
import jax.numpy as jnp
import ml_dtypes
import numpy as np
from jax import lax
from jax.experimental import pallas as pl
from jax.experimental.pallas import tpu as pltpu
from jax.sharding import PartitionSpec as P

CAP = 2
UNROLL = 2
LANES = 128
ROW_BITS = 10
TILE_SHIFT = 2 * ROW_BITS
LOW = (1 << ROW_BITS) - 1


def dft_blocks(width):
    counter = np.arange(width, dtype=np.int32)
    product = counter[:, None] * counter[None, :] % width
    angles = product.astype(np.float32) * np.float32(2.0 * np.pi / width)
    factor = np.float32(1.0) / np.sqrt(np.float32(width))
    c = (np.cos(angles) * factor).astype(ml_dtypes.bfloat16)
    s = (-np.sin(angles) * factor).astype(ml_dtypes.bfloat16)
    return np.block([[c, -s], [s, c]]), np.block([[c, s], [-s, c]])


def send_kernel(groups, depth, per_device, where_ref, packed_ref, measured_ref, out_ref, slot_ref):
    base = (where_ref[0] * depth + where_ref[1]) * per_device
    tiles = [lax.shift_right_logical(packed_ref[base + i], TILE_SHIFT) for i in range(per_device)]
    for i in range(per_device):
        rank = jnp.int32(0)
        for j in range(i):
            rank = rank + (tiles[j] == tiles[i]).astype(jnp.int32)
        slot = tiles[i] * CAP + rank
        slot_ref[i] = slot
        out_ref[slot] = measured_ref[i]


def list_kernel(groups, depth, per_device, where_ref, packed_ref, list_ref):
    tile = where_ref[0]
    plane = where_ref[1]

    def one_group(group, count):
        base = (group * depth + plane) * per_device
        rank = jnp.int32(0)
        for i in range(per_device):
            value = packed_ref[base + i]
            hit = (lax.shift_right_logical(value, TILE_SHIFT) == tile).astype(jnp.int32)
            slot = group * CAP + rank
            list_ref[count] = (slot << TILE_SHIFT) | (value & ((1 << TILE_SHIFT) - 1))
            count = count + hit
            rank = rank + hit
        return count

    count = lax.fori_loop(0, groups, one_group, jnp.int32(0))
    for u in range(UNROLL - 1):
        list_ref[count + u] = jnp.int32((groups * CAP) << TILE_SHIFT)
    list_ref[groups * CAP + UNROLL] = (count + UNROLL - 1) // UNROLL


def window_of(entry, blocks):
    slot = lax.shift_right_logical(entry, TILE_SHIFT)
    row = lax.shift_right_logical(entry, ROW_BITS) & LOW
    col = entry & LOW
    block = jnp.minimum(lax.shift_right_logical(col, 7), blocks - 2)
    return slot, row, block, col - block * LANES


def stack(half, width):
    fields = half.shape[0] // width
    columns = []
    for f in range(fields):
        rows = half[f * width : (f + 1) * width]
        columns.append(jnp.concatenate([rows[:, :width], rows[:, width:]], axis=0))
    return jnp.concatenate(columns, axis=1)


def forward_kernel(
    slots,
    list_ref,
    obj_ref,
    probe_ref,
    x_ref,
    y_ref,
    far_ref,
    patch_ref,
    tile_s,
    far_s,
    patch_s,
    sems,
    out_sems,
):
    width = LANES
    modes = probe_ref.shape[0]
    blocks = tile_s.shape[1]
    steps = list_ref[slots + UNROLL]
    copies = [
        pltpu.make_async_copy(
            obj_ref.at[a, :, pl.ds(b * LANES, LANES)], tile_s.at[a, b], sems.at[a * blocks + b]
        )
        for a in range(2)
        for b in range(blocks)
    ]
    for copy in copies:
        copy.start()
    for copy in copies:
        copy.wait()

    def leaving(n):
        turn = n & 1
        there = pl.ds(n * UNROLL, UNROLL)
        return (
            pltpu.make_async_copy(far_s.at[turn], far_ref.at[there], out_sems.at[0, turn]),
            pltpu.make_async_copy(patch_s.at[turn], patch_ref.at[there], out_sems.at[1, turn]),
        )

    lane = lax.broadcasted_iota(jnp.int32, (width, LANES), 1)

    def step(n, carry):
        turn = n & 1

        @pl.when(n >= 2)
        def _():
            for copy in leaving(n - 2):
                copy.wait()

        waves = []
        for u in range(UNROLL):
            _, row, block, shift = window_of(list_ref[n * UNROLL + u], blocks)
            back_shift = (LANES - shift) & (LANES - 1)
            own = lane < LANES - shift
            parts = []
            for a in range(2):
                left = pltpu.roll(tile_s[a, block, pl.ds(row, width), :], back_shift, 1)
                right = pltpu.roll(tile_s[a, block + 1, pl.ds(row, width), :], back_shift, 1)
                rounded = jnp.where(own, left, right).astype(jnp.bfloat16)
                patch_s[turn, u, a] = rounded
                parts.append(rounded.astype(jnp.float32))
            obj_r, obj_i = parts
            for k in range(modes):
                p_r = probe_ref[k, 0]
                p_i = probe_ref[k, 1]
                waves.append(
                    jnp.concatenate(
                        [p_r * obj_r - p_i * obj_i, p_r * obj_i + p_i * obj_r], axis=1
                    ).astype(jnp.bfloat16)
                )
        half = jnp.dot(jnp.concatenate(waves, axis=0), y_ref[...], preferred_element_type=jnp.float32)
        far = jnp.dot(
            x_ref[...], stack(half.astype(jnp.bfloat16), width), preferred_element_type=jnp.float32
        )
        for u in range(UNROLL):
            far_s[turn, u] = far[:, u * modes * width : (u + 1) * modes * width]
        for copy in leaving(n):
            copy.start()
        return carry

    lax.fori_loop(0, steps, step, jnp.int32(0))
    for late in (2, 1):

        @pl.when(steps >= late)
        def _():
            for copy in leaving(steps - late):
                copy.wait()


def backward_kernel(
    slots,
    list_ref,
    far_ref,
    patch_ref,
    probe_ref,
    meas_ref,
    x_ref,
    y_ref,
    grad_ref,
    sums_ref,
    acc_s,
    probe_s,
    misfit_s,
    far_s,
    patch_s,
    sems,
    in_sems,
):
    width = LANES
    modes = probe_ref.shape[0]
    blocks = acc_s.shape[1]
    steps = list_ref[slots + UNROLL]

    def coming(n):
        turn = n & 1
        there = pl.ds(n * UNROLL, UNROLL)
        return (
            pltpu.make_async_copy(far_ref.at[there], far_s.at[turn], in_sems.at[0, turn]),
            pltpu.make_async_copy(patch_ref.at[there], patch_s.at[turn], in_sems.at[1, turn]),
        )

    @pl.when(steps > 0)
    def _():
        for copy in coming(0):
            copy.start()

    acc_s[...] = jnp.zeros_like(acc_s)
    probe_s[...] = jnp.zeros_like(probe_s)
    misfit_s[...] = jnp.zeros_like(misfit_s)
    lane = lax.broadcasted_iota(jnp.int32, (width, LANES), 1)

    def step(n, carry):
        turn = n & 1

        @pl.when(n + 1 < steps)
        def _():
            for copy in coming(n + 1):
                copy.start()

        for copy in coming(n):
            copy.wait()
        entries = [list_ref[n * UNROLL + u] for u in range(UNROLL)]
        residuals = []
        for u in range(UNROLL):
            slot = lax.shift_right_logical(entries[u], TILE_SHIFT)
            intensity = jnp.ones((width, LANES), jnp.float32)
            for k in range(modes):
                f_r = far_s[turn, u, pl.ds(0, width), pl.ds(k * width, width)]
                f_i = far_s[turn, u, pl.ds(width, width), pl.ds(k * width, width)]
                intensity = intensity + (f_r * f_r + f_i * f_i)
            data = meas_ref[jnp.minimum(slot, slots - 1)].astype(jnp.float32)
            inverse = lax.rsqrt(intensity)
            gap = intensity * inverse - data
            misfit_s[slot] = jnp.sum(gap * gap, axis=0, keepdims=True)
            factor = jnp.where(slot < slots, 1.0 - data * inverse, 0.0)
            for k in range(modes):
                f_r = far_s[turn, u, pl.ds(0, width), pl.ds(k * width, width)]
                f_i = far_s[turn, u, pl.ds(width, width), pl.ds(k * width, width)]
                residuals.append(jnp.concatenate([f_r * factor, f_i * factor], axis=1).astype(jnp.bfloat16))
        half = jnp.dot(jnp.concatenate(residuals, axis=0), x_ref[...], preferred_element_type=jnp.float32)
        back = jnp.dot(
            y_ref[...], stack(half.astype(jnp.bfloat16), width), preferred_element_type=jnp.float32
        )
        objs = [[patch_s[turn, u, a].astype(jnp.float32) for a in range(2)] for u in range(UNROLL)]
        parts = [[0.0, 0.0] for _ in range(UNROLL)]
        for k in range(modes):
            p_r = probe_ref[k, 0]
            p_i = probe_ref[k, 1]
            sum_r = probe_s[k, 0]
            sum_i = probe_s[k, 1]
            for u in range(UNROLL):
                at = (u * modes + k) * width
                b_r = back[:width, at : at + width]
                b_i = back[width:, at : at + width]
                obj_r, obj_i = objs[u]
                parts[u][0] = parts[u][0] + (p_r * b_r + p_i * b_i)
                parts[u][1] = parts[u][1] + (p_r * b_i - p_i * b_r)
                sum_r = sum_r + (obj_r * b_r + obj_i * b_i)
                sum_i = sum_i + (obj_r * b_i - obj_i * b_r)
            probe_s[k, 0] = sum_r
            probe_s[k, 1] = sum_i
        for u in range(UNROLL):
            _, row, block, shift = window_of(entries[u], blocks)
            keep = lane >= shift
            for a in range(2):
                turned = pltpu.roll(parts[u][a], shift & (LANES - 1), 1)
                spot = (a, block, pl.ds(row, width), slice(None))
                acc_s[spot] = acc_s[spot] + jnp.where(keep, turned, 0.0)
                spot = (a, block + 1, pl.ds(row, width), slice(None))
                acc_s[spot] = acc_s[spot] + jnp.where(keep, 0.0, turned)
        return carry

    lax.fori_loop(0, steps, step, jnp.int32(0))
    groups = sums_ref.shape[0]
    rows = sums_ref.shape[1] - 8
    copies = [
        pltpu.make_async_copy(
            acc_s.at[a, b], grad_ref.at[a, :, pl.ds(b * LANES, LANES)], sems.at[a * blocks + b]
        )
        for a in range(2)
        for b in range(blocks)
    ]
    for copy in copies:
        copy.start()
    per_plane = width // rows
    for g in range(groups):
        plane, part = divmod(g, per_plane)
        sums_ref[g, pl.ds(0, rows), :] = probe_s[plane // 2, plane % 2, pl.ds(part * rows, rows), :]
        for s in range(CAP):
            sums_ref[g, pl.ds(rows + s, 1), :] = misfit_s[g * CAP + s]
        sums_ref[g, pl.ds(rows + CAP, 8 - CAP), :] = jnp.zeros((8 - CAP, LANES), jnp.float32)
    for copy in copies:
        copy.wait()


def receive_kernel(scale, pixels, slot_ref, sums_ref, probe_ref, misfit_ref):
    groups, rows = sums_ref.shape[0], probe_ref.shape[0]
    total = jnp.zeros((rows, LANES), jnp.float32)
    for g in range(groups):
        total = total + sums_ref[g, pl.ds(0, rows), :]
    probe_ref[...] = total * scale
    for i in range(slot_ref.shape[0]):
        slot = slot_ref[i]
        picked = sums_ref[lax.shift_right_logical(slot, 1), pl.ds(rows + (slot & 1), 1), :]
        misfit_ref[i] = jnp.sum(picked) * (1.0 / pixels)


SMEM = pl.BlockSpec(memory_space=pltpu.SMEM)
VMEM = pl.BlockSpec(memory_space=pltpu.VMEM)
ANY = pl.BlockSpec(memory_space=pl.ANY)


def local(obj, probe, measured, tile_of, inner):
    cols_along = lax.axis_size("ty")
    groups = lax.axis_size("tx") * cols_along
    depth = lax.axis_size("pos")
    modes, _, width, _ = probe.shape
    tile_width = obj.shape[-1]
    blocks = tile_width // LANES
    per_device = measured.shape[0]
    positions = per_device * groups * depth
    slots = groups * CAP
    plane = ("tx", "ty")
    my_tile = lax.axis_index("tx") * cols_along + lax.axis_index("ty")
    where = jnp.stack([my_tile, lax.axis_index("pos")]).astype(jnp.int32)
    packed = (tile_of[:, 0] << TILE_SHIFT) | (inner[:, 0] << ROW_BITS) | inner[:, 1]
    sizes = (groups, depth, per_device)

    outgoing, own_slots = pl.pallas_call(
        lambda *refs: send_kernel(*sizes, *refs),
        out_shape=(
            jax.ShapeDtypeStruct((slots, width, width), measured.dtype),
            jax.ShapeDtypeStruct((per_device,), jnp.int32),
        ),
        in_specs=[SMEM, SMEM, VMEM],
        out_specs=(VMEM, SMEM),
        name="send_slots",
    )(where, packed, measured)
    arrived = lax.all_to_all(
        outgoing.reshape(groups, CAP, width, width), plane, split_axis=0, concat_axis=0, tiled=True
    ).reshape(slots, width, width)
    listed = pl.pallas_call(
        lambda *refs: list_kernel(*sizes, *refs),
        out_shape=jax.ShapeDtypeStruct((slots + 2 * UNROLL + 4,), jnp.int32),
        in_specs=[SMEM, SMEM],
        out_specs=SMEM,
        cost_estimate=pl.CostEstimate(flops=1_000_000, bytes_accessed=10_000_000, transcendentals=0),
        name="list_windows",
    )(where, packed)
    tables = [jnp.asarray(table) for table in dft_blocks(width)]
    rows = modes * 2 * width // groups
    flops = slots // 2 * modes * 2 * (2 * width) ** 2 * width * 2
    staging = [
        pltpu.VMEM((2, UNROLL, 2 * width, modes * width), jnp.float32),
        pltpu.VMEM((2, UNROLL, 2, width, width), jnp.bfloat16),
    ]
    far, patches = pl.pallas_call(
        lambda *refs: forward_kernel(slots, *refs),
        out_shape=(
            jax.ShapeDtypeStruct((slots + UNROLL, 2 * width, modes * width), jnp.float32),
            jax.ShapeDtypeStruct((slots + UNROLL, 2, width, width), jnp.bfloat16),
        ),
        in_specs=[SMEM, ANY, VMEM, VMEM, VMEM],
        out_specs=(ANY, ANY),
        scratch_shapes=[
            pltpu.VMEM((2, blocks, tile_width, LANES), jnp.float32),
            *staging,
            pltpu.SemaphoreType.DMA((2 * blocks,)),
            pltpu.SemaphoreType.DMA((2, 2)),
        ],
        compiler_params=pltpu.CompilerParams(vmem_limit_bytes=48 << 20),
        cost_estimate=pl.CostEstimate(flops=flops, bytes_accessed=40_000_000, transcendentals=0),
        name="forward_windows",
    )(listed, obj, probe, *tables)
    tile_grad, sums = pl.pallas_call(
        lambda *refs: backward_kernel(slots, *refs),
        out_shape=(
            jax.ShapeDtypeStruct(obj.shape, jnp.float32),
            jax.ShapeDtypeStruct((groups, rows + 8, LANES), jnp.float32),
        ),
        in_specs=[SMEM, ANY, ANY, VMEM, VMEM, VMEM, VMEM],
        out_specs=(ANY, VMEM),
        scratch_shapes=[
            pltpu.VMEM((2, blocks, tile_width, LANES), jnp.float32),
            pltpu.VMEM((modes, 2, width, LANES), jnp.float32),
            pltpu.VMEM((slots + 1, 1, LANES), jnp.float32),
            *staging,
            pltpu.SemaphoreType.DMA((2 * blocks,)),
            pltpu.SemaphoreType.DMA((2, 2)),
        ],
        compiler_params=pltpu.CompilerParams(vmem_limit_bytes=48 << 20),
        cost_estimate=pl.CostEstimate(flops=flops, bytes_accessed=40_000_000, transcendentals=0),
        name="backward_windows",
    )(listed, far, patches, probe, arrived, *tables)
    shares = lax.psum_scatter(tile_grad, "pos", scatter_dimension=1, tiled=True)
    sums = lax.all_to_all(sums, plane, split_axis=0, concat_axis=0, tiled=True)
    probe_part, misfit = pl.pallas_call(
        lambda *refs: receive_kernel(1.0 / positions, width * width, *refs),
        out_shape=(
            jax.ShapeDtypeStruct((rows, LANES), jnp.float32),
            jax.ShapeDtypeStruct((per_device,), jnp.float32),
        ),
        in_specs=[SMEM, VMEM],
        out_specs=(VMEM, SMEM),
        name="receive_sums",
    )(own_slots, sums)
    probe_part = jnp.sum(lax.all_gather(probe_part, "pos", axis=0), axis=0)
    probe_total = lax.all_gather(probe_part, plane, axis=0, tiled=True)
    return (shares, probe_total.reshape(modes, 2, width, width), misfit)


def solution(mesh):
    return jax.shard_map(
        local,
        mesh=mesh,
        in_specs=(P(None, "tx", "ty"), P(), P(("tx", "ty", "pos"), None, None), P(), P()),
        out_specs=(P(None, ("tx", "pos"), "ty"), P(), P(("tx", "ty", "pos"))),
        check_vma=False,
    )
```

time: 223 us -> 180 us (0.81)
  blocking collectives: 130 us -> 111 us
  Pallas kernels: 41.7 us -> 23.5 us
  waiting for transfers between devices: 24.7 us -> 14.7 us
    all_to_all x1, blocking collectives: 77 us -> 58.1 us  [local(): sums = lax.all_to_all(sums, plane, split_axis=0, concat_axis=0, tiled=True)]
    pallas_call x1, Pallas kernels: 18.6 us -> 2.56 us  [local(): pl.pallas_call(lambda *refs: send_kernel(*sizes, *refs), out_shape=(jax.S...]
    all_to_all x1, waiting for transfers between devices: 24.7 us -> 14.7 us  [local(): lax.all_to_all(outgoing.reshape(groups, CAP, width, width), plane, split_...]
    pallas_call x1 -> x2, Pallas kernels: 17.7 us -> 15.6 us  [the longest x1 8.3 us: local(): pl.pallas_call(lambda *refs: backward_kernel(slots, *refs), out_shape=(ja...]
  transfers between devices with their start and end apart: 2 -> 2, of which waited for: 1 -> 1; matrix products, arithmetic and copies ran while one was open for 0% -> 0% of each run, Pallas kernels for 2% -> 7%
where the time goes in v2:
time: 180 us; the launch traced here: 178 us
  blocking collectives  111 us (62%)
  Pallas kernels  23.5 us (13%)
  waiting for transfers between devices  14.7 us (8%)
  between operations  14.2 us (8%)
  starting transfers between devices  8.64 us (5%)
  local copies, waits for them, and re-layouts  3.47 us (2%)
  other arithmetic  2.07 us (1%)
    all_to_all x1, blocking collectives, local(): sums = lax.all_to_all(sums, plane, split_axis=0, concat_axis=0, tiled=True)  58.1 us
    all_gather x1, blocking collectives, local(): probe_total = lax.all_gather(probe_part, plane, axis=0, tiled=True)  27.1 us
    all_gather x1, blocking collectives, local(): probe_part = jnp.sum(lax.all_gather(probe_part, 'pos', axis=0), axis=0)  25.9 us
    all_to_all x1, waiting for transfers between devices, local(): lax.all_to_all(outgoing.reshape(groups, CAP, width, width), plane, split_...  14.7 us
    all_to_all x1, starting transfers between devices, local(): lax.all_to_all(outgoing.reshape(groups, CAP, width, width), plane, split_...  8.6 us
    pallas_call x1, Pallas kernels, local(): pl.pallas_call(lambda *refs: backward_kernel(slots, *refs), out_shape=(ja...  8.3 us
    pallas_call x1, Pallas kernels, local(): pl.pallas_call(lambda *refs: forward_kernel(slots, *refs), out_shape=(jax...  7.29 us
  transfers between devices with their start and end apart: 2, of which 1 were waited for; matrix products, arithmetic and copies ran while one was open for 0% of the time, Pallas kernels for 7%

profile of v2, /device:TPU:1, one launch (start us, length us, event | category | flops | bytes accessed | tf_op | source)
XLA Modules:
  0.0 177.6 jit_solution(11213498477145845118)
XLA Ops:
  7.2 0.0 copy-start.2
  7.2 0.0 copy-start.3
  7.2 0.0 copy-start.1
  7.2 0.6 pad_add_fusion.refs_0_
  7.8 1.5 slice_or_fusion
  9.3 2.6 %send_slots.1 = (bf16[64,128,128]{2,1,0:T(8,128)(2,1)}, s32[16]{0:T(128)}) custom-call(s32[2]{0:T(128)} %pad_add_fusion.refs_0_, s32[4096]{0:T(1024)} %bitcast.11, bf16[16,128,128]{2,1,0:T(8,128)(2,1)} %refs_2_.3), custom_call_target="tpu_custom_call" | custom-call | tf_op jit(solution)/shard_map/send_slots/pallas_call | solution.py:327
  11.8 8.6 %all-to-all-start = ((bf16[32,2,128,128]{3,2,1,0:T(8,128)(2,1)}), bf16[32,2,128,128]{3,2,1,0:T(8,128)(2,1)S(1)}, u32[]{:S(2)}, u32[]{:S(2)}) async-start(bf16[32,2,128,128]{3,2,1,0:T(8,128)(2,1)} %bitcast.8), calls=%async_computation | async-start | bytes 4194304 | tf_op jit(solution)/shard_map/all_to_all | solution.py:337
  20.4 0.0 reduce-scatter.2.cloned.1.call-start
  20.5 3.5 %list_windows.1.refs_0_ = s32[72]{0:T(128)} custom-call(s32[2]{0:T(128)} %pad_add_fusion.refs_0_, s32[4096]{0:T(1024)} %bitcast.12), custom_call_target="tpu_custom_call" | custom-call | flops 1000000 | bytes 10000000 | tf_op jit(solution)/shard_map/list_windows/pallas_call | solution.py:340
  24.0 0.0 copy-done.2
  24.1 0.0 copy-done.3
  24.1 0.0 copy-done.1
  24.1 0.0 copy-start.4
  24.1 0.6 copy-done.4
  24.7 0.0 copy-start.5
  24.7 7.3 %forward_windows.1 = (f32[66,256,512]{2,1,0:T(8,128)}, bf16[66,2,128,128]{3,2,1,0:T(8,128)(2,1)S(1)}) custom-call(s32[72]{0:T(128)S(1)} %copy-done.4, f32[2,768,768]{2,1,0:T(8,128)} %refs_1_.1, f32[4,2,128,128]{3,2,1,0:T(8,128)S(1)} %copy-done.1, bf16[256,256]{1,0:T(8,128)(2,1)S(1)} %copy-done.3, bf16[256,256]{1,0:T(8,128)(2,1)S(1)} %copy-done.2), custom_call_target="tpu_custom_call" | custom-call | flops 4294967296 | bytes 40000000 | tf_op jit(solution)/shard_map/forward_windows/pallas_call | solution.py:355
  32.0 0.0 copy-start
  32.0 2.0 %copy-done = bf16[66,2,128,128]{3,2,1,0:T(8,128)(2,1)} copy-done((bf16[66,2,128,128]{3,2,1,0:T(8,128)(2,1)}, bf16[66,2,128,128]{3,2,1,0:T(8,128)(2,1)S(1)}, u32[]{:S(2)}) %copy-start) | copy-done | bytes 4325400
  34.0 14.7 %all-to-all-done = bf16[32,2,128,128]{3,2,1,0:T(8,128)(2,1)S(1)} async-done(((bf16[32,2,128,128]{3,2,1,0:T(8,128)(2,1)}), bf16[32,2,128,128]{3,2,1,0:T(8,128)(2,1)S(1)}, u32[]{:S(2)}, u32[]{:S(2)}) %all-to-all-start) | async-done | bytes 2097184 | tf_op jit(solution)/shard_map/all_to_all | solution.py:337
  48.7 0.0 copy-done.5
  48.7 8.3 %backward_windows.1 = (f32[2,768,768]{2,1,0:T(8,128)}, f32[32,40,128]{2,1,0:T(8,128)S(1)}) custom-call(s32[72]{0:T(128)S(1)} %copy-done.5, f32[66,256,512]{2,1,0:T(8,128)} %get-tuple-element.11.refs_1_, bf16[66,2,128,128]{3,2,1,0:T(8,128)(2,1)} %copy-done, f32[4,2,128,128]{3,2,1,0:T(8,128)S(1)} %copy-done.1, bf16[64,128,128]{2,1,0:T(8,128)(2,1)S(1)} %bitcast.7, ...), custom_call_target="tpu_custom_call" | custom-call | flops 4294967296 | bytes 40000000 | tf_op jit(solution)/shard_map/backward_windows/pallas_call | solution.py:373
  57.0 0.0 reduce-scatter.2.cloned.1.call-update
  57.1 58.1 %all_to_all.10.refs_1_ = f32[32,40,128]{2,1,0:T(8,128)} all-to-all(f32[32,40,128]{2,1,0:T(8,128)S(1)} %get-tuple-element.16), channel_id=1, replica_groups=mesh['tx'=4,'ty'=8,'pos'=8] {'tx','ty'}, dimensions={0} | all-to-all | bytes 1310720 | tf_op jit(solution)/shard_map/all_to_all | solution.py:394
  115.1 1.8 %receive_sums.1 = (f32[32,128]{1,0:T(8,128)}, f32[16]{0:T(128)}) custom-call(s32[16]{0:T(128)} %get-tuple-element.15.refs_0_, f32[32,40,128]{2,1,0:T(8,128)} %all_to_all.10.refs_1_), custom_call_target="tpu_custom_call" | custom-call | tf_op jit(solution)/shard_map/receive_sums/pallas_call | solution.py:395
  116.9 25.9 %all-gather = f32[256,128]{1,0:T(8,128)S(1)} all-gather(f32[32,128]{1,0:T(8,128)} %get-tuple-element.17), channel_id=2, replica_groups=mesh['tx'=4,'ty'=8,'pos'=8] {'pos'}, dimensions={0}, use_global_device_ids=true | all-gather | bytes 147456 | tf_op jit(solution)/shard_map/all_gather | solution.py:405
  142.9 27.1 %all_gather.11 = f32[1024,128]{1,0:T(8,128)S(1)} all-gather(f32[32,128]{1,0:T(8,128)S(1)} %reduce_sum.9), channel_id=1, replica_groups=mesh['tx'=4,'ty'=8,'pos'=8] {'tx','ty'}, dimensions={0}, use_global_device_ids=true | all-gather | bytes 540672 | tf_op jit(solution)/shard_map/all_gather | solution.py:406
  169.9 0.0 reduce-scatter.2.cloned.1.call-done
  169.9 0.8 copy.11
  (1 shorter events, 0.0 us)
Async XLA Ops:
  7.2 16.9 %copy-start.2 = (bf16[256,256]{1,0:T(8,128)(2,1)S(1)}, bf16[256,256]{1,0:T(8,128)(2,1)}, u32[]{:S(2)}) copy-start(bf16[256,256]{1,0:T(8,128)(2,1)} %constant.25.clone.refs_4_.refs_6_) | copy-start | bytes 393220
  7.2 16.9 %copy-start.3 = (bf16[256,256]{1,0:T(8,128)(2,1)S(1)}, bf16[256,256]{1,0:T(8,128)(2,1)}, u32[]{:S(2)}) copy-start(bf16[256,256]{1,0:T(8,128)(2,1)} %constant.24.clone.refs_3_.refs_5_) | copy-start | bytes 393220
  7.2 16.9 %copy-start.1 = (f32[4,2,128,128]{3,2,1,0:T(8,128)S(1)}, f32[4,2,128,128]{3,2,1,0:T(8,128)}, u32[]{:S(2)}) copy-start(f32[4,2,128,128]{3,2,1,0:T(8,128)} %refs_3_.2) | copy-start | bytes 1572868
  11.8 36.9 %all-to-all-start = ((bf16[32,2,128,128]{3,2,1,0:T(8,128)(2,1)}), bf16[32,2,128,128]{3,2,1,0:T(8,128)(2,1)S(1)}, u32[]{:S(2)}, u32[]{:S(2)}) async-start(bf16[32,2,128,128]{3,2,1,0:T(8,128)(2,1)} %bitcast.8), calls=%async_computation | async-start | bytes 4194304 | tf_op jit(solution)/shard_map/all_to_all | solution.py:337
  20.4 149.5 %reduce-scatter.2.cloned.1.call-start = ((), (), s32[]{:S(2)}) async-start(), calls=%async_computation.3 | async-start | bytes 5308416 | tf_op jit(solution)/shard_map/reduce_scatter | solution.py:393
  24.1 0.7 copy-start.4
  24.7 24.0 %copy-start.5 = (s32[72]{0:T(128)S(1)}, s32[72]{0:T(128)}, u32[]{:S(2)}) copy-start(s32[72]{0:T(128)} %list_windows.1.refs_0_) | copy-start | bytes 868
  32.0 2.0 %copy-start = (bf16[66,2,128,128]{3,2,1,0:T(8,128)(2,1)}, bf16[66,2,128,128]{3,2,1,0:T(8,128)(2,1)S(1)}, u32[]{:S(2)}) copy-start(bf16[66,2,128,128]{3,2,1,0:T(8,128)(2,1)S(1)} %get-tuple-element.12.refs_2_) | copy-start | bytes 12976132
Sparse Core Ops, SparseCore 0:
  57.2 101.9 reduce-scatter.1

commit v3 on v2

--- a/solution.py
+++ b/solution.py
@@ -308,13 +308,61 @@
 ANY = pl.BlockSpec(memory_space=pl.ANY)
 
 
+def kernels(tile_shape, modes, width, slots, per_device, groups):
+    tile_width = tile_shape[-1]
+    blocks = tile_width // LANES
+    rows = modes * 2 * width // groups
+    flops = slots // 2 * modes * 2 * (2 * width) ** 2 * width * 2
+    staging = [
+        pltpu.VMEM((2, UNROLL, 2 * width, modes * width), jnp.float32),
+        pltpu.VMEM((2, UNROLL, 2, width, width), jnp.bfloat16),
+    ]
+    forward = pl.pallas_call(
+        lambda *refs: forward_kernel(slots, *refs),
+        out_shape=(
+            jax.ShapeDtypeStruct((slots + UNROLL, 2 * width, modes * width), jnp.float32),
+            jax.ShapeDtypeStruct((slots + UNROLL, 2, width, width), jnp.bfloat16),
+        ),
+        in_specs=[SMEM, ANY, VMEM, VMEM, VMEM],
+        out_specs=(ANY, ANY),
+        scratch_shapes=[
+            pltpu.VMEM((2, blocks, tile_width, LANES), jnp.float32),
+            *staging,
+            pltpu.SemaphoreType.DMA((2 * blocks,)),
+            pltpu.SemaphoreType.DMA((2, 2)),
+        ],
+        compiler_params=pltpu.CompilerParams(vmem_limit_bytes=48 << 20),
+        cost_estimate=pl.CostEstimate(flops=flops, bytes_accessed=40_000_000, transcendentals=0),
+        name="forward_windows",
+    )
+    backward = pl.pallas_call(
+        lambda *refs: backward_kernel(slots, *refs),
+        out_shape=(
+            jax.ShapeDtypeStruct(tile_shape, jnp.float32),
+            jax.ShapeDtypeStruct((groups, rows + 8, LANES), jnp.float32),
+        ),
+        in_specs=[SMEM, ANY, ANY, VMEM, VMEM, VMEM, VMEM],
+        out_specs=(ANY, VMEM),
+        scratch_shapes=[
+            pltpu.VMEM((2, blocks, tile_width, LANES), jnp.float32),
+            pltpu.VMEM((modes, 2, width, LANES), jnp.float32),
+            pltpu.VMEM((slots + 1, 1, LANES), jnp.float32),
+            *staging,
+            pltpu.SemaphoreType.DMA((2 * blocks,)),
+            pltpu.SemaphoreType.DMA((2, 2)),
+        ],
+        compiler_params=pltpu.CompilerParams(vmem_limit_bytes=48 << 20),
+        cost_estimate=pl.CostEstimate(flops=flops, bytes_accessed=40_000_000, transcendentals=0),
+        name="backward_windows",
+    )
+    return forward, backward
+
+
 def local(obj, probe, measured, tile_of, inner):
     cols_along = lax.axis_size("ty")
     groups = lax.axis_size("tx") * cols_along
     depth = lax.axis_size("pos")
     modes, _, width, _ = probe.shape
-    tile_width = obj.shape[-1]
-    blocks = tile_width // LANES
     per_device = measured.shape[0]
     positions = per_device * groups * depth
     slots = groups * CAP
@@ -347,49 +395,9 @@
     )(where, packed)
     tables = [jnp.asarray(table) for table in dft_blocks(width)]
     rows = modes * 2 * width // groups
-    flops = slots // 2 * modes * 2 * (2 * width) ** 2 * width * 2
-    staging = [
-        pltpu.VMEM((2, UNROLL, 2 * width, modes * width), jnp.float32),
-        pltpu.VMEM((2, UNROLL, 2, width, width), jnp.bfloat16),
-    ]
-    far, patches = pl.pallas_call(
-        lambda *refs: forward_kernel(slots, *refs),
-        out_shape=(
-            jax.ShapeDtypeStruct((slots + UNROLL, 2 * width, modes * width), jnp.float32),
-            jax.ShapeDtypeStruct((slots + UNROLL, 2, width, width), jnp.bfloat16),
-        ),
-        in_specs=[SMEM, ANY, VMEM, VMEM, VMEM],
-        out_specs=(ANY, ANY),
-        scratch_shapes=[
-            pltpu.VMEM((2, blocks, tile_width, LANES), jnp.float32),
-            *staging,
-            pltpu.SemaphoreType.DMA((2 * blocks,)),
-            pltpu.SemaphoreType.DMA((2, 2)),
-        ],
-        compiler_params=pltpu.CompilerParams(vmem_limit_bytes=48 << 20),
-        cost_estimate=pl.CostEstimate(flops=flops, bytes_accessed=40_000_000, transcendentals=0),
-        name="forward_windows",
-    )(listed, obj, probe, *tables)
-    tile_grad, sums = pl.pallas_call(
-        lambda *refs: backward_kernel(slots, *refs),
-        out_shape=(
-            jax.ShapeDtypeStruct(obj.shape, jnp.float32),
-            jax.ShapeDtypeStruct((groups, rows + 8, LANES), jnp.float32),
-        ),
-        in_specs=[SMEM, ANY, ANY, VMEM, VMEM, VMEM, VMEM],
-        out_specs=(ANY, VMEM),
-        scratch_shapes=[
-            pltpu.VMEM((2, blocks, tile_width, LANES), jnp.float32),
-            pltpu.VMEM((modes, 2, width, LANES), jnp.float32),
-            pltpu.VMEM((slots + 1, 1, LANES), jnp.float32),
-            *staging,
-            pltpu.SemaphoreType.DMA((2 * blocks,)),
-            pltpu.SemaphoreType.DMA((2, 2)),
-        ],
-        compiler_params=pltpu.CompilerParams(vmem_limit_bytes=48 << 20),
-        cost_estimate=pl.CostEstimate(flops=flops, bytes_accessed=40_000_000, transcendentals=0),
-        name="backward_windows",
-    )(listed, far, patches, probe, arrived, *tables)
+    forward, backward = kernels(obj.shape, modes, width, slots, per_device, groups)
+    far, patches = forward(listed, obj, probe, *tables)
+    tile_grad, sums = backward(listed, far, patches, probe, arrived, *tables)
     shares = lax.psum_scatter(tile_grad, "pos", scatter_dimension=1, tiled=True)
     sums = lax.all_to_all(sums, plane, split_axis=0, concat_axis=0, tiled=True)
     probe_part, misfit = pl.pallas_call(

time: 180 us -> 180 us (level)
  Pallas kernels: 23.5 us -> 27.4 us
    pallas_call x2, Pallas kernels: 15.6 us -> 19.5 us  [the longest x1 10.5 us: local(): tile_grad, sums = backward(listed, far, patches, probe, arrived, *tables)]
  transfers between devices with their start and end apart: 2 -> 2, of which waited for: 1 -> 1; matrix products, arithmetic and copies ran while one was open for 0% -> 0% of each run, Pallas kernels for 7% -> 8%
where the time goes in v3:
time: 180 us; the launch traced here: 179 us
  blocking collectives  110 us (61%)
  Pallas kernels  27.4 us (15%)
  between operations  14.2 us (8%)
  waiting for transfers between devices  13 us (7%)
  starting transfers between devices  8.64 us (5%)
  local copies, waits for them, and re-layouts  3.47 us (2%)
  other arithmetic  2.07 us (1%)
    all_to_all x1, blocking collectives, local(): sums = lax.all_to_all(sums, plane, split_axis=0, concat_axis=0, tiled=True)  57.5 us
    all_gather x1, blocking collectives, local(): probe_total = lax.all_gather(probe_part, plane, axis=0, tiled=True)  26.9 us
    all_gather x1, blocking collectives, local(): probe_part = jnp.sum(lax.all_gather(probe_part, 'pos', axis=0), axis=0)  25.9 us
    all_to_all x1, waiting for transfers between devices, local(): lax.all_to_all(outgoing.reshape(groups, CAP, width, width), plane, split_...  13 us
    pallas_call x1, Pallas kernels, local(): tile_grad, sums = backward(listed, far, patches, probe, arrived, *tables)  10.5 us
    pallas_call x1, Pallas kernels, local(): far, patches = forward(listed, obj, probe, *tables)  8.99 us
    all_to_all x1, starting transfers between devices, local(): lax.all_to_all(outgoing.reshape(groups, CAP, width, width), plane, split_...  8.6 us
  transfers between devices with their start and end apart: 2, of which 1 were waited for; matrix products, arithmetic and copies ran while one was open for 0% of the time, Pallas kernels for 8%

profile of v3, /device:TPU:1, one launch (start us, length us, event | category | flops | bytes accessed | tf_op | source)
XLA Modules:
  0.0 179.1 jit_solution(11213498477145845118)
XLA Ops:
  7.2 0.0 copy-start.2
  7.2 0.0 copy-start.3
  7.2 0.0 copy-start.1
  7.2 0.6 pad_add_fusion.refs_0_
  7.8 1.5 slice_or_fusion
  9.3 2.6 %send_slots.1 = (bf16[64,128,128]{2,1,0:T(8,128)(2,1)}, s32[16]{0:T(128)}) custom-call(s32[2]{0:T(128)} %pad_add_fusion.refs_0_, s32[4096]{0:T(1024)} %bitcast.11, bf16[16,128,128]{2,1,0:T(8,128)(2,1)} %refs_2_.3), custom_call_target="tpu_custom_call" | custom-call | tf_op jit(solution)/shard_map/send_slots/pallas_call | solution.py:375
  11.8 8.6 %all-to-all-start = ((bf16[32,2,128,128]{3,2,1,0:T(8,128)(2,1)}), bf16[32,2,128,128]{3,2,1,0:T(8,128)(2,1)S(1)}, u32[]{:S(2)}, u32[]{:S(2)}) async-start(bf16[32,2,128,128]{3,2,1,0:T(8,128)(2,1)} %bitcast.8), calls=%async_computation | async-start | bytes 4194304 | tf_op jit(solution)/shard_map/all_to_all | solution.py:385
  20.4 0.0 reduce-scatter.2.cloned.1.call-start
  20.5 3.5 %list_windows.1.refs_0_ = s32[72]{0:T(128)} custom-call(s32[2]{0:T(128)} %pad_add_fusion.refs_0_, s32[4096]{0:T(1024)} %bitcast.12), custom_call_target="tpu_custom_call" | custom-call | flops 1000000 | bytes 10000000 | tf_op jit(solution)/shard_map/list_windows/pallas_call | solution.py:388
  24.0 0.0 copy-done.2
  24.1 0.0 copy-done.3
  24.1 0.0 copy-done.1
  24.1 0.0 copy-start.4
  24.1 0.6 copy-done.4
  24.7 0.0 copy-start.5
  24.7 9.0 %forward_windows.1 = (f32[66,256,512]{2,1,0:T(8,128)}, bf16[66,2,128,128]{3,2,1,0:T(8,128)(2,1)S(1)}) custom-call(s32[72]{0:T(128)S(1)} %copy-done.4, f32[2,768,768]{2,1,0:T(8,128)} %refs_1_.1, f32[4,2,128,128]{3,2,1,0:T(8,128)S(1)} %copy-done.1, bf16[256,256]{1,0:T(8,128)(2,1)S(1)} %copy-done.3, bf16[256,256]{1,0:T(8,128)(2,1)S(1)} %copy-done.2), custom_call_target="tpu_custom_call" | custom-call | flops 4294967296 | bytes 40000000 | tf_op jit(solution)/shard_map/forward_windows/pallas_call | solution.py:399
  33.7 0.0 copy-start
  33.7 2.0 %copy-done = bf16[66,2,128,128]{3,2,1,0:T(8,128)(2,1)} copy-done((bf16[66,2,128,128]{3,2,1,0:T(8,128)(2,1)}, bf16[66,2,128,128]{3,2,1,0:T(8,128)(2,1)S(1)}, u32[]{:S(2)}) %copy-start) | copy-done | bytes 4325400
  35.7 13.0 %all-to-all-done = bf16[32,2,128,128]{3,2,1,0:T(8,128)(2,1)S(1)} async-done(((bf16[32,2,128,128]{3,2,1,0:T(8,128)(2,1)}), bf16[32,2,128,128]{3,2,1,0:T(8,128)(2,1)S(1)}, u32[]{:S(2)}, u32[]{:S(2)}) %all-to-all-start) | async-done | bytes 2097184 | tf_op jit(solution)/shard_map/all_to_all | solution.py:385
  48.7 0.0 copy-done.5
  48.7 10.5 %backward_windows.1 = (f32[2,768,768]{2,1,0:T(8,128)}, f32[32,40,128]{2,1,0:T(8,128)S(1)}) custom-call(s32[72]{0:T(128)S(1)} %copy-done.5, f32[66,256,512]{2,1,0:T(8,128)} %get-tuple-element.11.refs_1_, bf16[66,2,128,128]{3,2,1,0:T(8,128)(2,1)} %copy-done, f32[4,2,128,128]{3,2,1,0:T(8,128)S(1)} %copy-done.1, bf16[64,128,128]{2,1,0:T(8,128)(2,1)S(1)} %bitcast.7, ...), custom_call_target="tpu_custom_call" | custom-call | flops 4294967296 | bytes 40000000 | tf_op jit(solution)/shard_map/backward_windows/pallas_call | solution.py:400
  59.3 0.0 reduce-scatter.2.cloned.1.call-update
  59.3 57.5 %all_to_all.10.refs_1_ = f32[32,40,128]{2,1,0:T(8,128)} all-to-all(f32[32,40,128]{2,1,0:T(8,128)S(1)} %get-tuple-element.16), channel_id=1, replica_groups=mesh['tx'=4,'ty'=8,'pos'=8] {'tx','ty'}, dimensions={0} | all-to-all | bytes 1310720 | tf_op jit(solution)/shard_map/all_to_all | solution.py:402
  116.8 1.8 receive_sums.1
  118.6 25.9 %all-gather = f32[256,128]{1,0:T(8,128)S(1)} all-gather(f32[32,128]{1,0:T(8,128)} %get-tuple-element.17), channel_id=2, replica_groups=mesh['tx'=4,'ty'=8,'pos'=8] {'pos'}, dimensions={0}, use_global_device_ids=true | all-gather | bytes 147456 | tf_op jit(solution)/shard_map/all_gather | solution.py:413
  144.5 26.9 %all_gather.11 = f32[1024,128]{1,0:T(8,128)S(1)} all-gather(f32[32,128]{1,0:T(8,128)S(1)} %reduce_sum.9), channel_id=1, replica_groups=mesh['tx'=4,'ty'=8,'pos'=8] {'tx','ty'}, dimensions={0}, use_global_device_ids=true | all-gather | bytes 540672 | tf_op jit(solution)/shard_map/all_gather | solution.py:414
  171.4 0.0 reduce-scatter.2.cloned.1.call-done
  171.4 0.8 copy.11
  (1 shorter events, 0.0 us)
Async XLA Ops:
  7.2 16.9 %copy-start.2 = (bf16[256,256]{1,0:T(8,128)(2,1)S(1)}, bf16[256,256]{1,0:T(8,128)(2,1)}, u32[]{:S(2)}) copy-start(bf16[256,256]{1,0:T(8,128)(2,1)} %constant.25.clone.refs_4_.refs_6_) | copy-start | bytes 393220
  7.2 16.9 %copy-start.3 = (bf16[256,256]{1,0:T(8,128)(2,1)S(1)}, bf16[256,256]{1,0:T(8,128)(2,1)}, u32[]{:S(2)}) copy-start(bf16[256,256]{1,0:T(8,128)(2,1)} %constant.24.clone.refs_3_.refs_5_) | copy-start | bytes 393220
  7.2 16.9 %copy-start.1 = (f32[4,2,128,128]{3,2,1,0:T(8,128)S(1)}, f32[4,2,128,128]{3,2,1,0:T(8,128)}, u32[]{:S(2)}) copy-start(f32[4,2,128,128]{3,2,1,0:T(8,128)} %refs_3_.2) | copy-start | bytes 1572868
  11.8 36.9 %all-to-all-start = ((bf16[32,2,128,128]{3,2,1,0:T(8,128)(2,1)}), bf16[32,2,128,128]{3,2,1,0:T(8,128)(2,1)S(1)}, u32[]{:S(2)}, u32[]{:S(2)}) async-start(bf16[32,2,128,128]{3,2,1,0:T(8,128)(2,1)} %bitcast.8), calls=%async_computation | async-start | bytes 4194304 | tf_op jit(solution)/shard_map/all_to_all | solution.py:385
  20.4 151.0 %reduce-scatter.2.cloned.1.call-start = ((), (), s32[]{:S(2)}) async-start(), calls=%async_computation.3 | async-start | bytes 5308416 | tf_op jit(solution)/shard_map/reduce_scatter | solution.py:401
  24.1 0.7 copy-start.4
  24.7 24.0 %copy-start.5 = (s32[72]{0:T(128)S(1)}, s32[72]{0:T(128)}, u32[]{:S(2)}) copy-start(s32[72]{0:T(128)} %list_windows.1.refs_0_) | copy-start | bytes 868
  33.7 2.0 %copy-start = (bf16[66,2,128,128]{3,2,1,0:T(8,128)(2,1)}, bf16[66,2,128,128]{3,2,1,0:T(8,128)(2,1)S(1)}, u32[]{:S(2)}) copy-start(bf16[66,2,128,128]{3,2,1,0:T(8,128)(2,1)S(1)} %get-tuple-element.12.refs_2_) | copy-start | bytes 12976132
Sparse Core Ops, SparseCore 0:
  59.4 101.4 reduce-scatter.1

commit v4 on v3

--- a/solution.py
+++ b/solution.py
@@ -8,7 +8,8 @@
 from jax.sharding import PartitionSpec as P
 
 CAP = 2
-UNROLL = 2
+UNROLL = 4
+STRIP = 16
 LANES = 128
 ROW_BITS = 10
 TILE_SHIFT = 2 * ROW_BITS
@@ -67,13 +68,14 @@
     return slot, row, block, col - block * LANES
 
 
-def stack(half, width):
-    fields = half.shape[0] // width
-    columns = []
-    for f in range(fields):
-        rows = half[f * width : (f + 1) * width]
-        columns.append(jnp.concatenate([rows[:, :width], rows[:, width:]], axis=0))
-    return jnp.concatenate(columns, axis=1)
+def right_product(field_s, table_ref, half_s, u):
+    width = LANES
+    half = jnp.dot(field_s[u], table_ref[...], preferred_element_type=jnp.float32)
+    for k in range(field_s.shape[1] // width):
+        for h in range(2):
+            half_s[u, pl.ds(h * width, width), pl.ds(k * width, width)] = half[
+                k * width : (k + 1) * width, h * width : (h + 1) * width
+            ].astype(jnp.bfloat16)
 
 
 def forward_kernel(
@@ -88,6 +90,8 @@
     tile_s,
     far_s,
     patch_s,
+    field_s,
+    half_s,
     sems,
     out_sems,
 ):
@@ -115,7 +119,7 @@
             pltpu.make_async_copy(patch_s.at[turn], patch_ref.at[there], out_sems.at[1, turn]),
         )
 
-    lane = lax.broadcasted_iota(jnp.int32, (width, LANES), 1)
+    lane = lax.broadcasted_iota(jnp.int32, (STRIP, LANES), 1)
 
     def step(n, carry):
         turn = n & 1
@@ -125,33 +129,33 @@
             for copy in leaving(n - 2):
                 copy.wait()
 
-        waves = []
+        places = [window_of(list_ref[n * UNROLL + u], blocks) for u in range(UNROLL)]
+        for s in range(0, width, STRIP):
+            objs = []
+            for u in range(UNROLL):
+                _, row, block, shift = places[u]
+                back_shift = (LANES - shift) & (LANES - 1)
+                own = lane < LANES - shift
+                parts = []
+                for a in range(2):
+                    left = pltpu.roll(tile_s[a, block, pl.ds(row + s, STRIP), :], back_shift, 1)
+                    right = pltpu.roll(tile_s[a, block + 1, pl.ds(row + s, STRIP), :], back_shift, 1)
+                    rounded = jnp.where(own, left, right).astype(jnp.bfloat16)
+                    patch_s[turn, u, a, pl.ds(s, STRIP), :] = rounded
+                    parts.append(rounded.astype(jnp.float32))
+                objs.append(parts)
+            for k in range(modes):
+                p_r = probe_ref[k, 0, pl.ds(s, STRIP), :]
+                p_i = probe_ref[k, 1, pl.ds(s, STRIP), :]
+                for u in range(UNROLL):
+                    o_r, o_i = objs[u]
+                    at = pl.ds(k * width + s, STRIP)
+                    field_s[u, at, pl.ds(0, width)] = (p_r * o_r - p_i * o_i).astype(jnp.bfloat16)
+                    field_s[u, at, pl.ds(width, width)] = (p_r * o_i + p_i * o_r).astype(jnp.bfloat16)
         for u in range(UNROLL):
-            _, row, block, shift = window_of(list_ref[n * UNROLL + u], blocks)
-            back_shift = (LANES - shift) & (LANES - 1)
-            own = lane < LANES - shift
-            parts = []
-            for a in range(2):
-                left = pltpu.roll(tile_s[a, block, pl.ds(row, width), :], back_shift, 1)
-                right = pltpu.roll(tile_s[a, block + 1, pl.ds(row, width), :], back_shift, 1)
-                rounded = jnp.where(own, left, right).astype(jnp.bfloat16)
-                patch_s[turn, u, a] = rounded
-                parts.append(rounded.astype(jnp.float32))
-            obj_r, obj_i = parts
-            for k in range(modes):
-                p_r = probe_ref[k, 0]
-                p_i = probe_ref[k, 1]
-                waves.append(
-                    jnp.concatenate(
-                        [p_r * obj_r - p_i * obj_i, p_r * obj_i + p_i * obj_r], axis=1
-                    ).astype(jnp.bfloat16)
-                )
-        half = jnp.dot(jnp.concatenate(waves, axis=0), y_ref[...], preferred_element_type=jnp.float32)
-        far = jnp.dot(
-            x_ref[...], stack(half.astype(jnp.bfloat16), width), preferred_element_type=jnp.float32
-        )
+            right_product(field_s, y_ref, half_s, u)
         for u in range(UNROLL):
-            far_s[turn, u] = far[:, u * modes * width : (u + 1) * modes * width]
+            far_s[turn, u] = jnp.dot(x_ref[...], half_s[u], preferred_element_type=jnp.float32)
         for copy in leaving(n):
             copy.start()
         return carry
@@ -181,6 +185,9 @@
     misfit_s,
     far_s,
     patch_s,
+    field_s,
+    half_s,
+    back_s,
     sems,
     in_sems,
 ):
@@ -205,7 +212,7 @@
     acc_s[...] = jnp.zeros_like(acc_s)
     probe_s[...] = jnp.zeros_like(probe_s)
     misfit_s[...] = jnp.zeros_like(misfit_s)
-    lane = lax.broadcasted_iota(jnp.int32, (width, LANES), 1)
+    lane = lax.broadcasted_iota(jnp.int32, (STRIP, LANES), 1)
 
     def step(n, carry):
         turn = n & 1
@@ -218,54 +225,62 @@
         for copy in coming(n):
             copy.wait()
         entries = [list_ref[n * UNROLL + u] for u in range(UNROLL)]
-        residuals = []
         for u in range(UNROLL):
             slot = lax.shift_right_logical(entries[u], TILE_SHIFT)
-            intensity = jnp.ones((width, LANES), jnp.float32)
+            held = jnp.minimum(slot, slots - 1)
+            misfit = jnp.zeros((STRIP, LANES), jnp.float32)
+            for s in range(0, width, STRIP):
+                fields = [
+                    far_s[turn, u, pl.ds(h * width + s, STRIP), pl.ds(k * width, width)]
+                    for k in range(modes)
+                    for h in range(2)
+                ]
+                intensity = 1.0 + sum(f * f for f in fields)
+                data = meas_ref[held, pl.ds(s, STRIP), :].astype(jnp.float32)
+                inverse = lax.rsqrt(intensity)
+                gap = intensity * inverse - data
+                misfit = misfit + gap * gap
+                factor = jnp.where(slot < slots, 1.0 - data * inverse, 0.0)
+                for k in range(modes):
+                    for h in range(2):
+                        field_s[u, pl.ds(k * width + s, STRIP), pl.ds(h * width, width)] = (
+                            fields[2 * k + h] * factor
+                        ).astype(jnp.bfloat16)
+            misfit_s[slot] = jnp.sum(misfit, axis=0, keepdims=True)
+        for u in range(UNROLL):
+            right_product(field_s, x_ref, half_s, u)
+        for u in range(UNROLL):
+            back_s[u] = jnp.dot(y_ref[...], half_s[u], preferred_element_type=jnp.float32)
+        places = [window_of(entries[u], blocks) for u in range(UNROLL)]
+        for s in range(0, width, STRIP):
+            rows = pl.ds(s, STRIP)
+            objs = [[patch_s[turn, u, a, rows, :].astype(jnp.float32) for a in range(2)] for u in range(UNROLL)]
+            parts = [[None, None] for _ in range(UNROLL)]
             for k in range(modes):
-                f_r = far_s[turn, u, pl.ds(0, width), pl.ds(k * width, width)]
-                f_i = far_s[turn, u, pl.ds(width, width), pl.ds(k * width, width)]
-                intensity = intensity + (f_r * f_r + f_i * f_i)
-            data = meas_ref[jnp.minimum(slot, slots - 1)].astype(jnp.float32)
-            inverse = lax.rsqrt(intensity)
-            gap = intensity * inverse - data
-            misfit_s[slot] = jnp.sum(gap * gap, axis=0, keepdims=True)
-            factor = jnp.where(slot < slots, 1.0 - data * inverse, 0.0)
-            for k in range(modes):
-                f_r = far_s[turn, u, pl.ds(0, width), pl.ds(k * width, width)]
-                f_i = far_s[turn, u, pl.ds(width, width), pl.ds(k * width, width)]
-                residuals.append(jnp.concatenate([f_r * factor, f_i * factor], axis=1).astype(jnp.bfloat16))
-        half = jnp.dot(jnp.concatenate(residuals, axis=0), x_ref[...], preferred_element_type=jnp.float32)
-        back = jnp.dot(
-            y_ref[...], stack(half.astype(jnp.bfloat16), width), preferred_element_type=jnp.float32
-        )
-        objs = [[patch_s[turn, u, a].astype(jnp.float32) for a in range(2)] for u in range(UNROLL)]
-        parts = [[0.0, 0.0] for _ in range(UNROLL)]
-        for k in range(modes):
-            p_r = probe_ref[k, 0]
-            p_i = probe_ref[k, 1]
-            sum_r = probe_s[k, 0]
-            sum_i = probe_s[k, 1]
+                p_r = probe_ref[k, 0, rows, :]
+                p_i = probe_ref[k, 1, rows, :]
+                sum_r = probe_s[k, 0, rows, :]
+                sum_i = probe_s[k, 1, rows, :]
+                for u in range(UNROLL):
+                    b_r = back_s[u, rows, pl.ds(k * width, width)]
+                    b_i = back_s[u, pl.ds(width + s, STRIP), pl.ds(k * width, width)]
+                    o_r, o_i = objs[u]
+                    new_r = p_r * b_r + p_i * b_i
+                    new_i = p_r * b_i - p_i * b_r
+                    parts[u] = [new_r, new_i] if k == 0 else [parts[u][0] + new_r, parts[u][1] + new_i]
+                    sum_r = sum_r + (o_r * b_r + o_i * b_i)
+                    sum_i = sum_i + (o_r * b_i - o_i * b_r)
+                probe_s[k, 0, rows, :] = sum_r
+                probe_s[k, 1, rows, :] = sum_i
             for u in range(UNROLL):
-                at = (u * modes + k) * width
-                b_r = back[:width, at : at + width]
-                b_i = back[width:, at : at + width]
-                obj_r, obj_i = objs[u]
-                parts[u][0] = parts[u][0] + (p_r * b_r + p_i * b_i)
-                parts[u][1] = parts[u][1] + (p_r * b_i - p_i * b_r)
-                sum_r = sum_r + (obj_r * b_r + obj_i * b_i)
-                sum_i = sum_i + (obj_r * b_i - obj_i * b_r)
-            probe_s[k, 0] = sum_r
-            probe_s[k, 1] = sum_i
-        for u in range(UNROLL):
-            _, row, block, shift = window_of(entries[u], blocks)
-            keep = lane >= shift
-            for a in range(2):
-                turned = pltpu.roll(parts[u][a], shift & (LANES - 1), 1)
-                spot = (a, block, pl.ds(row, width), slice(None))
-                acc_s[spot] = acc_s[spot] + jnp.where(keep, turned, 0.0)
-                spot = (a, block + 1, pl.ds(row, width), slice(None))
-                acc_s[spot] = acc_s[spot] + jnp.where(keep, 0.0, turned)
+                _, row, block, shift = places[u]
+                keep = lane >= shift
+                for a in range(2):
+                    turned = pltpu.roll(parts[u][a], shift & (LANES - 1), 1)
+                    spot = (a, block, pl.ds(row + s, STRIP), slice(None))
+                    acc_s[spot] = acc_s[spot] + jnp.where(keep, turned, 0.0)
+                    spot = (a, block + 1, pl.ds(row + s, STRIP), slice(None))
+                    acc_s[spot] = acc_s[spot] + jnp.where(keep, 0.0, turned)
         return carry
 
     lax.fori_loop(0, steps, step, jnp.int32(0))
@@ -316,6 +331,8 @@
     staging = [
         pltpu.VMEM((2, UNROLL, 2 * width, modes * width), jnp.float32),
         pltpu.VMEM((2, UNROLL, 2, width, width), jnp.bfloat16),
+        pltpu.VMEM((UNROLL, modes * width, 2 * width), jnp.bfloat16),
+        pltpu.VMEM((UNROLL, 2 * width, modes * width), jnp.bfloat16),
     ]
     forward = pl.pallas_call(
         lambda *refs: forward_kernel(slots, *refs),
@@ -348,6 +365,7 @@
             pltpu.VMEM((modes, 2, width, LANES), jnp.float32),
             pltpu.VMEM((slots + 1, 1, LANES), jnp.float32),
             *staging,
+            pltpu.VMEM((UNROLL, 2 * width, modes * width), jnp.float32),
             pltpu.SemaphoreType.DMA((2 * blocks,)),
             pltpu.SemaphoreType.DMA((2, 2)),
         ],
@@ -410,8 +428,14 @@
         out_specs=(VMEM, SMEM),
         name="receive_sums",
     )(own_slots, sums)
-    probe_part = jnp.sum(lax.all_gather(probe_part, "pos", axis=0), axis=0)
-    probe_total = lax.all_gather(probe_part, plane, axis=0, tiled=True)
+    hop = 1
+    while hop < depth:
+        partner = [(z, z ^ hop) for z in range(depth)]
+        probe_part = probe_part + lax.ppermute(probe_part, "pos", partner)
+        hop *= 2
+    probe_total = lax.all_to_all(
+        jnp.broadcast_to(probe_part, (groups, rows, LANES)), plane, split_axis=0, concat_axis=0, tiled=True
+    )
     return (shares, probe_total.reshape(modes, 2, width, width), misfit)
 
 

time: 180 us -> 156 us (0.87)
  blocking collectives: 110 us -> 53.6 us
  Pallas kernels: 27.4 us -> 41 us
  starting transfers between devices: 8.64 us -> 19.4 us
  waiting for transfers between devices: 13 us -> 21 us
    all_gather x2 -> x0, blocking collectives: 52.8 us -> none  [the longest x1 26.9 us: local(): probe_total = lax.all_gather(probe_part, plane, axis=0, tiled=True)]
    all_to_all x1, blocking collectives: 57.5 us -> 36.3 us  [local(): sums = lax.all_to_all(sums, plane, split_axis=0, concat_axis=0, tiled=True)]
    all_to_all x0 -> x1, blocking collectives: none -> 17.4 us  [local(): lax.all_to_all(jnp.broadcast_to(probe_part, (groups, rows, LANES)), plane...]
    ppermute x0 -> x3, starting transfers between devices: none -> 10.7 us  [local(): probe_part = probe_part + lax.ppermute(probe_part, 'pos', partner)]
    pallas_call x1, Pallas kernels: 10.5 us -> 19.2 us  [local(): tile_grad, sums = backward(listed, far, patches, probe, arrived, *tables)]
    reduce_scatter x1, waiting for transfers between devices: 0.01 us -> 6.73 us  [local(): shares = lax.psum_scatter(tile_grad, 'pos', scatter_dimension=1, tiled=True)]
    ppermute x0 -> x3, waiting for transfers between devices: none -> 6.21 us  [local(): probe_part = probe_part + lax.ppermute(probe_part, 'pos', partner)]
    all_to_all x1, waiting for transfers between devices: 13 us -> 8.04 us  [local(): lax.all_to_all(outgoing.reshape(groups, CAP, width, width), plane, split_...]
  transfers between devices with their start and end apart: 2 -> 5, of which waited for: 1 -> 5; matrix products, arithmetic and copies ran while one was open for 0% -> 1% of each run, Pallas kernels for 8% -> 12%
where the time goes in v4:
time: 156 us
  blocking collectives  53.6 us (34%)
  Pallas kernels  41 us (26%)
  waiting for transfers between devices  21 us (13%)
  starting transfers between devices  19.4 us (12%)
  between operations  14.2 us (9%)
  local copies, waits for them, and re-layouts  3.56 us (2%)
  other arithmetic  2.79 us (2%)
    all_to_all x1, blocking collectives, local(): sums = lax.all_to_all(sums, plane, split_axis=0, concat_axis=0, tiled=True)  36.3 us
    pallas_call x1, Pallas kernels, local(): tile_grad, sums = backward(listed, far, patches, probe, arrived, *tables)  19.2 us
    all_to_all x1, blocking collectives, local(): lax.all_to_all(jnp.broadcast_to(probe_part, (groups, rows, LANES)), plane...  17.4 us
    pallas_call x1, Pallas kernels, local(): far, patches = forward(listed, obj, probe, *tables)  13.9 us
    ppermute x3, starting transfers between devices, local(): probe_part = probe_part + lax.ppermute(probe_part, 'pos', partner)  10.7 us
    all_to_all x1, starting transfers between devices, local(): lax.all_to_all(outgoing.reshape(groups, CAP, width, width), plane, split_...  8.6 us
    all_to_all x1, waiting for transfers between devices, local(): lax.all_to_all(outgoing.reshape(groups, CAP, width, width), plane, split_...  8.04 us
    reduce_scatter x1, waiting for transfers between devices, local(): shares = lax.psum_scatter(tile_grad, 'pos', scatter_dimension=1, tiled=True)  6.73 us
  transfers between devices with their start and end apart: 5, of which 5 were waited for; matrix products, arithmetic and copies ran while one was open for 1% of the time, Pallas kernels for 12%

profile of v4, /device:TPU:1, one launch (start us, length us, event | category | flops | bytes accessed | tf_op | source)
XLA Modules:
  0.0 155.6 jit_solution(12199073242347393592)
XLA Ops:
  7.2 0.0 copy-start.2
  7.2 0.0 copy-start.3
  7.2 0.0 copy-start.1
  7.2 0.6 pad_add_fusion.refs_0_
  7.8 1.5 slice_or_fusion
  9.3 2.6 %send_slots.1 = (bf16[64,128,128]{2,1,0:T(8,128)(2,1)}, s32[16]{0:T(128)}) custom-call(s32[2]{0:T(128)} %pad_add_fusion.refs_0_, s32[4096]{0:T(1024)} %bitcast.9, bf16[16,128,128]{2,1,0:T(8,128)(2,1)} %refs_2_.3), custom_call_target="tpu_custom_call" | custom-call | tf_op jit(solution)/shard_map/send_slots/pallas_call | solution.py:393
  11.9 8.6 %all-to-all-start = ((bf16[32,2,128,128]{3,2,1,0:T(8,128)(2,1)}), bf16[32,2,128,128]{3,2,1,0:T(8,128)(2,1)S(1)}, u32[]{:S(2)}, u32[]{:S(2)}) async-start(bf16[32,2,128,128]{3,2,1,0:T(8,128)(2,1)} %bitcast.7), calls=%async_computation | async-start | bytes 4194304 | tf_op jit(solution)/shard_map/all_to_all | solution.py:403
  20.5 0.0 reduce-scatter.2.cloned.1.call-start
  20.6 3.5 %list_windows.1.refs_0_ = s32[76]{0:T(128)} custom-call(s32[2]{0:T(128)} %pad_add_fusion.refs_0_, s32[4096]{0:T(1024)} %bitcast.10), custom_call_target="tpu_custom_call" | custom-call | flops 1000000 | bytes 10000000 | tf_op jit(solution)/shard_map/list_windows/pallas_call | solution.py:406
  24.1 0.0 copy-done.2
  24.1 0.0 copy-done.3
  24.1 0.0 copy-done.1
  24.1 0.0 copy-start.4
  24.1 0.6 copy-done.4
  24.8 0.0 copy-start.5
  24.8 13.9 %forward_windows.1 = (f32[68,256,512]{2,1,0:T(8,128)}, bf16[68,2,128,128]{3,2,1,0:T(8,128)(2,1)S(1)}) custom-call(s32[76]{0:T(128)S(1)} %copy-done.4, f32[2,768,768]{2,1,0:T(8,128)} %refs_1_.1, f32[4,2,128,128]{3,2,1,0:T(8,128)S(1)} %copy-done.1, bf16[256,256]{1,0:T(8,128)(2,1)S(1)} %copy-done.3, bf16[256,256]{1,0:T(8,128)(2,1)S(1)} %copy-done.2), custom_call_target="tpu_custom_call" | custom-call | flops 4294967296 | bytes 40000000 | tf_op jit(solution)/shard_map/forward_windows/pallas_call | solution.py:417
  38.7 0.0 copy-start
  38.7 2.0 %copy-done = bf16[68,2,128,128]{3,2,1,0:T(8,128)(2,1)} copy-done((bf16[68,2,128,128]{3,2,1,0:T(8,128)(2,1)}, bf16[68,2,128,128]{3,2,1,0:T(8,128)(2,1)S(1)}, u32[]{:S(2)}) %copy-start) | copy-done | bytes 4456472
  40.8 8.0 %all-to-all-done = bf16[32,2,128,128]{3,2,1,0:T(8,128)(2,1)S(1)} async-done(((bf16[32,2,128,128]{3,2,1,0:T(8,128)(2,1)}), bf16[32,2,128,128]{3,2,1,0:T(8,128)(2,1)S(1)}, u32[]{:S(2)}, u32[]{:S(2)}) %all-to-all-start) | async-done | bytes 2097184 | tf_op jit(solution)/shard_map/all_to_all | solution.py:403
  48.8 0.0 copy-done.5
  48.8 19.2 %backward_windows.1 = (f32[2,768,768]{2,1,0:T(8,128)}, f32[32,40,128]{2,1,0:T(8,128)S(1)}) custom-call(s32[76]{0:T(128)S(1)} %copy-done.5, f32[68,256,512]{2,1,0:T(8,128)} %get-tuple-element.11.refs_1_, bf16[68,2,128,128]{3,2,1,0:T(8,128)(2,1)} %copy-done, f32[4,2,128,128]{3,2,1,0:T(8,128)S(1)} %copy-done.1, bf16[64,128,128]{2,1,0:T(8,128)(2,1)S(1)} %bitcast.6, ...), custom_call_target="tpu_custom_call" | custom-call | flops 4294967296 | bytes 40000000 | tf_op jit(solution)/shard_map/backward_windows/pallas_call | solution.py:418
  68.0 0.0 reduce-scatter.2.cloned.1.call-update
  68.0 36.3 %all_to_all.15.refs_1_ = f32[32,40,128]{2,1,0:T(8,128)} all-to-all(f32[32,40,128]{2,1,0:T(8,128)S(1)} %get-tuple-element.16), channel_id=1, replica_groups=mesh['tx'=4,'ty'=8,'pos'=8] {'tx','ty'}, dimensions={0} | all-to-all | bytes 1310720 | tf_op jit(solution)/shard_map/all_to_all | solution.py:420
  104.3 1.8 %receive_sums.1 = (f32[32,128]{1,0:T(8,128)}, f32[16]{0:T(128)}) custom-call(s32[16]{0:T(128)} %get-tuple-element.15.refs_0_, f32[32,40,128]{2,1,0:T(8,128)} %all_to_all.15.refs_1_), custom_call_target="tpu_custom_call" | custom-call | tf_op jit(solution)/shard_map/receive_sums/pallas_call | solution.py:421
  106.1 1.8 %collective-permute-start = (f32[32,128]{1,0:T(8,128)}, f32[32,128]{1,0:T(8,128)S(1)}, u32[]{:S(2)}, u32[]{:S(2)}) collective-permute-start(f32[32,128]{1,0:T(8,128)} %get-tuple-element.17), channel_id=1, source_target_pairs={{0,1},{1,0},{2,3},{3,2},{4,5},{5,4},{6,7},{7,6},{8,9},{9,8},{10,11... | collective-permute-start | bytes 49160 | tf_op jit(solution)/shard_map/ppermute | solution.py:434
  107.9 2.4 %collective-permute-done = f32[32,128]{1,0:T(8,128)S(1)} collective-permute-done((f32[32,128]{1,0:T(8,128)}, f32[32,128]{1,0:T(8,128)S(1)}, u32[]{:S(2)}, u32[]{:S(2)}) %collective-permute-start) | collective-permute-done | bytes 16416 | tf_op jit(solution)/shard_map/ppermute | solution.py:434
  110.3 0.7 add.15
  111.1 3.0 %collective-permute-start.1 = (f32[32,128]{1,0:T(8,128)S(1)}, f32[32,128]{1,0:T(8,128)S(1)}, u32[]{:S(2)}, u32[]{:S(2)}) collective-permute-start(f32[32,128]{1,0:T(8,128)S(1)} %add.15), channel_id=1, source_target_pairs={{0,2},{1,3},{2,0},{3,1},{4,6},{5,7},{6,4},{7,5},{8,10},{9,11},{10,... | collective-permute-start | bytes 49160 | tf_op jit(solution)/shard_map/ppermute | solution.py:434
  114.0 2.1 %collective-permute-done.1 = f32[32,128]{1,0:T(8,128)S(1)} collective-permute-done((f32[32,128]{1,0:T(8,128)S(1)}, f32[32,128]{1,0:T(8,128)S(1)}, u32[]{:S(2)}, u32[]{:S(2)}) %collective-permute-start.1) | collective-permute-done | bytes 16416 | tf_op jit(solution)/shard_map/ppermute | solution.py:434
  116.1 6.0 %collective-permute-start.2 = (f32[32,128]{1,0:T(8,128)S(1)}, f32[32,128]{1,0:T(8,128)S(1)}, u32[]{:S(2)}, u32[]{:S(2)}) collective-permute-start(f32[32,128]{1,0:T(8,128)S(1)} %add.16), channel_id=1, source_target_pairs={{0,4},{1,5},{2,6},{3,7},{4,0},{5,1},{6,2},{7,3},{8,12},{9,13},{10,... | collective-permute-start | bytes 49160 | tf_op jit(solution)/shard_map/ppermute | solution.py:434
  122.1 1.7 %collective-permute-done.2 = f32[32,128]{1,0:T(8,128)S(1)} collective-permute-done((f32[32,128]{1,0:T(8,128)S(1)}, f32[32,128]{1,0:T(8,128)S(1)}, u32[]{:S(2)}, u32[]{:S(2)}) %collective-permute-start.2) | collective-permute-done | bytes 16416 | tf_op jit(solution)/shard_map/ppermute | solution.py:434
  123.8 0.1 broadcast_in_dim.3
  123.9 17.4 %all_to_all.16 = f32[32,32,128]{2,1,0:T(8,128)S(1)} all-to-all(f32[32,32,128]{2,1,0:T(8,128)S(1)} %broadcast_in_dim.3), channel_id=1, replica_groups=mesh['tx'=4,'ty'=8,'pos'=8] {'tx','ty'}, dimensions={0} | all-to-all | bytes 1048576 | tf_op jit(solution)/shard_map/all_to_all | solution.py:436
  141.2 6.7 %reduce-scatter.2.cloned.1.call-done = f32[2,96,768]{2,1,0:T(8,128)} async-done(((f32[2,768,768]{2,1,0:T(8,128)}), f32[2,96,768]{2,1,0:T(8,128)}) %reduce-scatter.2.cloned.1.call-update) | async-done | bytes 589840 | tf_op jit(solution)/shard_map/reduce_scatter | solution.py:419
  147.9 0.8 copy.11
  (2 shorter events, 0.0 us)
Async XLA Ops:
  7.2 16.9 %copy-start.2 = (bf16[256,256]{1,0:T(8,128)(2,1)S(1)}, bf16[256,256]{1,0:T(8,128)(2,1)}, u32[]{:S(2)}) copy-start(bf16[256,256]{1,0:T(8,128)(2,1)} %constant.23.clone.refs_4_.refs_6_) | copy-start | bytes 393220
  7.2 16.9 %copy-start.3 = (bf16[256,256]{1,0:T(8,128)(2,1)S(1)}, bf16[256,256]{1,0:T(8,128)(2,1)}, u32[]{:S(2)}) copy-start(bf16[256,256]{1,0:T(8,128)(2,1)} %constant.22.clone.refs_3_.refs_5_) | copy-start | bytes 393220
  7.2 16.9 %copy-start.1 = (f32[4,2,128,128]{3,2,1,0:T(8,128)S(1)}, f32[4,2,128,128]{3,2,1,0:T(8,128)}, u32[]{:S(2)}) copy-start(f32[4,2,128,128]{3,2,1,0:T(8,128)} %refs_3_.2) | copy-start | bytes 1572868
  11.9 36.9 %all-to-all-start = ((bf16[32,2,128,128]{3,2,1,0:T(8,128)(2,1)}), bf16[32,2,128,128]{3,2,1,0:T(8,128)(2,1)S(1)}, u32[]{:S(2)}, u32[]{:S(2)}) async-start(bf16[32,2,128,128]{3,2,1,0:T(8,128)(2,1)} %bitcast.7), calls=%async_computation | async-start | bytes 4194304 | tf_op jit(solution)/shard_map/all_to_all | solution.py:403
  20.5 127.4 %reduce-scatter.2.cloned.1.call-start = ((), (), s32[]{:S(2)}) async-start(), calls=%async_computation.4 | async-start | bytes 5308416 | tf_op jit(solution)/shard_map/reduce_scatter | solution.py:419
  24.1 0.7 copy-start.4
  24.8 24.0 %copy-start.5 = (s32[76]{0:T(128)S(1)}, s32[76]{0:T(128)}, u32[]{:S(2)}) copy-start(s32[76]{0:T(128)} %list_windows.1.refs_0_) | copy-start | bytes 916
  38.7 2.1 %copy-start = (bf16[68,2,128,128]{3,2,1,0:T(8,128)(2,1)}, bf16[68,2,128,128]{3,2,1,0:T(8,128)(2,1)S(1)}, u32[]{:S(2)}) copy-start(bf16[68,2,128,128]{3,2,1,0:T(8,128)(2,1)S(1)} %get-tuple-element.12.refs_2_) | copy-start | bytes 13369348
  106.1 4.2 %collective-permute-start = (f32[32,128]{1,0:T(8,128)}, f32[32,128]{1,0:T(8,128)S(1)}, u32[]{:S(2)}, u32[]{:S(2)}) collective-permute-start(f32[32,128]{1,0:T(8,128)} %get-tuple-element.17), channel_id=1, source_target_pairs={{0,1},{1,0},{2,3},{3,2},{4,5},{5,4},{6,7},{7,6},{8,9},{9,8},{10,11... | collective-permute-start | bytes 49160 | tf_op jit(solution)/shard_map/ppermute | solution.py:434
  111.1 5.1 %collective-permute-start.1 = (f32[32,128]{1,0:T(8,128)S(1)}, f32[32,128]{1,0:T(8,128)S(1)}, u32[]{:S(2)}, u32[]{:S(2)}) collective-permute-start(f32[32,128]{1,0:T(8,128)S(1)} %add.15), channel_id=1, source_target_pairs={{0,2},{1,3},{2,0},{3,1},{4,6},{5,7},{6,4},{7,5},{8,10},{9,11},{10,... | collective-permute-start | bytes 49160 | tf_op jit(solution)/shard_map/ppermute | solution.py:434
  116.1 7.7 %collective-permute-start.2 = (f32[32,128]{1,0:T(8,128)S(1)}, f32[32,128]{1,0:T(8,128)S(1)}, u32[]{:S(2)}, u32[]{:S(2)}) collective-permute-start(f32[32,128]{1,0:T(8,128)S(1)} %add.16), channel_id=1, source_target_pairs={{0,4},{1,5},{2,6},{3,7},{4,0},{5,1},{6,2},{7,3},{8,12},{9,13},{10,... | collective-permute-start | bytes 49160 | tf_op jit(solution)/shard_map/ppermute | solution.py:434
Sparse Core Ops, SparseCore 0:
  68.2 79.7 reduce-scatter.1

commit v5 on v4

--- a/solution.py
+++ b/solution.py
@@ -10,6 +10,7 @@
 CAP = 2
 UNROLL = 4
 STRIP = 16
+PACK = 32
 LANES = 128
 ROW_BITS = 10
 TILE_SHIFT = 2 * ROW_BITS
@@ -26,9 +27,14 @@
     return np.block([[c, -s], [s, c]]), np.block([[c, s], [-s, c]])
 
 
-def send_kernel(groups, depth, per_device, where_ref, packed_ref, measured_ref, out_ref, slot_ref):
-    base = (where_ref[0] * depth + where_ref[1]) * per_device
-    tiles = [lax.shift_right_logical(packed_ref[base + i], TILE_SHIFT) for i in range(per_device)]
+def own_place(cols_along):
+    return lax.axis_index("tx") * cols_along + lax.axis_index("ty"), lax.axis_index("pos")
+
+
+def send_kernel(cols_along, depth, per_device, tile_ref, measured_ref, out_ref, slot_ref):
+    tile, plane = own_place(cols_along)
+    base = (tile * depth + plane) * per_device
+    tiles = [tile_ref[base + i] for i in range(per_device)]
     for i in range(per_device):
         rank = jnp.int32(0)
         for j in range(i):
@@ -38,9 +44,8 @@
         out_ref[slot] = measured_ref[i]
 
 
-def list_kernel(groups, depth, per_device, where_ref, packed_ref, list_ref):
-    tile = where_ref[0]
-    plane = where_ref[1]
+def list_windows(cols_along, groups, depth, per_device, packed_ref, list_ref):
+    tile, plane = own_place(cols_along)
 
     def one_group(group, count):
         base = (group * depth + plane) * per_device
@@ -68,6 +73,10 @@
     return slot, row, block, col - block * LANES
 
 
+def patch_spot(width, part, row):
+    return pl.ds(2 * width + part * PACK + row % PACK, STRIP), pl.ds(row // PACK * LANES, LANES)
+
+
 def right_product(field_s, table_ref, half_s, u):
     width = LANES
     half = jnp.dot(field_s[u], table_ref[...], preferred_element_type=jnp.float32)
@@ -79,17 +88,16 @@
 
 
 def forward_kernel(
-    slots,
-    list_ref,
+    sizes,
+    packed_ref,
     obj_ref,
     probe_ref,
     x_ref,
     y_ref,
     far_ref,
-    patch_ref,
+    list_ref,
     tile_s,
     far_s,
-    patch_s,
     field_s,
     half_s,
     sems,
@@ -98,7 +106,6 @@
     width = LANES
     modes = probe_ref.shape[0]
     blocks = tile_s.shape[1]
-    steps = list_ref[slots + UNROLL]
     copies = [
         pltpu.make_async_copy(
             obj_ref.at[a, :, pl.ds(b * LANES, LANES)], tile_s.at[a, b], sems.at[a * blocks + b]
@@ -108,6 +115,8 @@
     ]
     for copy in copies:
         copy.start()
+    list_windows(*sizes, packed_ref, list_ref)
+    steps = list_ref[sizes[1] * CAP + UNROLL]
     for copy in copies:
         copy.wait()
 
@@ -115,8 +124,7 @@
         turn = n & 1
         there = pl.ds(n * UNROLL, UNROLL)
         return (
-            pltpu.make_async_copy(far_s.at[turn], far_ref.at[there], out_sems.at[0, turn]),
-            pltpu.make_async_copy(patch_s.at[turn], patch_ref.at[there], out_sems.at[1, turn]),
+            pltpu.make_async_copy(far_s.at[turn], far_ref.at[there], out_sems.at[turn]),
         )
 
     lane = lax.broadcasted_iota(jnp.int32, (STRIP, LANES), 1)
@@ -141,8 +149,9 @@
                     left = pltpu.roll(tile_s[a, block, pl.ds(row + s, STRIP), :], back_shift, 1)
                     right = pltpu.roll(tile_s[a, block + 1, pl.ds(row + s, STRIP), :], back_shift, 1)
                     rounded = jnp.where(own, left, right).astype(jnp.bfloat16)
-                    patch_s[turn, u, a, pl.ds(s, STRIP), :] = rounded
-                    parts.append(rounded.astype(jnp.float32))
+                    patch = rounded.astype(jnp.float32)
+                    far_s[(turn, u, *patch_spot(width, a, s))] = patch
+                    parts.append(patch)
                 objs.append(parts)
             for k in range(modes):
                 p_r = probe_ref[k, 0, pl.ds(s, STRIP), :]
@@ -155,7 +164,7 @@
         for u in range(UNROLL):
             right_product(field_s, y_ref, half_s, u)
         for u in range(UNROLL):
-            far_s[turn, u] = jnp.dot(x_ref[...], half_s[u], preferred_element_type=jnp.float32)
+            far_s[turn, u, pl.ds(0, 2 * width), :] = jnp.dot(x_ref[...], half_s[u], preferred_element_type=jnp.float32)
         for copy in leaving(n):
             copy.start()
         return carry
@@ -173,7 +182,6 @@
     slots,
     list_ref,
     far_ref,
-    patch_ref,
     probe_ref,
     meas_ref,
     x_ref,
@@ -184,7 +192,6 @@
     probe_s,
     misfit_s,
     far_s,
-    patch_s,
     field_s,
     half_s,
     back_s,
@@ -200,8 +207,7 @@
         turn = n & 1
         there = pl.ds(n * UNROLL, UNROLL)
         return (
-            pltpu.make_async_copy(far_ref.at[there], far_s.at[turn], in_sems.at[0, turn]),
-            pltpu.make_async_copy(patch_ref.at[there], patch_s.at[turn], in_sems.at[1, turn]),
+            pltpu.make_async_copy(far_ref.at[there], far_s.at[turn], in_sems.at[turn]),
         )
 
     @pl.when(steps > 0)
@@ -247,14 +253,14 @@
                             fields[2 * k + h] * factor
                         ).astype(jnp.bfloat16)
             misfit_s[slot] = jnp.sum(misfit, axis=0, keepdims=True)
-        for u in range(UNROLL):
             right_product(field_s, x_ref, half_s, u)
-        for u in range(UNROLL):
-            back_s[u] = jnp.dot(y_ref[...], half_s[u], preferred_element_type=jnp.float32)
+            if u:
+                back_s[u - 1] = jnp.dot(y_ref[...], half_s[u - 1], preferred_element_type=jnp.float32)
+        back_s[UNROLL - 1] = jnp.dot(y_ref[...], half_s[UNROLL - 1], preferred_element_type=jnp.float32)
         places = [window_of(entries[u], blocks) for u in range(UNROLL)]
         for s in range(0, width, STRIP):
             rows = pl.ds(s, STRIP)
-            objs = [[patch_s[turn, u, a, rows, :].astype(jnp.float32) for a in range(2)] for u in range(UNROLL)]
+            objs = [[far_s[(turn, u, *patch_spot(width, a, s))] for a in range(2)] for u in range(UNROLL)]
             parts = [[None, None] for _ in range(UNROLL)]
             for k in range(modes):
                 p_r = probe_ref[k, 0, rows, :]
@@ -323,30 +329,29 @@
 ANY = pl.BlockSpec(memory_space=pl.ANY)
 
 
-def kernels(tile_shape, modes, width, slots, per_device, groups):
+def kernels(tile_shape, modes, width, slots, per_device, groups, cols_along, depth):
     tile_width = tile_shape[-1]
     blocks = tile_width // LANES
     rows = modes * 2 * width // groups
     flops = slots // 2 * modes * 2 * (2 * width) ** 2 * width * 2
     staging = [
-        pltpu.VMEM((2, UNROLL, 2 * width, modes * width), jnp.float32),
-        pltpu.VMEM((2, UNROLL, 2, width, width), jnp.bfloat16),
+        pltpu.VMEM((2, UNROLL, 2 * width + 2 * PACK, modes * width), jnp.float32),
         pltpu.VMEM((UNROLL, modes * width, 2 * width), jnp.bfloat16),
         pltpu.VMEM((UNROLL, 2 * width, modes * width), jnp.bfloat16),
     ]
     forward = pl.pallas_call(
-        lambda *refs: forward_kernel(slots, *refs),
+        lambda *refs: forward_kernel((cols_along, groups, depth, per_device), *refs),
         out_shape=(
-            jax.ShapeDtypeStruct((slots + UNROLL, 2 * width, modes * width), jnp.float32),
-            jax.ShapeDtypeStruct((slots + UNROLL, 2, width, width), jnp.bfloat16),
+            jax.ShapeDtypeStruct((slots + UNROLL, 2 * width + 2 * PACK, modes * width), jnp.float32),
+            jax.ShapeDtypeStruct((slots + 2 * UNROLL + 4,), jnp.int32),
         ),
         in_specs=[SMEM, ANY, VMEM, VMEM, VMEM],
-        out_specs=(ANY, ANY),
+        out_specs=(ANY, SMEM),
         scratch_shapes=[
             pltpu.VMEM((2, blocks, tile_width, LANES), jnp.float32),
             *staging,
             pltpu.SemaphoreType.DMA((2 * blocks,)),
-            pltpu.SemaphoreType.DMA((2, 2)),
+            pltpu.SemaphoreType.DMA((2,)),
         ],
         compiler_params=pltpu.CompilerParams(vmem_limit_bytes=48 << 20),
         cost_estimate=pl.CostEstimate(flops=flops, bytes_accessed=40_000_000, transcendentals=0),
@@ -358,7 +363,7 @@
             jax.ShapeDtypeStruct(tile_shape, jnp.float32),
             jax.ShapeDtypeStruct((groups, rows + 8, LANES), jnp.float32),
         ),
-        in_specs=[SMEM, ANY, ANY, VMEM, VMEM, VMEM, VMEM],
+        in_specs=[SMEM, ANY, VMEM, VMEM, VMEM, VMEM],
         out_specs=(ANY, VMEM),
         scratch_shapes=[
             pltpu.VMEM((2, blocks, tile_width, LANES), jnp.float32),
@@ -367,7 +372,7 @@
             *staging,
             pltpu.VMEM((UNROLL, 2 * width, modes * width), jnp.float32),
             pltpu.SemaphoreType.DMA((2 * blocks,)),
-            pltpu.SemaphoreType.DMA((2, 2)),
+            pltpu.SemaphoreType.DMA((2,)),
         ],
         compiler_params=pltpu.CompilerParams(vmem_limit_bytes=48 << 20),
         cost_estimate=pl.CostEstimate(flops=flops, bytes_accessed=40_000_000, transcendentals=0),
@@ -385,37 +390,25 @@
     positions = per_device * groups * depth
     slots = groups * CAP
     plane = ("tx", "ty")
-    my_tile = lax.axis_index("tx") * cols_along + lax.axis_index("ty")
-    where = jnp.stack([my_tile, lax.axis_index("pos")]).astype(jnp.int32)
-    packed = (tile_of[:, 0] << TILE_SHIFT) | (inner[:, 0] << ROW_BITS) | inner[:, 1]
-    sizes = (groups, depth, per_device)
-
     outgoing, own_slots = pl.pallas_call(
-        lambda *refs: send_kernel(*sizes, *refs),
+        lambda *refs: send_kernel(cols_along, depth, per_device, *refs),
         out_shape=(
             jax.ShapeDtypeStruct((slots, width, width), measured.dtype),
             jax.ShapeDtypeStruct((per_device,), jnp.int32),
         ),
-        in_specs=[SMEM, SMEM, VMEM],
+        in_specs=[SMEM, VMEM],
         out_specs=(VMEM, SMEM),
         name="send_slots",
-    )(where, packed, measured)
+    )(tile_of.reshape(positions), measured)
     arrived = lax.all_to_all(
         outgoing.reshape(groups, CAP, width, width), plane, split_axis=0, concat_axis=0, tiled=True
     ).reshape(slots, width, width)
-    listed = pl.pallas_call(
-        lambda *refs: list_kernel(*sizes, *refs),
-        out_shape=jax.ShapeDtypeStruct((slots + 2 * UNROLL + 4,), jnp.int32),
-        in_specs=[SMEM, SMEM],
-        out_specs=SMEM,
-        cost_estimate=pl.CostEstimate(flops=1_000_000, bytes_accessed=10_000_000, transcendentals=0),
-        name="list_windows",
-    )(where, packed)
+    packed = (tile_of[:, 0] << TILE_SHIFT) | (inner[:, 0] << ROW_BITS) | inner[:, 1]
     tables = [jnp.asarray(table) for table in dft_blocks(width)]
     rows = modes * 2 * width // groups
-    forward, backward = kernels(obj.shape, modes, width, slots, per_device, groups)
-    far, patches = forward(listed, obj, probe, *tables)
-    tile_grad, sums = backward(listed, far, patches, probe, arrived, *tables)
+    forward, backward = kernels(obj.shape, modes, width, slots, per_device, groups, cols_along, depth)
+    far, listed = forward(packed, obj, probe, *tables)
+    tile_grad, sums = backward(listed, far, probe, arrived, *tables)
     shares = lax.psum_scatter(tile_grad, "pos", scatter_dimension=1, tiled=True)
     sums = lax.all_to_all(sums, plane, split_axis=0, concat_axis=0, tiled=True)
     probe_part, misfit = pl.pallas_call(

time: 156 us -> 150 us (0.962)
  Pallas kernels: 41 us -> 23.4 us
  waiting for transfers between devices: 21 us -> 29.5 us
  blocking collectives: 53.6 us -> 59.9 us
  other arithmetic: 2.79 us -> 0.77 us
    pallas_call x4 -> x3, Pallas kernels: 39.3 us -> 21.6 us  [the longest x1 9.76 us: local(): tile_grad, sums = backward(listed, far, probe, arrived, *tables)]
    all_to_all x1, waiting for transfers between devices: 8.04 us -> 16.6 us  [local(): lax.all_to_all(outgoing.reshape(groups, CAP, width, width), plane, split_...]
    all_to_all x1, blocking collectives: 36.3 us -> 42.6 us  [local(): sums = lax.all_to_all(sums, plane, split_axis=0, concat_axis=0, tiled=True)]
  transfers between devices with their start and end apart: 5 -> 5, of which waited for: 5 -> 5; matrix products, arithmetic and copies ran while one was open for 1% -> 1% of each run, Pallas kernels for 12% -> 7%
where the time goes in v5:
time: 150 us
  blocking collectives  59.9 us (40%)
  waiting for transfers between devices  29.5 us (20%)
  Pallas kernels  23.4 us (16%)
  starting transfers between devices  19.4 us (13%)
  between operations  14.2 us (9%)
  local copies, waits for them, and re-layouts  3.2 us (2%)
    all_to_all x1, blocking collectives, local(): sums = lax.all_to_all(sums, plane, split_axis=0, concat_axis=0, tiled=True)  42.6 us
    all_to_all x1, blocking collectives, local(): lax.all_to_all(jnp.broadcast_to(probe_part, (groups, rows, LANES)), plane...  17.4 us
    all_to_all x1, waiting for transfers between devices, local(): lax.all_to_all(outgoing.reshape(groups, CAP, width, width), plane, split_...  16.6 us
    ppermute x3, starting transfers between devices, local(): probe_part = probe_part + lax.ppermute(probe_part, 'pos', partner)  10.7 us
    pallas_call x1, Pallas kernels, local(): tile_grad, sums = backward(listed, far, probe, arrived, *tables)  9.76 us
    pallas_call x1, Pallas kernels, local(): far, listed = forward(packed, obj, probe, *tables)  9.16 us
    all_to_all x1, starting transfers between devices, local(): lax.all_to_all(outgoing.reshape(groups, CAP, width, width), plane, split_...  8.6 us
    reduce_scatter x1, waiting for transfers between devices, local(): shares = lax.psum_scatter(tile_grad, 'pos', scatter_dimension=1, tiled=True)  6.7 us
  transfers between devices with their start and end apart: 5, of which 5 were waited for; matrix products, arithmetic and copies ran while one was open for 1% of the time, Pallas kernels for 7%

profile of v5, /device:TPU:1, one launch (start us, length us, event | category | flops | bytes accessed | tf_op | source)
XLA Modules:
  0.0 150.4 jit_solution(12927931218527042757)
XLA Ops:
  7.2 0.0 copy-start.1
  7.2 0.0 copy-start.2
  7.2 0.0 copy-start.4
  7.2 0.0 copy-start.5
  7.2 0.0 copy-start
  7.2 2.7 %send_slots.1 = (bf16[64,128,128]{2,1,0:T(8,128)(2,1)}, s32[16]{0:T(128)}) custom-call(s32[4096]{0:T(1024)} %bitcast.9, bf16[16,128,128]{2,1,0:T(8,128)(2,1)} %refs_1_.3), custom_call_target="tpu_custom_call" | custom-call | tf_op jit(solution)/shard_map/send_slots/pallas_call | solution.py:393
  9.9 8.6 %all-to-all-start = ((bf16[32,2,128,128]{3,2,1,0:T(8,128)(2,1)}), bf16[32,2,128,128]{3,2,1,0:T(8,128)(2,1)S(1)}, u32[]{:S(2)}, u32[]{:S(2)}) async-start(bf16[32,2,128,128]{3,2,1,0:T(8,128)(2,1)} %bitcast.7), calls=%async_computation | async-start | bytes 4194304 | tf_op jit(solution)/shard_map/all_to_all | solution.py:403
  18.5 0.0 reduce-scatter.2.cloned.1.call-start
  18.6 0.0 copy-done.5
  18.6 0.0 copy-done.4
  18.6 0.0 copy-done.1
  18.6 0.0 copy-done.2
  18.7 0.0 copy-done
  18.7 0.0 copy-start.3
  18.7 2.3 %copy-done.3 = f32[2,768,768]{2,1,0:T(8,128)S(1)} copy-done((f32[2,768,768]{2,1,0:T(8,128)S(1)}, f32[2,768,768]{2,1,0:T(8,128)}, u32[]{:S(2)}) %copy-start.3) | copy-done | bytes 4718616
  21.0 9.2 %forward_windows.1 = (f32[68,320,512]{2,1,0:T(8,128)}, s32[76]{0:T(128)S(1)}) custom-call(s32[4096]{0:T(1024)S(1)} %or_or_fusion.refs_0_, f32[2,768,768]{2,1,0:T(8,128)S(1)} %copy-done.3, f32[4,2,128,128]{3,2,1,0:T(8,128)S(1)} %copy-done, bf16[256,256]{1,0:T(8,128)(2,1)S(1)} %copy-done.2, bf16[256,256]{1,0:T(8,128)(2,1)S(1)} %copy-done.1), custom_call_target="tpu_custom_call" | custom-call | flops 4294967296 | bytes 40000000 | tf_op jit(solution)/shard_map/forward_windows/pallas_call | solution.py:410
  30.2 16.6 %all-to-all-done = bf16[32,2,128,128]{3,2,1,0:T(8,128)(2,1)S(1)} async-done(((bf16[32,2,128,128]{3,2,1,0:T(8,128)(2,1)}), bf16[32,2,128,128]{3,2,1,0:T(8,128)(2,1)S(1)}, u32[]{:S(2)}, u32[]{:S(2)}) %all-to-all-start) | async-done | bytes 2097184 | tf_op jit(solution)/shard_map/all_to_all | solution.py:403
  46.8 9.8 %backward_windows.1 = (f32[2,768,768]{2,1,0:T(8,128)}, f32[32,40,128]{2,1,0:T(8,128)S(1)}) custom-call(s32[76]{0:T(128)S(1)} %get-tuple-element.11.refs_0_, f32[68,320,512]{2,1,0:T(8,128)} %get-tuple-element.12.refs_1_, f32[4,2,128,128]{3,2,1,0:T(8,128)S(1)} %copy-done, bf16[64,128,128]{2,1,0:T(8,128)(2,1)S(1)} %bitcast.6, bf16[256,256]{1,0:T(8,128)(2,1)S(1)} %copy-done.2, ...), custom_call_target="tpu_custom_call" | custom-call | flops 4294967296 | bytes 40000000 | tf_op jit(solution)/shard_map/backward_windows/pallas_call | solution.py:411
  56.6 0.0 reduce-scatter.2.cloned.1.call-update
  56.6 42.6 %all_to_all.15.refs_1_ = f32[32,40,128]{2,1,0:T(8,128)} all-to-all(f32[32,40,128]{2,1,0:T(8,128)S(1)} %get-tuple-element.16), channel_id=1, replica_groups=mesh['tx'=4,'ty'=8,'pos'=8] {'tx','ty'}, dimensions={0} | all-to-all | bytes 1310720 | tf_op jit(solution)/shard_map/all_to_all | solution.py:413
  99.2 1.8 %receive_sums.1 = (f32[32,128]{1,0:T(8,128)}, f32[16]{0:T(128)}) custom-call(s32[16]{0:T(128)} %get-tuple-element.15.refs_0_, f32[32,40,128]{2,1,0:T(8,128)} %all_to_all.15.refs_1_), custom_call_target="tpu_custom_call" | custom-call | tf_op jit(solution)/shard_map/receive_sums/pallas_call | solution.py:414
  101.0 1.7 %collective-permute-start = (f32[32,128]{1,0:T(8,128)}, f32[32,128]{1,0:T(8,128)S(1)}, u32[]{:S(2)}, u32[]{:S(2)}) collective-permute-start(f32[32,128]{1,0:T(8,128)} %get-tuple-element.17), channel_id=1, source_target_pairs={{0,1},{1,0},{2,3},{3,2},{4,5},{5,4},{6,7},{7,6},{8,9},{9,8},{10,11... | collective-permute-start | bytes 49160 | tf_op jit(solution)/shard_map/ppermute | solution.py:427
  102.7 2.4 %collective-permute-done = f32[32,128]{1,0:T(8,128)S(1)} collective-permute-done((f32[32,128]{1,0:T(8,128)}, f32[32,128]{1,0:T(8,128)S(1)}, u32[]{:S(2)}, u32[]{:S(2)}) %collective-permute-start) | collective-permute-done | bytes 16416 | tf_op jit(solution)/shard_map/ppermute | solution.py:427
  105.1 0.7 add.11
  105.9 3.0 %collective-permute-start.1 = (f32[32,128]{1,0:T(8,128)S(1)}, f32[32,128]{1,0:T(8,128)S(1)}, u32[]{:S(2)}, u32[]{:S(2)}) collective-permute-start(f32[32,128]{1,0:T(8,128)S(1)} %add.11), channel_id=1, source_target_pairs={{0,2},{1,3},{2,0},{3,1},{4,6},{5,7},{6,4},{7,5},{8,10},{9,11},{10,... | collective-permute-start | bytes 49160 | tf_op jit(solution)/shard_map/ppermute | solution.py:427
  108.9 2.1 %collective-permute-done.1 = f32[32,128]{1,0:T(8,128)S(1)} collective-permute-done((f32[32,128]{1,0:T(8,128)S(1)}, f32[32,128]{1,0:T(8,128)S(1)}, u32[]{:S(2)}, u32[]{:S(2)}) %collective-permute-start.1) | collective-permute-done | bytes 16416 | tf_op jit(solution)/shard_map/ppermute | solution.py:427
  111.0 6.0 %collective-permute-start.2 = (f32[32,128]{1,0:T(8,128)S(1)}, f32[32,128]{1,0:T(8,128)S(1)}, u32[]{:S(2)}, u32[]{:S(2)}) collective-permute-start(f32[32,128]{1,0:T(8,128)S(1)} %add.12), channel_id=1, source_target_pairs={{0,4},{1,5},{2,6},{3,7},{4,0},{5,1},{6,2},{7,3},{8,12},{9,13},{10,... | collective-permute-start | bytes 49160 | tf_op jit(solution)/shard_map/ppermute | solution.py:427
  117.0 1.7 %collective-permute-done.2 = f32[32,128]{1,0:T(8,128)S(1)} collective-permute-done((f32[32,128]{1,0:T(8,128)S(1)}, f32[32,128]{1,0:T(8,128)S(1)}, u32[]{:S(2)}, u32[]{:S(2)}) %collective-permute-start.2) | collective-permute-done | bytes 16416 | tf_op jit(solution)/shard_map/ppermute | solution.py:427
  118.6 0.1 broadcast_in_dim.3
  118.7 17.4 %all_to_all.16 = f32[32,32,128]{2,1,0:T(8,128)S(1)} all-to-all(f32[32,32,128]{2,1,0:T(8,128)S(1)} %broadcast_in_dim.3), channel_id=1, replica_groups=mesh['tx'=4,'ty'=8,'pos'=8] {'tx','ty'}, dimensions={0} | all-to-all | bytes 1048576 | tf_op jit(solution)/shard_map/all_to_all | solution.py:429
  136.0 6.7 %reduce-scatter.2.cloned.1.call-done = f32[2,96,768]{2,1,0:T(8,128)} async-done(((f32[2,768,768]{2,1,0:T(8,128)}), f32[2,96,768]{2,1,0:T(8,128)}) %reduce-scatter.2.cloned.1.call-update) | async-done | bytes 589840 | tf_op jit(solution)/shard_map/reduce_scatter | solution.py:412
  142.7 0.8 copy.11
  (4 shorter events, 0.0 us)
Async XLA Ops:
  7.2 11.5 %copy-start.1 = (bf16[256,256]{1,0:T(8,128)(2,1)S(1)}, bf16[256,256]{1,0:T(8,128)(2,1)}, u32[]{:S(2)}) copy-start(bf16[256,256]{1,0:T(8,128)(2,1)} %constant.9.clone.refs_4_.refs_5_) | copy-start | bytes 393220
  7.2 11.5 %copy-start.2 = (bf16[256,256]{1,0:T(8,128)(2,1)S(1)}, bf16[256,256]{1,0:T(8,128)(2,1)}, u32[]{:S(2)}) copy-start(bf16[256,256]{1,0:T(8,128)(2,1)} %constant.8.clone.refs_3_.refs_4_) | copy-start | bytes 393220
  7.2 11.4 %copy-start.4 = (s32[4096,1]{0,1:T(1,128)S(1)}, s32[4096,1]{0,1:T(1,128)}, u32[]{:S(2)}) copy-start(s32[4096,1]{0,1:T(1,128)} %param.10) | copy-start | bytes 49156
  7.2 11.4 %copy-start.5 = (s32[4096,2]{0,1:T(2,128)S(1)}, s32[4096,2]{0,1:T(2,128)}, u32[]{:S(2)}) copy-start(s32[4096,2]{0,1:T(2,128)} %param.11) | copy-start | bytes 98308
  7.2 11.5 %copy-start = (f32[4,2,128,128]{3,2,1,0:T(8,128)S(1)}, f32[4,2,128,128]{3,2,1,0:T(8,128)}, u32[]{:S(2)}) copy-start(f32[4,2,128,128]{3,2,1,0:T(8,128)} %refs_2_.3) | copy-start | bytes 1572868
  9.9 36.9 %all-to-all-start = ((bf16[32,2,128,128]{3,2,1,0:T(8,128)(2,1)}), bf16[32,2,128,128]{3,2,1,0:T(8,128)(2,1)S(1)}, u32[]{:S(2)}, u32[]{:S(2)}) async-start(bf16[32,2,128,128]{3,2,1,0:T(8,128)(2,1)} %bitcast.7), calls=%async_computation | async-start | bytes 4194304 | tf_op jit(solution)/shard_map/all_to_all | solution.py:403
  18.5 124.2 %reduce-scatter.2.cloned.1.call-start = ((), (), s32[]{:S(2)}) async-start(), calls=%async_computation.4 | async-start | bytes 5308416 | tf_op jit(solution)/shard_map/reduce_scatter | solution.py:412
  18.7 2.3 %copy-start.3 = (f32[2,768,768]{2,1,0:T(8,128)S(1)}, f32[2,768,768]{2,1,0:T(8,128)}, u32[]{:S(2)}) copy-start(f32[2,768,768]{2,1,0:T(8,128)} %refs_1_.2) | copy-start | bytes 14155780
  101.0 4.2 %collective-permute-start = (f32[32,128]{1,0:T(8,128)}, f32[32,128]{1,0:T(8,128)S(1)}, u32[]{:S(2)}, u32[]{:S(2)}) collective-permute-start(f32[32,128]{1,0:T(8,128)} %get-tuple-element.17), channel_id=1, source_target_pairs={{0,1},{1,0},{2,3},{3,2},{4,5},{5,4},{6,7},{7,6},{8,9},{9,8},{10,11... | collective-permute-start | bytes 49160 | tf_op jit(solution)/shard_map/ppermute | solution.py:427
  105.9 5.1 %collective-permute-start.1 = (f32[32,128]{1,0:T(8,128)S(1)}, f32[32,128]{1,0:T(8,128)S(1)}, u32[]{:S(2)}, u32[]{:S(2)}) collective-permute-start(f32[32,128]{1,0:T(8,128)S(1)} %add.11), channel_id=1, source_target_pairs={{0,2},{1,3},{2,0},{3,1},{4,6},{5,7},{6,4},{7,5},{8,10},{9,11},{10,... | collective-permute-start | bytes 49160 | tf_op jit(solution)/shard_map/ppermute | solution.py:427
  111.0 7.6 %collective-permute-start.2 = (f32[32,128]{1,0:T(8,128)S(1)}, f32[32,128]{1,0:T(8,128)S(1)}, u32[]{:S(2)}, u32[]{:S(2)}) collective-permute-start(f32[32,128]{1,0:T(8,128)S(1)} %add.12), channel_id=1, source_target_pairs={{0,4},{1,5},{2,6},{3,7},{4,0},{5,1},{6,2},{7,3},{8,12},{9,13},{10,... | collective-permute-start | bytes 49160 | tf_op jit(solution)/shard_map/ppermute | solution.py:427
Sparse Core Ops, SparseCore 0:
  56.7 85.9 reduce-scatter.1

commit v6 on v5

--- a/solution.py
+++ b/solution.py
@@ -49,18 +49,20 @@
 
     def one_group(group, count):
         base = (group * depth + plane) * per_device
-        rank = jnp.int32(0)
+        values = [packed_ref[base + i] for i in range(per_device)]
+        hits = [lax.shift_right_logical(value, TILE_SHIFT) == tile for value in values]
+        first = last = jnp.int32(0)
+        found = jnp.int32(0)
         for i in range(per_device):
-            value = packed_ref[base + i]
-            hit = (lax.shift_right_logical(value, TILE_SHIFT) == tile).astype(jnp.int32)
-            slot = group * CAP + rank
-            list_ref[count] = (slot << TILE_SHIFT) | (value & ((1 << TILE_SHIFT) - 1))
-            count = count + hit
-            rank = rank + hit
-        return count
+            last = jnp.where(hits[i], values[i], last)
+            first = jnp.where(hits[per_device - 1 - i], values[per_device - 1 - i], first)
+            found = found + hits[i].astype(jnp.int32)
+        for rank, value in enumerate((first, last)):
+            list_ref[count + rank] = ((group * CAP + rank) << TILE_SHIFT) | (value & ((1 << TILE_SHIFT) - 1))
+        return count + found
 
     count = lax.fori_loop(0, groups, one_group, jnp.int32(0))
-    for u in range(UNROLL - 1):
+    for u in range(UNROLL):
         list_ref[count + u] = jnp.int32((groups * CAP) << TILE_SHIFT)
     list_ref[groups * CAP + UNROLL] = (count + UNROLL - 1) // UNROLL
 
@@ -204,92 +206,113 @@
     steps = list_ref[slots + UNROLL]
 
     def coming(n):
-        turn = n & 1
+        turn = lax.rem(n, 3)
         there = pl.ds(n * UNROLL, UNROLL)
-        return (
-            pltpu.make_async_copy(far_ref.at[there], far_s.at[turn], in_sems.at[turn]),
-        )
+        return pltpu.make_async_copy(far_ref.at[there], far_s.at[turn], in_sems.at[turn])
 
     @pl.when(steps > 0)
     def _():
-        for copy in coming(0):
-            copy.start()
+        coming(0).start()
 
     acc_s[...] = jnp.zeros_like(acc_s)
     probe_s[...] = jnp.zeros_like(probe_s)
     misfit_s[...] = jnp.zeros_like(misfit_s)
+    early, late = range(UNROLL // 2), range(UNROLL // 2, UNROLL)
+    for u in late:
+        back_s[u] = jnp.zeros(back_s.shape[1:], jnp.float32)
+        far_s[2, u, pl.ds(2 * width, 2 * PACK), :] = jnp.zeros((2 * PACK, modes * width), jnp.float32)
     lane = lax.broadcasted_iota(jnp.int32, (STRIP, LANES), 1)
 
-    def step(n, carry):
-        turn = n & 1
-
-        @pl.when(n + 1 < steps)
-        def _():
-            for copy in coming(n + 1):
-                copy.start()
-
-        for copy in coming(n):
-            copy.wait()
-        entries = [list_ref[n * UNROLL + u] for u in range(UNROLL)]
-        for u in range(UNROLL):
-            slot = lax.shift_right_logical(entries[u], TILE_SHIFT)
-            held = jnp.minimum(slot, slots - 1)
-            misfit = jnp.zeros((STRIP, LANES), jnp.float32)
-            for s in range(0, width, STRIP):
-                fields = [
-                    far_s[turn, u, pl.ds(h * width + s, STRIP), pl.ds(k * width, width)]
-                    for k in range(modes)
-                    for h in range(2)
-                ]
-                intensity = 1.0 + sum(f * f for f in fields)
-                data = meas_ref[held, pl.ds(s, STRIP), :].astype(jnp.float32)
-                inverse = lax.rsqrt(intensity)
-                gap = intensity * inverse - data
-                misfit = misfit + gap * gap
-                factor = jnp.where(slot < slots, 1.0 - data * inverse, 0.0)
-                for k in range(modes):
-                    for h in range(2):
-                        field_s[u, pl.ds(k * width + s, STRIP), pl.ds(h * width, width)] = (
-                            fields[2 * k + h] * factor
-                        ).astype(jnp.bfloat16)
-            misfit_s[slot] = jnp.sum(misfit, axis=0, keepdims=True)
-            right_product(field_s, x_ref, half_s, u)
-            if u:
-                back_s[u - 1] = jnp.dot(y_ref[...], half_s[u - 1], preferred_element_type=jnp.float32)
-        back_s[UNROLL - 1] = jnp.dot(y_ref[...], half_s[UNROLL - 1], preferred_element_type=jnp.float32)
-        places = [window_of(entries[u], blocks) for u in range(UNROLL)]
+    def first_product(turn, u, entry):
+        slot = lax.shift_right_logical(entry, TILE_SHIFT)
+        held = jnp.minimum(slot, slots - 1)
+        misfit = jnp.zeros((STRIP, LANES), jnp.float32)
         for s in range(0, width, STRIP):
+            fields = [
+                far_s[turn, u, pl.ds(h * width + s, STRIP), pl.ds(k * width, width)]
+                for k in range(modes)
+                for h in range(2)
+            ]
+            intensity = 1.0 + sum(f * f for f in fields)
+            data = meas_ref[held, pl.ds(s, STRIP), :].astype(jnp.float32)
+            inverse = lax.rsqrt(intensity)
+            gap = intensity * inverse - data
+            misfit = misfit + gap * gap
+            factor = jnp.where(slot < slots, 1.0 - data * inverse, 0.0)
+            for k in range(modes):
+                for h in range(2):
+                    field_s[u, pl.ds(k * width + s, STRIP), pl.ds(h * width, width)] = (
+                        fields[2 * k + h] * factor
+                    ).astype(jnp.bfloat16)
+        misfit_s[slot] = jnp.sum(misfit, axis=0, keepdims=True)
+        right_product(field_s, x_ref, half_s, u)
+
+    def second_product(u):
+        back_s[u] = jnp.dot(y_ref[...], half_s[u], preferred_element_type=jnp.float32)
+
+    def add_strips(turn, members, entries, strips):
+        places = [window_of(entry, blocks) for entry in entries]
+        count = len(entries)
+        for s in strips:
             rows = pl.ds(s, STRIP)
-            objs = [[far_s[(turn, u, *patch_spot(width, a, s))] for a in range(2)] for u in range(UNROLL)]
-            parts = [[None, None] for _ in range(UNROLL)]
+            objs = [[far_s[(turn, u, *patch_spot(width, a, s))] for a in range(2)] for u in members]
+            parts = [None] * count
             for k in range(modes):
                 p_r = probe_ref[k, 0, rows, :]
                 p_i = probe_ref[k, 1, rows, :]
                 sum_r = probe_s[k, 0, rows, :]
                 sum_i = probe_s[k, 1, rows, :]
-                for u in range(UNROLL):
+                for n, u in enumerate(members):
                     b_r = back_s[u, rows, pl.ds(k * width, width)]
                     b_i = back_s[u, pl.ds(width + s, STRIP), pl.ds(k * width, width)]
-                    o_r, o_i = objs[u]
+                    o_r, o_i = objs[n]
                     new_r = p_r * b_r + p_i * b_i
                     new_i = p_r * b_i - p_i * b_r
-                    parts[u] = [new_r, new_i] if k == 0 else [parts[u][0] + new_r, parts[u][1] + new_i]
+                    parts[n] = [new_r, new_i] if k == 0 else [parts[n][0] + new_r, parts[n][1] + new_i]
                     sum_r = sum_r + (o_r * b_r + o_i * b_i)
                     sum_i = sum_i + (o_r * b_i - o_i * b_r)
                 probe_s[k, 0, rows, :] = sum_r
                 probe_s[k, 1, rows, :] = sum_i
-            for u in range(UNROLL):
-                _, row, block, shift = places[u]
+            for n in range(count):
+                _, row, block, shift = places[n]
                 keep = lane >= shift
                 for a in range(2):
-                    turned = pltpu.roll(parts[u][a], shift & (LANES - 1), 1)
+                    turned = pltpu.roll(parts[n][a], shift & (LANES - 1), 1)
                     spot = (a, block, pl.ds(row + s, STRIP), slice(None))
                     acc_s[spot] = acc_s[spot] + jnp.where(keep, turned, 0.0)
                     spot = (a, block + 1, pl.ds(row + s, STRIP), slice(None))
                     acc_s[spot] = acc_s[spot] + jnp.where(keep, 0.0, turned)
+
+    half_way = width // 2
+    upper, lower = range(0, half_way, STRIP), range(half_way, width, STRIP)
+
+    def products_beside(turn, members, entries, sums):
+        first_product(turn, members[0], entries[0])
+        add_strips(*sums, upper)
+        for at in range(1, len(members)):
+            first_product(turn, members[at], entries[at])
+            second_product(members[at - 1])
+        add_strips(*sums, lower)
+        second_product(members[-1])
+
+    def entries_of(n, members):
+        return [list_ref[jnp.maximum(n, 0) * UNROLL + u] for u in members]
+
+    def step(n, carry):
+        turn = lax.rem(n, 3)
+
+        @pl.when(n + 1 < steps)
+        def _():
+            coming(n + 1).start()
+
+        coming(n).wait()
+        now = entries_of(n, early)
+        products_beside(turn, early, now, (lax.rem(n + 2, 3), late, entries_of(n - 1, late)))
+        products_beside(turn, late, entries_of(n, late), (turn, early, now))
         return carry
 
     lax.fori_loop(0, steps, step, jnp.int32(0))
+    add_strips(lax.rem(steps + 2, 3), late, entries_of(steps - 1, late), range(0, width, STRIP))
     groups = sums_ref.shape[0]
     rows = sums_ref.shape[1] - 8
     copies = [
@@ -334,8 +357,10 @@
     blocks = tile_width // LANES
     rows = modes * 2 * width // groups
     flops = slots // 2 * modes * 2 * (2 * width) ** 2 * width * 2
+    far_buffers = [
+        pltpu.VMEM((turns, UNROLL, 2 * width + 2 * PACK, modes * width), jnp.float32) for turns in (2, 3)
+    ]
     staging = [
-        pltpu.VMEM((2, UNROLL, 2 * width + 2 * PACK, modes * width), jnp.float32),
         pltpu.VMEM((UNROLL, modes * width, 2 * width), jnp.bfloat16),
         pltpu.VMEM((UNROLL, 2 * width, modes * width), jnp.bfloat16),
     ]
@@ -349,11 +374,12 @@
         out_specs=(ANY, SMEM),
         scratch_shapes=[
             pltpu.VMEM((2, blocks, tile_width, LANES), jnp.float32),
+            far_buffers[0],
             *staging,
             pltpu.SemaphoreType.DMA((2 * blocks,)),
             pltpu.SemaphoreType.DMA((2,)),
         ],
-        compiler_params=pltpu.CompilerParams(vmem_limit_bytes=48 << 20),
+        compiler_params=pltpu.CompilerParams(vmem_limit_bytes=55 << 20),
         cost_estimate=pl.CostEstimate(flops=flops, bytes_accessed=40_000_000, transcendentals=0),
         name="forward_windows",
     )
@@ -369,10 +395,11 @@
             pltpu.VMEM((2, blocks, tile_width, LANES), jnp.float32),
             pltpu.VMEM((modes, 2, width, LANES), jnp.float32),
             pltpu.VMEM((slots + 1, 1, LANES), jnp.float32),
+            far_buffers[1],
             *staging,
             pltpu.VMEM((UNROLL, 2 * width, modes * width), jnp.float32),
             pltpu.SemaphoreType.DMA((2 * blocks,)),
-            pltpu.SemaphoreType.DMA((2,)),
+            pltpu.SemaphoreType.DMA((3,)),
         ],
         compiler_params=pltpu.CompilerParams(vmem_limit_bytes=48 << 20),
         cost_estimate=pl.CostEstimate(flops=flops, bytes_accessed=40_000_000, transcendentals=0),

time: 150 us -> 149 us (level)
  blocking collectives: 59.9 us -> 56.9 us
  local copies, waits for them, and re-layouts: 3.2 us -> 1.51 us
  waiting for transfers between devices: 29.5 us -> 31.1 us
    all_to_all x1, blocking collectives: 42.6 us -> 39.5 us  [local(): sums = lax.all_to_all(sums, plane, split_axis=0, concat_axis=0, tiled=True)]
    unnamed x13, local copies, waits for them, and re-layouts: 3.15 us -> 1.46 us
    all_to_all x1, waiting for transfers between devices: 16.6 us -> 18.2 us  [local(): lax.all_to_all(outgoing.reshape(groups, CAP, width, width), plane, split_...]
  transfers between devices with their start and end apart: 5 -> 5, of which waited for: 5 -> 5; matrix products, arithmetic and copies ran while one was open for 1% -> 1% of each run, Pallas kernels for 7% -> 8%
where the time goes in v6:
time: 149 us; the launch traced here: 148 us
  blocking collectives  56.9 us (38%)
  waiting for transfers between devices  31.1 us (21%)
  Pallas kernels  24 us (16%)
  starting transfers between devices  19.4 us (13%)
  between operations  14.1 us (9%)
  local copies, waits for them, and re-layouts  1.51 us (1%)
    all_to_all x1, blocking collectives, local(): sums = lax.all_to_all(sums, plane, split_axis=0, concat_axis=0, tiled=True)  39.5 us
    all_to_all x1, waiting for transfers between devices, local(): lax.all_to_all(outgoing.reshape(groups, CAP, width, width), plane, split_...  18.2 us
    all_to_all x1, blocking collectives, local(): lax.all_to_all(jnp.broadcast_to(probe_part, (groups, rows, LANES)), plane...  17.4 us
    ppermute x3, starting transfers between devices, local(): probe_part = probe_part + lax.ppermute(probe_part, 'pos', partner)  10.7 us
    pallas_call x1, Pallas kernels, local(): tile_grad, sums = backward(listed, far, probe, arrived, *tables)  10.2 us
    pallas_call x1, Pallas kernels, local(): far, listed = forward(packed, obj, probe, *tables)  9.4 us
    all_to_all x1, starting transfers between devices, local(): lax.all_to_all(outgoing.reshape(groups, CAP, width, width), plane, split_...  8.6 us
    reduce_scatter x1, waiting for transfers between devices, local(): shares = lax.psum_scatter(tile_grad, 'pos', scatter_dimension=1, tiled=True)  6.68 us
  transfers between devices with their start and end apart: 5, of which 5 were waited for; matrix products, arithmetic and copies ran while one was open for 1% of the time, Pallas kernels for 8%

profile of v6, /device:TPU:1, one launch (start us, length us, event | category | flops | bytes accessed | tf_op | source)
XLA Modules:
  0.0 148.3 jit_solution(17123441546294580932)
XLA Ops:
  7.2 0.0 copy-start.4
  7.2 0.0 copy-start.5
  7.2 2.6 %send_slots.1 = (bf16[64,128,128]{2,1,0:T(8,128)(2,1)}, s32[16]{0:T(128)}) custom-call(s32[4096]{0:T(1024)} %bitcast.9, bf16[16,128,128]{2,1,0:T(8,128)(2,1)} %refs_1_.3), custom_call_target="tpu_custom_call" | custom-call | tf_op jit(solution)/shard_map/send_slots/pallas_call | solution.py:420
  9.8 8.6 %all-to-all-start = ((bf16[32,2,128,128]{3,2,1,0:T(8,128)(2,1)}), bf16[32,2,128,128]{3,2,1,0:T(8,128)(2,1)S(1)}, u32[]{:S(2)}, u32[]{:S(2)}) async-start(bf16[32,2,128,128]{3,2,1,0:T(8,128)(2,1)} %bitcast.7), calls=%async_computation | async-start | bytes 4194304 | tf_op jit(solution)/shard_map/all_to_all | solution.py:430
  18.4 0.0 reduce-scatter.2.cloned.1.call-start
  18.5 0.0 copy-done.5
  18.5 0.0 copy-done.4
  18.5 0.6 or_or_fusion.refs_0_
  19.1 0.0 copy-start
  19.1 0.0 copy-start.1
  19.1 0.0 copy-start.2
  19.1 9.4 %forward_windows.1 = (f32[68,320,512]{2,1,0:T(8,128)}, s32[76]{0:T(128)}) custom-call(s32[4096]{0:T(1024)} %or_or_fusion.refs_0_, f32[2,768,768]{2,1,0:T(8,128)} %refs_1_.2, f32[4,2,128,128]{3,2,1,0:T(8,128)} %refs_2_.3, bf16[256,256]{1,0:T(8,128)(2,1)} %constant.8.clone.refs_3_.refs_4_, bf16[256,256]{1,0:T(8,128)(2,1)} %constant.9.clone.refs_4_.refs_5_), custom_call_target="tpu_custom_call" | custom-call | flops 4294967296 | bytes 40000000 | tf_op jit(solution)/shard_map/forward_windows/pallas_call | solution.py:437
  28.6 18.2 %all-to-all-done = bf16[32,2,128,128]{3,2,1,0:T(8,128)(2,1)S(1)} async-done(((bf16[32,2,128,128]{3,2,1,0:T(8,128)(2,1)}), bf16[32,2,128,128]{3,2,1,0:T(8,128)(2,1)S(1)}, u32[]{:S(2)}, u32[]{:S(2)}) %all-to-all-start) | async-done | bytes 2097184 | tf_op jit(solution)/shard_map/all_to_all | solution.py:430
  46.7 0.0 copy-done
  46.7 0.0 copy-done.1
  46.7 0.0 copy-done.2
  46.7 0.0 copy-start.3
  46.7 0.6 copy-done.3
  47.4 10.2 %backward_windows.1 = (f32[2,768,768]{2,1,0:T(8,128)}, f32[32,40,128]{2,1,0:T(8,128)S(1)}) custom-call(s32[76]{0:T(128)S(1)} %copy-done.3, f32[68,320,512]{2,1,0:T(8,128)} %get-tuple-element.12.refs_1_, f32[4,2,128,128]{3,2,1,0:T(8,128)S(1)} %copy-done, bf16[64,128,128]{2,1,0:T(8,128)(2,1)S(1)} %bitcast.6, bf16[256,256]{1,0:T(8,128)(2,1)S(1)} %copy-done.2, ...), custom_call_target="tpu_custom_call" | custom-call | flops 4294967296 | bytes 40000000 | tf_op jit(solution)/shard_map/backward_windows/pallas_call | solution.py:438
  57.6 0.0 reduce-scatter.2.cloned.1.call-update
  57.6 39.5 %all_to_all.15.refs_1_ = f32[32,40,128]{2,1,0:T(8,128)} all-to-all(f32[32,40,128]{2,1,0:T(8,128)S(1)} %get-tuple-element.16), channel_id=1, replica_groups=mesh['tx'=4,'ty'=8,'pos'=8] {'tx','ty'}, dimensions={0} | all-to-all | bytes 1310720 | tf_op jit(solution)/shard_map/all_to_all | solution.py:440
  97.2 1.8 %receive_sums.1 = (f32[32,128]{1,0:T(8,128)}, f32[16]{0:T(128)}) custom-call(s32[16]{0:T(128)} %get-tuple-element.15.refs_0_, f32[32,40,128]{2,1,0:T(8,128)} %all_to_all.15.refs_1_), custom_call_target="tpu_custom_call" | custom-call | tf_op jit(solution)/shard_map/receive_sums/pallas_call | solution.py:441
  98.9 1.6 %collective-permute-start = (f32[32,128]{1,0:T(8,128)}, f32[32,128]{1,0:T(8,128)S(1)}, u32[]{:S(2)}, u32[]{:S(2)}) collective-permute-start(f32[32,128]{1,0:T(8,128)} %get-tuple-element.17), channel_id=1, source_target_pairs={{0,1},{1,0},{2,3},{3,2},{4,5},{5,4},{6,7},{7,6},{8,9},{9,8},{10,11... | collective-permute-start | bytes 49160 | tf_op jit(solution)/shard_map/ppermute | solution.py:454
  100.6 2.4 %collective-permute-done = f32[32,128]{1,0:T(8,128)S(1)} collective-permute-done((f32[32,128]{1,0:T(8,128)}, f32[32,128]{1,0:T(8,128)S(1)}, u32[]{:S(2)}, u32[]{:S(2)}) %collective-permute-start) | collective-permute-done | bytes 16416 | tf_op jit(solution)/shard_map/ppermute | solution.py:454
  103.0 0.7 add.11
  103.7 3.0 %collective-permute-start.1 = (f32[32,128]{1,0:T(8,128)S(1)}, f32[32,128]{1,0:T(8,128)S(1)}, u32[]{:S(2)}, u32[]{:S(2)}) collective-permute-start(f32[32,128]{1,0:T(8,128)S(1)} %add.11), channel_id=1, source_target_pairs={{0,2},{1,3},{2,0},{3,1},{4,6},{5,7},{6,4},{7,5},{8,10},{9,11},{10,... | collective-permute-start | bytes 49160 | tf_op jit(solution)/shard_map/ppermute | solution.py:454
  106.7 2.1 %collective-permute-done.1 = f32[32,128]{1,0:T(8,128)S(1)} collective-permute-done((f32[32,128]{1,0:T(8,128)S(1)}, f32[32,128]{1,0:T(8,128)S(1)}, u32[]{:S(2)}, u32[]{:S(2)}) %collective-permute-start.1) | collective-permute-done | bytes 16416 | tf_op jit(solution)/shard_map/ppermute | solution.py:454
  108.9 6.1 %collective-permute-start.2 = (f32[32,128]{1,0:T(8,128)S(1)}, f32[32,128]{1,0:T(8,128)S(1)}, u32[]{:S(2)}, u32[]{:S(2)}) collective-permute-start(f32[32,128]{1,0:T(8,128)S(1)} %add.12), channel_id=1, source_target_pairs={{0,4},{1,5},{2,6},{3,7},{4,0},{5,1},{6,2},{7,3},{8,12},{9,13},{10,... | collective-permute-start | bytes 49160 | tf_op jit(solution)/shard_map/ppermute | solution.py:454
  114.9 1.7 %collective-permute-done.2 = f32[32,128]{1,0:T(8,128)S(1)} collective-permute-done((f32[32,128]{1,0:T(8,128)S(1)}, f32[32,128]{1,0:T(8,128)S(1)}, u32[]{:S(2)}, u32[]{:S(2)}) %collective-permute-start.2) | collective-permute-done | bytes 16416 | tf_op jit(solution)/shard_map/ppermute | solution.py:454
  116.6 0.1 broadcast_in_dim.3
  116.6 17.4 %all_to_all.16 = f32[32,32,128]{2,1,0:T(8,128)S(1)} all-to-all(f32[32,32,128]{2,1,0:T(8,128)S(1)} %broadcast_in_dim.3), channel_id=1, replica_groups=mesh['tx'=4,'ty'=8,'pos'=8] {'tx','ty'}, dimensions={0} | all-to-all | bytes 1048576 | tf_op jit(solution)/shard_map/all_to_all | solution.py:456
  134.0 6.7 %reduce-scatter.2.cloned.1.call-done = f32[2,96,768]{2,1,0:T(8,128)} async-done(((f32[2,768,768]{2,1,0:T(8,128)}), f32[2,96,768]{2,1,0:T(8,128)}) %reduce-scatter.2.cloned.1.call-update) | async-done | bytes 589840 | tf_op jit(solution)/shard_map/reduce_scatter | solution.py:439
  140.7 0.8 copy.11
  (3 shorter events, 0.0 us)
Async XLA Ops:
  7.2 11.4 %copy-start.4 = (s32[4096,1]{0,1:T(1,128)S(1)}, s32[4096,1]{0,1:T(1,128)}, u32[]{:S(2)}) copy-start(s32[4096,1]{0,1:T(1,128)} %param.10) | copy-start | bytes 49156
  7.2 11.3 %copy-start.5 = (s32[4096,2]{0,1:T(2,128)S(1)}, s32[4096,2]{0,1:T(2,128)}, u32[]{:S(2)}) copy-start(s32[4096,2]{0,1:T(2,128)} %param.11) | copy-start | bytes 98308
  9.8 36.9 %all-to-all-start = ((bf16[32,2,128,128]{3,2,1,0:T(8,128)(2,1)}), bf16[32,2,128,128]{3,2,1,0:T(8,128)(2,1)S(1)}, u32[]{:S(2)}, u32[]{:S(2)}) async-start(bf16[32,2,128,128]{3,2,1,0:T(8,128)(2,1)} %bitcast.7), calls=%async_computation | async-start | bytes 4194304 | tf_op jit(solution)/shard_map/all_to_all | solution.py:430
  18.4 122.3 %reduce-scatter.2.cloned.1.call-start = ((), (), s32[]{:S(2)}) async-start(), calls=%async_computation.4 | async-start | bytes 5308416 | tf_op jit(solution)/shard_map/reduce_scatter | solution.py:439
  19.1 27.6 %copy-start = (f32[4,2,128,128]{3,2,1,0:T(8,128)S(1)}, f32[4,2,128,128]{3,2,1,0:T(8,128)}, u32[]{:S(2)}) copy-start(f32[4,2,128,128]{3,2,1,0:T(8,128)} %refs_2_.3) | copy-start | bytes 1572868
  19.1 27.6 %copy-start.1 = (bf16[256,256]{1,0:T(8,128)(2,1)S(1)}, bf16[256,256]{1,0:T(8,128)(2,1)}, u32[]{:S(2)}) copy-start(bf16[256,256]{1,0:T(8,128)(2,1)} %constant.9.clone.refs_4_.refs_5_) | copy-start | bytes 393220
  19.1 27.6 %copy-start.2 = (bf16[256,256]{1,0:T(8,128)(2,1)S(1)}, bf16[256,256]{1,0:T(8,128)(2,1)}, u32[]{:S(2)}) copy-start(bf16[256,256]{1,0:T(8,128)(2,1)} %constant.8.clone.refs_3_.refs_4_) | copy-start | bytes 393220
  46.7 0.7 copy-start.3
  98.9 4.0 %collective-permute-start = (f32[32,128]{1,0:T(8,128)}, f32[32,128]{1,0:T(8,128)S(1)}, u32[]{:S(2)}, u32[]{:S(2)}) collective-permute-start(f32[32,128]{1,0:T(8,128)} %get-tuple-element.17), channel_id=1, source_target_pairs={{0,1},{1,0},{2,3},{3,2},{4,5},{5,4},{6,7},{7,6},{8,9},{9,8},{10,11... | collective-permute-start | bytes 49160 | tf_op jit(solution)/shard_map/ppermute | solution.py:454
  103.7 5.1 %collective-permute-start.1 = (f32[32,128]{1,0:T(8,128)S(1)}, f32[32,128]{1,0:T(8,128)S(1)}, u32[]{:S(2)}, u32[]{:S(2)}) collective-permute-start(f32[32,128]{1,0:T(8,128)S(1)} %add.11), channel_id=1, source_target_pairs={{0,2},{1,3},{2,0},{3,1},{4,6},{5,7},{6,4},{7,5},{8,10},{9,11},{10,... | collective-permute-start | bytes 49160 | tf_op jit(solution)/shard_map/ppermute | solution.py:454
  108.9 7.7 %collective-permute-start.2 = (f32[32,128]{1,0:T(8,128)S(1)}, f32[32,128]{1,0:T(8,128)S(1)}, u32[]{:S(2)}, u32[]{:S(2)}) collective-permute-start(f32[32,128]{1,0:T(8,128)S(1)} %add.12), channel_id=1, source_target_pairs={{0,4},{1,5},{2,6},{3,7},{4,0},{5,1},{6,2},{7,3},{8,12},{9,13},{10,... | collective-permute-start | bytes 49160 | tf_op jit(solution)/shard_map/ppermute | solution.py:454
Sparse Core Ops, SparseCore 0:
  57.7 82.9 reduce-scatter.1

commit v7 on v6

--- a/solution.py
+++ b/solution.py
@@ -79,12 +79,12 @@
     return pl.ds(2 * width + part * PACK + row % PACK, STRIP), pl.ds(row // PACK * LANES, LANES)
 
 
-def right_product(field_s, table_ref, half_s, u):
+def right_product(field_s, table_ref, half_ref, u):
     width = LANES
     half = jnp.dot(field_s[u], table_ref[...], preferred_element_type=jnp.float32)
     for k in range(field_s.shape[1] // width):
         for h in range(2):
-            half_s[u, pl.ds(h * width, width), pl.ds(k * width, width)] = half[
+            half_ref[pl.ds(h * width, width), pl.ds(k * width, width)] = half[
                 k * width : (k + 1) * width, h * width : (h + 1) * width
             ].astype(jnp.bfloat16)
 
@@ -94,14 +94,12 @@
     packed_ref,
     obj_ref,
     probe_ref,
-    x_ref,
     y_ref,
-    far_ref,
+    kept_ref,
     list_ref,
     tile_s,
-    far_s,
+    kept_s,
     field_s,
-    half_s,
     sems,
     out_sems,
 ):
@@ -124,10 +122,10 @@
 
     def leaving(n):
         turn = n & 1
-        there = pl.ds(n * UNROLL, UNROLL)
-        return (
-            pltpu.make_async_copy(far_s.at[turn], far_ref.at[there], out_sems.at[turn]),
-        )
+        return [
+            pltpu.make_async_copy(kept_s.at[turn, u], kept_ref.at[n * UNROLL + u], out_sems.at[turn, u])
+            for u in range(UNROLL)
+        ]
 
     lane = lax.broadcasted_iota(jnp.int32, (STRIP, LANES), 1)
 
@@ -151,9 +149,8 @@
                     left = pltpu.roll(tile_s[a, block, pl.ds(row + s, STRIP), :], back_shift, 1)
                     right = pltpu.roll(tile_s[a, block + 1, pl.ds(row + s, STRIP), :], back_shift, 1)
                     rounded = jnp.where(own, left, right).astype(jnp.bfloat16)
-                    patch = rounded.astype(jnp.float32)
-                    far_s[(turn, u, *patch_spot(width, a, s))] = patch
-                    parts.append(patch)
+                    kept_s[(turn, u, *patch_spot(width, a, s))] = rounded
+                    parts.append(rounded.astype(jnp.float32))
                 objs.append(parts)
             for k in range(modes):
                 p_r = probe_ref[k, 0, pl.ds(s, STRIP), :]
@@ -164,9 +161,7 @@
                     field_s[u, at, pl.ds(0, width)] = (p_r * o_r - p_i * o_i).astype(jnp.bfloat16)
                     field_s[u, at, pl.ds(width, width)] = (p_r * o_i + p_i * o_r).astype(jnp.bfloat16)
         for u in range(UNROLL):
-            right_product(field_s, y_ref, half_s, u)
-        for u in range(UNROLL):
-            far_s[turn, u, pl.ds(0, 2 * width), :] = jnp.dot(x_ref[...], half_s[u], preferred_element_type=jnp.float32)
+            right_product(field_s, y_ref, kept_s.at[turn, u], u)
         for copy in leaving(n):
             copy.start()
         return carry
@@ -183,7 +178,7 @@
 def backward_kernel(
     slots,
     list_ref,
-    far_ref,
+    kept_ref,
     probe_ref,
     meas_ref,
     x_ref,
@@ -193,9 +188,10 @@
     acc_s,
     probe_s,
     misfit_s,
-    far_s,
+    kept_s,
     field_s,
     half_s,
+    far_s,
     back_s,
     sems,
     in_sems,
@@ -207,12 +203,15 @@
 
     def coming(n):
         turn = lax.rem(n, 3)
-        there = pl.ds(n * UNROLL, UNROLL)
-        return pltpu.make_async_copy(far_ref.at[there], far_s.at[turn], in_sems.at[turn])
+        return [
+            pltpu.make_async_copy(kept_ref.at[n * UNROLL + u], kept_s.at[turn, u], in_sems.at[turn, u])
+            for u in range(UNROLL)
+        ]
 
     @pl.when(steps > 0)
     def _():
-        coming(0).start()
+        for copy in coming(0):
+            copy.start()
 
     acc_s[...] = jnp.zeros_like(acc_s)
     probe_s[...] = jnp.zeros_like(probe_s)
@@ -220,16 +219,19 @@
     early, late = range(UNROLL // 2), range(UNROLL // 2, UNROLL)
     for u in late:
         back_s[u] = jnp.zeros(back_s.shape[1:], jnp.float32)
-        far_s[2, u, pl.ds(2 * width, 2 * PACK), :] = jnp.zeros((2 * PACK, modes * width), jnp.float32)
+        kept_s[2, u, pl.ds(2 * width, 2 * PACK), :] = jnp.zeros((2 * PACK, modes * width), jnp.bfloat16)
     lane = lax.broadcasted_iota(jnp.int32, (STRIP, LANES), 1)
 
-    def first_product(turn, u, entry):
+    def far_field(turn, u):
+        far_s[u] = jnp.dot(x_ref[...], kept_s[turn, u, pl.ds(0, 2 * width), :], preferred_element_type=jnp.float32)
+
+    def first_product(u, entry):
         slot = lax.shift_right_logical(entry, TILE_SHIFT)
         held = jnp.minimum(slot, slots - 1)
         misfit = jnp.zeros((STRIP, LANES), jnp.float32)
         for s in range(0, width, STRIP):
             fields = [
-                far_s[turn, u, pl.ds(h * width + s, STRIP), pl.ds(k * width, width)]
+                far_s[u, pl.ds(h * width + s, STRIP), pl.ds(k * width, width)]
                 for k in range(modes)
                 for h in range(2)
             ]
@@ -245,7 +247,7 @@
                         fields[2 * k + h] * factor
                     ).astype(jnp.bfloat16)
         misfit_s[slot] = jnp.sum(misfit, axis=0, keepdims=True)
-        right_product(field_s, x_ref, half_s, u)
+        right_product(field_s, x_ref, half_s.at[u], u)
 
     def second_product(u):
         back_s[u] = jnp.dot(y_ref[...], half_s[u], preferred_element_type=jnp.float32)
@@ -255,7 +257,9 @@
         count = len(entries)
         for s in strips:
             rows = pl.ds(s, STRIP)
-            objs = [[far_s[(turn, u, *patch_spot(width, a, s))] for a in range(2)] for u in members]
+            objs = [
+                [kept_s[(turn, u, *patch_spot(width, a, s))].astype(jnp.float32) for a in range(2)] for u in members
+            ]
             parts = [None] * count
             for k in range(modes):
                 p_r = probe_ref[k, 0, rows, :]
@@ -286,11 +290,13 @@
     half_way = width // 2
     upper, lower = range(0, half_way, STRIP), range(half_way, width, STRIP)
 
-    def products_beside(turn, members, entries, sums):
-        first_product(turn, members[0], entries[0])
+    def products_beside(turn, members, entries, sums, ahead):
+        first_product(members[0], entries[0])
+        for u in ahead:
+            far_field(turn, u)
         add_strips(*sums, upper)
         for at in range(1, len(members)):
-            first_product(turn, members[at], entries[at])
+            first_product(members[at], entries[at])
             second_product(members[at - 1])
         add_strips(*sums, lower)
         second_product(members[-1])
@@ -303,12 +309,16 @@
 
         @pl.when(n + 1 < steps)
         def _():
-            coming(n + 1).start()
-
-        coming(n).wait()
+            for copy in coming(n + 1):
+                copy.start()
+
+        for copy in coming(n):
+            copy.wait()
         now = entries_of(n, early)
-        products_beside(turn, early, now, (lax.rem(n + 2, 3), late, entries_of(n - 1, late)))
-        products_beside(turn, late, entries_of(n, late), (turn, early, now))
+        for u in early:
+            far_field(turn, u)
+        products_beside(turn, early, now, (lax.rem(n + 2, 3), late, entries_of(n - 1, late)), late)
+        products_beside(turn, late, entries_of(n, late), (turn, early, now), ())
         return carry
 
     lax.fori_loop(0, steps, step, jnp.int32(0))
@@ -335,12 +345,12 @@
         copy.wait()
 
 
-def receive_kernel(scale, pixels, slot_ref, sums_ref, probe_ref, misfit_ref):
+def receive_kernel(pixels, slot_ref, sums_ref, probe_ref, misfit_ref):
     groups, rows = sums_ref.shape[0], probe_ref.shape[0]
     total = jnp.zeros((rows, LANES), jnp.float32)
     for g in range(groups):
         total = total + sums_ref[g, pl.ds(0, rows), :]
-    probe_ref[...] = total * scale
+    probe_ref[...] = total
     for i in range(slot_ref.shape[0]):
         slot = slot_ref[i]
         picked = sums_ref[lax.shift_right_logical(slot, 1), pl.ds(rows + (slot & 1), 1), :]
@@ -357,27 +367,24 @@
     blocks = tile_width // LANES
     rows = modes * 2 * width // groups
     flops = slots // 2 * modes * 2 * (2 * width) ** 2 * width * 2
-    far_buffers = [
-        pltpu.VMEM((turns, UNROLL, 2 * width + 2 * PACK, modes * width), jnp.float32) for turns in (2, 3)
-    ]
-    staging = [
-        pltpu.VMEM((UNROLL, modes * width, 2 * width), jnp.bfloat16),
-        pltpu.VMEM((UNROLL, 2 * width, modes * width), jnp.bfloat16),
-    ]
+    kept_shape = (2 * width + 2 * PACK, modes * width)
+    rows_s = pltpu.VMEM((UNROLL, modes * width, 2 * width), jnp.bfloat16)
+    columns_s = pltpu.VMEM((UNROLL, 2 * width, modes * width), jnp.bfloat16)
+    fields_s = pltpu.VMEM((UNROLL, 2 * width, modes * width), jnp.float32)
     forward = pl.pallas_call(
         lambda *refs: forward_kernel((cols_along, groups, depth, per_device), *refs),
         out_shape=(
-            jax.ShapeDtypeStruct((slots + UNROLL, 2 * width + 2 * PACK, modes * width), jnp.float32),
+            jax.ShapeDtypeStruct((slots + UNROLL, *kept_shape), jnp.bfloat16),
             jax.ShapeDtypeStruct((slots + 2 * UNROLL + 4,), jnp.int32),
         ),
-        in_specs=[SMEM, ANY, VMEM, VMEM, VMEM],
+        in_specs=[SMEM, ANY, VMEM, VMEM],
         out_specs=(ANY, SMEM),
         scratch_shapes=[
             pltpu.VMEM((2, blocks, tile_width, LANES), jnp.float32),
-            far_buffers[0],
-            *staging,
+            pltpu.VMEM((2, UNROLL, *kept_shape), jnp.bfloat16),
+            rows_s,
             pltpu.SemaphoreType.DMA((2 * blocks,)),
-            pltpu.SemaphoreType.DMA((2,)),
+            pltpu.SemaphoreType.DMA((2, UNROLL)),
         ],
         compiler_params=pltpu.CompilerParams(vmem_limit_bytes=55 << 20),
         cost_estimate=pl.CostEstimate(flops=flops, bytes_accessed=40_000_000, transcendentals=0),
@@ -395,11 +402,13 @@
             pltpu.VMEM((2, blocks, tile_width, LANES), jnp.float32),
             pltpu.VMEM((modes, 2, width, LANES), jnp.float32),
             pltpu.VMEM((slots + 1, 1, LANES), jnp.float32),
-            far_buffers[1],
-            *staging,
-            pltpu.VMEM((UNROLL, 2 * width, modes * width), jnp.float32),
+            pltpu.VMEM((3, UNROLL, *kept_shape), jnp.bfloat16),
+            rows_s,
+            columns_s,
+            fields_s,
+            fields_s,
             pltpu.SemaphoreType.DMA((2 * blocks,)),
-            pltpu.SemaphoreType.DMA((3,)),
+            pltpu.SemaphoreType.DMA((3, UNROLL)),
         ],
         compiler_params=pltpu.CompilerParams(vmem_limit_bytes=48 << 20),
         cost_estimate=pl.CostEstimate(flops=flops, bytes_accessed=40_000_000, transcendentals=0),
@@ -434,12 +443,12 @@
     tables = [jnp.asarray(table) for table in dft_blocks(width)]
     rows = modes * 2 * width // groups
     forward, backward = kernels(obj.shape, modes, width, slots, per_device, groups, cols_along, depth)
-    far, listed = forward(packed, obj, probe, *tables)
-    tile_grad, sums = backward(listed, far, probe, arrived, *tables)
+    kept, listed = forward(packed, obj, probe, tables[1])
+    tile_grad, sums = backward(listed, kept, probe, arrived, *tables)
     shares = lax.psum_scatter(tile_grad, "pos", scatter_dimension=1, tiled=True)
     sums = lax.all_to_all(sums, plane, split_axis=0, concat_axis=0, tiled=True)
     probe_part, misfit = pl.pallas_call(
-        lambda *refs: receive_kernel(1.0 / positions, width * width, *refs),
+        lambda *refs: receive_kernel(width * width, *refs),
         out_shape=(
             jax.ShapeDtypeStruct((rows, LANES), jnp.float32),
             jax.ShapeDtypeStruct((per_device,), jnp.float32),
@@ -456,7 +465,7 @@
     probe_total = lax.all_to_all(
         jnp.broadcast_to(probe_part, (groups, rows, LANES)), plane, split_axis=0, concat_axis=0, tiled=True
     )
-    return (shares, probe_total.reshape(modes, 2, width, width), misfit)
+    return (shares, probe_total.reshape(modes, 2, width, width) * (1.0 / positions), misfit)
 
 
 def solution(mesh):

time: 149 us -> 148 us (level)
  transfers between devices with their start and end apart: 5 -> 5, of which waited for: 5 -> 5; matrix products, arithmetic and copies ran while one was open for 1% -> 2% of each run, Pallas kernels for 8% -> 7%
where the time goes in v7:
time: 148 us; the launch traced here: 147 us
  blocking collectives  56.8 us (38%)
  waiting for transfers between devices  31.5 us (21%)
  Pallas kernels  22.6 us (15%)
  starting transfers between devices  19.4 us (13%)
  between operations  14.1 us (10%)
  other arithmetic  2.21 us (1%)
    all_to_all x1, blocking collectives, local(): sums = lax.all_to_all(sums, plane, split_axis=0, concat_axis=0, tiled=True)  39.5 us
    all_to_all x1, waiting for transfers between devices, local(): lax.all_to_all(outgoing.reshape(groups, CAP, width, width), plane, split_...  19.4 us
    all_to_all x1, blocking collectives, local(): lax.all_to_all(jnp.broadcast_to(probe_part, (groups, rows, LANES)), plane...  17.4 us
    ppermute x3, starting transfers between devices, local(): probe_part = probe_part + lax.ppermute(probe_part, 'pos', partner)  10.8 us
    pallas_call x1, Pallas kernels, local(): tile_grad, sums = backward(listed, kept, probe, arrived, *tables)  10.1 us
    all_to_all x1, starting transfers between devices, local(): lax.all_to_all(outgoing.reshape(groups, CAP, width, width), plane, split_...  8.6 us
    pallas_call x1, Pallas kernels, local(): kept, listed = forward(packed, obj, probe, tables[1])  8.14 us
    ppermute x3, waiting for transfers between devices, local(): probe_part = probe_part + lax.ppermute(probe_part, 'pos', partner)  6.21 us
  transfers between devices with their start and end apart: 5, of which 5 were waited for; matrix products, arithmetic and copies ran while one was open for 2% of the time, Pallas kernels for 7%

profile of v7, /device:TPU:1, one launch (start us, length us, event | category | flops | bytes accessed | tf_op | source)
XLA Modules:
  0.0 147.4 jit_solution(15011490754788274425)
XLA Ops:
  7.2 0.0 copy-start.4
  7.2 0.0 copy-start.5
  7.2 2.6 %send_slots.1 = (bf16[64,128,128]{2,1,0:T(8,128)(2,1)}, s32[16]{0:T(128)}) custom-call(s32[4096]{0:T(1024)} %bitcast.9, bf16[16,128,128]{2,1,0:T(8,128)(2,1)} %refs_1_.3), custom_call_target="tpu_custom_call" | custom-call | tf_op jit(solution)/shard_map/send_slots/pallas_call | solution.py:429
  9.8 8.6 %all-to-all-start = ((bf16[32,2,128,128]{3,2,1,0:T(8,128)(2,1)}), bf16[32,2,128,128]{3,2,1,0:T(8,128)(2,1)S(1)}, u32[]{:S(2)}, u32[]{:S(2)}) async-start(bf16[32,2,128,128]{3,2,1,0:T(8,128)(2,1)} %bitcast.7), calls=%async_computation | async-start | bytes 4194304 | tf_op jit(solution)/shard_map/all_to_all | solution.py:439
  18.4 0.0 reduce-scatter.2.cloned.1.call-start
  18.4 0.0 copy-done.5
  18.5 0.0 copy-done.4
  18.5 0.6 or_or_fusion.refs_0_
  19.1 0.0 copy-start
  19.1 0.0 copy-start.1
  19.1 0.0 copy-start.2
  19.1 8.1 %forward_windows.1 = (bf16[68,320,512]{2,1,0:T(8,128)(2,1)}, s32[76]{0:T(128)}) custom-call(s32[4096]{0:T(1024)} %or_or_fusion.refs_0_, f32[2,768,768]{2,1,0:T(8,128)} %refs_1_.2, f32[4,2,128,128]{3,2,1,0:T(8,128)} %refs_2_.3, bf16[256,256]{1,0:T(8,128)(2,1)} %constant.11.clone.refs_3_.refs_5_), custom_call_target="tpu_custom_call" | custom-call | flops 4294967296 | bytes 40000000 | tf_op jit(solution)/shard_map/forward_windows/pallas_call | solution.py:446
  27.2 19.4 %all-to-all-done = bf16[32,2,128,128]{3,2,1,0:T(8,128)(2,1)S(1)} async-done(((bf16[32,2,128,128]{3,2,1,0:T(8,128)(2,1)}), bf16[32,2,128,128]{3,2,1,0:T(8,128)(2,1)S(1)}, u32[]{:S(2)}, u32[]{:S(2)}) %all-to-all-start) | async-done | bytes 2097184 | tf_op jit(solution)/shard_map/all_to_all | solution.py:439
  46.7 0.0 copy-done
  46.7 0.0 copy-done.1
  46.7 0.0 copy-done.2
  46.7 0.0 copy-start.3
  46.7 0.6 copy-done.3
  47.3 10.1 %backward_windows.1 = (f32[2,768,768]{2,1,0:T(8,128)}, f32[32,40,128]{2,1,0:T(8,128)S(1)}) custom-call(s32[76]{0:T(128)S(1)} %copy-done.3, bf16[68,320,512]{2,1,0:T(8,128)(2,1)} %get-tuple-element.12.refs_1_, f32[4,2,128,128]{3,2,1,0:T(8,128)S(1)} %copy-done, bf16[64,128,128]{2,1,0:T(8,128)(2,1)S(1)} %bitcast.6, bf16[256,256]{1,0:T(8,128)(2,1)S(1)} %copy-done.2, ...), custom_call_target="tpu_custom_call" | custom-call | flops 4294967296 | bytes 40000000 | tf_op jit(solution)/shard_map/backward_windows/pallas_call | solution.py:447
  57.5 0.0 reduce-scatter.2.cloned.1.call-update
  57.5 39.5 %all_to_all.15.refs_1_ = f32[32,40,128]{2,1,0:T(8,128)} all-to-all(f32[32,40,128]{2,1,0:T(8,128)S(1)} %get-tuple-element.16), channel_id=1, replica_groups=mesh['tx'=4,'ty'=8,'pos'=8] {'tx','ty'}, dimensions={0} | all-to-all | bytes 1310720 | tf_op jit(solution)/shard_map/all_to_all | solution.py:449
  97.0 1.8 %receive_sums.1 = (f32[32,128]{1,0:T(8,128)}, f32[16]{0:T(128)}) custom-call(s32[16]{0:T(128)} %get-tuple-element.15.refs_0_, f32[32,40,128]{2,1,0:T(8,128)} %all_to_all.15.refs_1_), custom_call_target="tpu_custom_call" | custom-call | tf_op jit(solution)/shard_map/receive_sums/pallas_call | solution.py:450
  98.8 1.7 %collective-permute-start = (f32[32,128]{1,0:T(8,128)}, f32[32,128]{1,0:T(8,128)S(1)}, u32[]{:S(2)}, u32[]{:S(2)}) collective-permute-start(f32[32,128]{1,0:T(8,128)} %get-tuple-element.17), channel_id=1, source_target_pairs={{0,1},{1,0},{2,3},{3,2},{4,5},{5,4},{6,7},{7,6},{8,9},{9,8},{10,11... | collective-permute-start | bytes 49160 | tf_op jit(solution)/shard_map/ppermute | solution.py:463
  100.5 2.4 %collective-permute-done = f32[32,128]{1,0:T(8,128)S(1)} collective-permute-done((f32[32,128]{1,0:T(8,128)}, f32[32,128]{1,0:T(8,128)S(1)}, u32[]{:S(2)}, u32[]{:S(2)}) %collective-permute-start) | collective-permute-done | bytes 16416 | tf_op jit(solution)/shard_map/ppermute | solution.py:463
  102.9 0.7 add.11
  103.6 3.0 %collective-permute-start.1 = (f32[32,128]{1,0:T(8,128)S(1)}, f32[32,128]{1,0:T(8,128)S(1)}, u32[]{:S(2)}, u32[]{:S(2)}) collective-permute-start(f32[32,128]{1,0:T(8,128)S(1)} %add.11), channel_id=1, source_target_pairs={{0,2},{1,3},{2,0},{3,1},{4,6},{5,7},{6,4},{7,5},{8,10},{9,11},{10,... | collective-permute-start | bytes 49160 | tf_op jit(solution)/shard_map/ppermute | solution.py:463
  106.6 2.1 %collective-permute-done.1 = f32[32,128]{1,0:T(8,128)S(1)} collective-permute-done((f32[32,128]{1,0:T(8,128)S(1)}, f32[32,128]{1,0:T(8,128)S(1)}, u32[]{:S(2)}, u32[]{:S(2)}) %collective-permute-start.1) | collective-permute-done | bytes 16416 | tf_op jit(solution)/shard_map/ppermute | solution.py:463
  108.7 6.1 %collective-permute-start.2 = (f32[32,128]{1,0:T(8,128)S(1)}, f32[32,128]{1,0:T(8,128)S(1)}, u32[]{:S(2)}, u32[]{:S(2)}) collective-permute-start(f32[32,128]{1,0:T(8,128)S(1)} %add.12), channel_id=1, source_target_pairs={{0,4},{1,5},{2,6},{3,7},{4,0},{5,1},{6,2},{7,3},{8,12},{9,13},{10,... | collective-permute-start | bytes 49160 | tf_op jit(solution)/shard_map/ppermute | solution.py:463
  114.8 1.7 %collective-permute-done.2 = f32[32,128]{1,0:T(8,128)S(1)} collective-permute-done((f32[32,128]{1,0:T(8,128)S(1)}, f32[32,128]{1,0:T(8,128)S(1)}, u32[]{:S(2)}, u32[]{:S(2)}) %collective-permute-start.2) | collective-permute-done | bytes 16416 | tf_op jit(solution)/shard_map/ppermute | solution.py:463
  116.5 0.1 broadcast_in_dim.3
  116.5 17.4 %all_to_all.16 = f32[32,32,128]{2,1,0:T(8,128)S(1)} all-to-all(f32[32,32,128]{2,1,0:T(8,128)S(1)} %broadcast_in_dim.3), channel_id=1, replica_groups=mesh['tx'=4,'ty'=8,'pos'=8] {'tx','ty'}, dimensions={0} | all-to-all | bytes 1048576 | tf_op jit(solution)/shard_map/all_to_all | solution.py:465
  133.9 0.8 broadcast_multiply_fusion
  134.7 5.9 %reduce-scatter.2.cloned.1.call-done = f32[2,96,768]{2,1,0:T(8,128)} async-done(((f32[2,768,768]{2,1,0:T(8,128)}), f32[2,96,768]{2,1,0:T(8,128)}) %reduce-scatter.2.cloned.1.call-update) | async-done | bytes 589840 | tf_op jit(solution)/shard_map/reduce_scatter | solution.py:448
  (3 shorter events, 0.0 us)
Async XLA Ops:
  7.2 11.3 %copy-start.4 = (s32[4096,1]{0,1:T(1,128)S(1)}, s32[4096,1]{0,1:T(1,128)}, u32[]{:S(2)}) copy-start(s32[4096,1]{0,1:T(1,128)} %param.10) | copy-start | bytes 49156
  7.2 11.2 %copy-start.5 = (s32[4096,2]{0,1:T(2,128)S(1)}, s32[4096,2]{0,1:T(2,128)}, u32[]{:S(2)}) copy-start(s32[4096,2]{0,1:T(2,128)} %param.11) | copy-start | bytes 98308
  9.8 36.9 %all-to-all-start = ((bf16[32,2,128,128]{3,2,1,0:T(8,128)(2,1)}), bf16[32,2,128,128]{3,2,1,0:T(8,128)(2,1)S(1)}, u32[]{:S(2)}, u32[]{:S(2)}) async-start(bf16[32,2,128,128]{3,2,1,0:T(8,128)(2,1)} %bitcast.7), calls=%async_computation | async-start | bytes 4194304 | tf_op jit(solution)/shard_map/all_to_all | solution.py:439
  18.4 122.2 %reduce-scatter.2.cloned.1.call-start = ((), (), s32[]{:S(2)}) async-start(), calls=%async_computation.4 | async-start | bytes 5308416 | tf_op jit(solution)/shard_map/reduce_scatter | solution.py:448
  19.1 27.6 %copy-start = (f32[4,2,128,128]{3,2,1,0:T(8,128)S(1)}, f32[4,2,128,128]{3,2,1,0:T(8,128)}, u32[]{:S(2)}) copy-start(f32[4,2,128,128]{3,2,1,0:T(8,128)} %refs_2_.3) | copy-start | bytes 1572868
  19.1 27.6 %copy-start.1 = (bf16[256,256]{1,0:T(8,128)(2,1)S(1)}, bf16[256,256]{1,0:T(8,128)(2,1)}, u32[]{:S(2)}) copy-start(bf16[256,256]{1,0:T(8,128)(2,1)} %constant.11.clone.refs_3_.refs_5_) | copy-start | bytes 393220
  19.1 27.6 %copy-start.2 = (bf16[256,256]{1,0:T(8,128)(2,1)S(1)}, bf16[256,256]{1,0:T(8,128)(2,1)}, u32[]{:S(2)}) copy-start(bf16[256,256]{1,0:T(8,128)(2,1)} %constant.10.clone.refs_4_) | copy-start | bytes 393220
  46.7 0.7 copy-start.3
  98.8 4.1 %collective-permute-start = (f32[32,128]{1,0:T(8,128)}, f32[32,128]{1,0:T(8,128)S(1)}, u32[]{:S(2)}, u32[]{:S(2)}) collective-permute-start(f32[32,128]{1,0:T(8,128)} %get-tuple-element.17), channel_id=1, source_target_pairs={{0,1},{1,0},{2,3},{3,2},{4,5},{5,4},{6,7},{7,6},{8,9},{9,8},{10,11... | collective-permute-start | bytes 49160 | tf_op jit(solution)/shard_map/ppermute | solution.py:463
  103.6 5.1 %collective-permute-start.1 = (f32[32,128]{1,0:T(8,128)S(1)}, f32[32,128]{1,0:T(8,128)S(1)}, u32[]{:S(2)}, u32[]{:S(2)}) collective-permute-start(f32[32,128]{1,0:T(8,128)S(1)} %add.11), channel_id=1, source_target_pairs={{0,2},{1,3},{2,0},{3,1},{4,6},{5,7},{6,4},{7,5},{8,10},{9,11},{10,... | collective-permute-start | bytes 49160 | tf_op jit(solution)/shard_map/ppermute | solution.py:463
  108.7 7.7 %collective-permute-start.2 = (f32[32,128]{1,0:T(8,128)S(1)}, f32[32,128]{1,0:T(8,128)S(1)}, u32[]{:S(2)}, u32[]{:S(2)}) collective-permute-start(f32[32,128]{1,0:T(8,128)S(1)} %add.12), channel_id=1, source_target_pairs={{0,4},{1,5},{2,6},{3,7},{4,0},{5,1},{6,2},{7,3},{8,12},{9,13},{10,... | collective-permute-start | bytes 49160 | tf_op jit(solution)/shard_map/ppermute | solution.py:463
Sparse Core Ops, SparseCore 0:
  57.6 82.9 reduce-scatter.1

commit v8 on v7

--- a/solution.py
+++ b/solution.py
@@ -31,17 +31,21 @@
     return lax.axis_index("tx") * cols_along + lax.axis_index("ty"), lax.axis_index("pos")
 
 
-def send_kernel(cols_along, depth, per_device, tile_ref, measured_ref, out_ref, slot_ref):
+def send_kernel(cols_along, depth, per_device, tile_ref, measured_ref, out_ref, slot_ref, sems):
     tile, plane = own_place(cols_along)
     base = (tile * depth + plane) * per_device
     tiles = [tile_ref[base + i] for i in range(per_device)]
+    copies = []
     for i in range(per_device):
         rank = jnp.int32(0)
         for j in range(i):
             rank = rank + (tiles[j] == tiles[i]).astype(jnp.int32)
         slot = tiles[i] * CAP + rank
         slot_ref[i] = slot
-        out_ref[slot] = measured_ref[i]
+        copies.append(pltpu.make_async_copy(measured_ref.at[i], out_ref.at[slot], sems.at[i]))
+        copies[-1].start()
+    for copy in copies:
+        copy.wait()
 
 
 def list_windows(cols_along, groups, depth, per_device, packed_ref, list_ref):
@@ -433,7 +437,8 @@
             jax.ShapeDtypeStruct((per_device,), jnp.int32),
         ),
         in_specs=[SMEM, VMEM],
-        out_specs=(VMEM, SMEM),
+        out_specs=(ANY, SMEM),
+        scratch_shapes=[pltpu.SemaphoreType.DMA((per_device,))],
         name="send_slots",
     )(tile_of.reshape(positions), measured)
     arrived = lax.all_to_all(

time: 148 us -> 147 us (level)
  Pallas kernels: 22.6 us -> 19.7 us
  blocking collectives: 56.8 us -> 58.6 us
    all_to_all x1, blocking collectives: 39.5 us -> 41.3 us  [local(): sums = lax.all_to_all(sums, plane, split_axis=0, concat_axis=0, tiled=True)]
    pallas_call x1, Pallas kernels: 10.1 us -> 8.31 us  [local(): tile_grad, sums = backward(listed, kept, probe, arrived, *tables)]
  transfers between devices with their start and end apart: 5 -> 5, of which waited for: 5 -> 5; matrix products, arithmetic and copies ran while one was open for 2% -> 2% of each run, Pallas kernels for 7% -> 6%
where the time goes in v8:
time: 147 us
  blocking collectives  58.6 us (40%)
  waiting for transfers between devices  32.6 us (22%)
  Pallas kernels  19.7 us (13%)
  starting transfers between devices  19.3 us (13%)
  between operations  14.1 us (10%)
  other arithmetic  2.21 us (2%)
    all_to_all x1, blocking collectives, local(): sums = lax.all_to_all(sums, plane, split_axis=0, concat_axis=0, tiled=True)  41.3 us
    all_to_all x1, waiting for transfers between devices, local(): lax.all_to_all(outgoing.reshape(groups, CAP, width, width), plane, split_...  20.5 us
    all_to_all x1, blocking collectives, local(): lax.all_to_all(jnp.broadcast_to(probe_part, (groups, rows, LANES)), plane...  17.3 us
    ppermute x3, starting transfers between devices, local(): probe_part = probe_part + lax.ppermute(probe_part, 'pos', partner)  10.7 us
    all_to_all x1, starting transfers between devices, local(): lax.all_to_all(outgoing.reshape(groups, CAP, width, width), plane, split_...  8.6 us
    pallas_call x1, Pallas kernels, local(): tile_grad, sums = backward(listed, kept, probe, arrived, *tables)  8.31 us
    pallas_call x1, Pallas kernels, local(): kept, listed = forward(packed, obj, probe, tables[1])  7.1 us
    ppermute x3, waiting for transfers between devices, local(): probe_part = probe_part + lax.ppermute(probe_part, 'pos', partner)  6.2 us
  transfers between devices with their start and end apart: 5, of which 5 were waited for; matrix products, arithmetic and copies ran while one was open for 2% of the time, Pallas kernels for 6%

profile of v8, /device:TPU:1, one launch (start us, length us, event | category | flops | bytes accessed | tf_op | source)
XLA Modules:
  0.0 147.4 jit_solution(15412101435108797683)
XLA Ops:
  7.2 0.0 copy-start.4
  7.2 0.0 copy-start.5
  7.2 2.6 %send_slots.1 = (bf16[64,128,128]{2,1,0:T(8,128)(2,1)}, s32[16]{0:T(128)}) custom-call(s32[4096]{0:T(1024)} %bitcast.9, bf16[16,128,128]{2,1,0:T(8,128)(2,1)} %refs_1_.3), custom_call_target="tpu_custom_call" | custom-call | tf_op jit(solution)/shard_map/send_slots/pallas_call | solution.py:433
  9.8 8.6 %all-to-all-start = ((bf16[32,2,128,128]{3,2,1,0:T(8,128)(2,1)}), bf16[32,2,128,128]{3,2,1,0:T(8,128)(2,1)S(1)}, u32[]{:S(2)}, u32[]{:S(2)}) async-start(bf16[32,2,128,128]{3,2,1,0:T(8,128)(2,1)} %bitcast.7), calls=%async_computation | async-start | bytes 4194304 | tf_op jit(solution)/shard_map/all_to_all | solution.py:444
  18.4 0.0 reduce-scatter.2.cloned.1.call-start
  18.4 0.0 copy-done.5
  18.5 0.0 copy-done.4
  18.5 0.6 or_or_fusion.refs_0_
  19.1 0.0 copy-start
  19.1 0.0 copy-start.1
  19.1 0.0 copy-start.2
  19.1 7.1 %forward_windows.1 = (bf16[68,320,512]{2,1,0:T(8,128)(2,1)}, s32[76]{0:T(128)}) custom-call(s32[4096]{0:T(1024)} %or_or_fusion.refs_0_, f32[2,768,768]{2,1,0:T(8,128)} %refs_1_.2, f32[4,2,128,128]{3,2,1,0:T(8,128)} %refs_2_.3, bf16[256,256]{1,0:T(8,128)(2,1)} %constant.11.clone.refs_3_.refs_5_), custom_call_target="tpu_custom_call" | custom-call | flops 4294967296 | bytes 40000000 | tf_op jit(solution)/shard_map/forward_windows/pallas_call | solution.py:451
  26.2 20.5 %all-to-all-done = bf16[32,2,128,128]{3,2,1,0:T(8,128)(2,1)S(1)} async-done(((bf16[32,2,128,128]{3,2,1,0:T(8,128)(2,1)}), bf16[32,2,128,128]{3,2,1,0:T(8,128)(2,1)S(1)}, u32[]{:S(2)}, u32[]{:S(2)}) %all-to-all-start) | async-done | bytes 2097184 | tf_op jit(solution)/shard_map/all_to_all | solution.py:444
  46.7 0.0 copy-done
  46.7 0.0 copy-done.1
  46.7 0.0 copy-done.2
  46.7 0.0 copy-start.3
  46.7 0.6 copy-done.3
  47.3 8.3 %backward_windows.1 = (f32[2,768,768]{2,1,0:T(8,128)}, f32[32,40,128]{2,1,0:T(8,128)S(1)}) custom-call(s32[76]{0:T(128)S(1)} %copy-done.3, bf16[68,320,512]{2,1,0:T(8,128)(2,1)} %get-tuple-element.12.refs_1_, f32[4,2,128,128]{3,2,1,0:T(8,128)S(1)} %copy-done, bf16[64,128,128]{2,1,0:T(8,128)(2,1)S(1)} %bitcast.6, bf16[256,256]{1,0:T(8,128)(2,1)S(1)} %copy-done.2, ...), custom_call_target="tpu_custom_call" | custom-call | flops 4294967296 | bytes 40000000 | tf_op jit(solution)/shard_map/backward_windows/pallas_call | solution.py:452
  55.7 0.0 reduce-scatter.2.cloned.1.call-update
  55.7 41.3 %all_to_all.15.refs_1_ = f32[32,40,128]{2,1,0:T(8,128)} all-to-all(f32[32,40,128]{2,1,0:T(8,128)S(1)} %get-tuple-element.16), channel_id=1, replica_groups=mesh['tx'=4,'ty'=8,'pos'=8] {'tx','ty'}, dimensions={0} | all-to-all | bytes 1310720 | tf_op jit(solution)/shard_map/all_to_all | solution.py:454
  97.0 1.8 %receive_sums.1 = (f32[32,128]{1,0:T(8,128)}, f32[16]{0:T(128)}) custom-call(s32[16]{0:T(128)} %get-tuple-element.15.refs_0_, f32[32,40,128]{2,1,0:T(8,128)} %all_to_all.15.refs_1_), custom_call_target="tpu_custom_call" | custom-call | tf_op jit(solution)/shard_map/receive_sums/pallas_call | solution.py:455
  98.8 1.7 %collective-permute-start = (f32[32,128]{1,0:T(8,128)}, f32[32,128]{1,0:T(8,128)S(1)}, u32[]{:S(2)}, u32[]{:S(2)}) collective-permute-start(f32[32,128]{1,0:T(8,128)} %get-tuple-element.17), channel_id=1, source_target_pairs={{0,1},{1,0},{2,3},{3,2},{4,5},{5,4},{6,7},{7,6},{8,9},{9,8},{10,11... | collective-permute-start | bytes 49160 | tf_op jit(solution)/shard_map/ppermute | solution.py:468
  100.5 2.4 %collective-permute-done = f32[32,128]{1,0:T(8,128)S(1)} collective-permute-done((f32[32,128]{1,0:T(8,128)}, f32[32,128]{1,0:T(8,128)S(1)}, u32[]{:S(2)}, u32[]{:S(2)}) %collective-permute-start) | collective-permute-done | bytes 16416 | tf_op jit(solution)/shard_map/ppermute | solution.py:468
  102.9 0.7 add.11
  103.6 3.0 %collective-permute-start.1 = (f32[32,128]{1,0:T(8,128)S(1)}, f32[32,128]{1,0:T(8,128)S(1)}, u32[]{:S(2)}, u32[]{:S(2)}) collective-permute-start(f32[32,128]{1,0:T(8,128)S(1)} %add.11), channel_id=1, source_target_pairs={{0,2},{1,3},{2,0},{3,1},{4,6},{5,7},{6,4},{7,5},{8,10},{9,11},{10,... | collective-permute-start | bytes 49160 | tf_op jit(solution)/shard_map/ppermute | solution.py:468
  106.6 2.1 %collective-permute-done.1 = f32[32,128]{1,0:T(8,128)S(1)} collective-permute-done((f32[32,128]{1,0:T(8,128)S(1)}, f32[32,128]{1,0:T(8,128)S(1)}, u32[]{:S(2)}, u32[]{:S(2)}) %collective-permute-start.1) | collective-permute-done | bytes 16416 | tf_op jit(solution)/shard_map/ppermute | solution.py:468
  108.8 6.0 %collective-permute-start.2 = (f32[32,128]{1,0:T(8,128)S(1)}, f32[32,128]{1,0:T(8,128)S(1)}, u32[]{:S(2)}, u32[]{:S(2)}) collective-permute-start(f32[32,128]{1,0:T(8,128)S(1)} %add.12), channel_id=1, source_target_pairs={{0,4},{1,5},{2,6},{3,7},{4,0},{5,1},{6,2},{7,3},{8,12},{9,13},{10,... | collective-permute-start | bytes 49160 | tf_op jit(solution)/shard_map/ppermute | solution.py:468
  114.7 1.7 %collective-permute-done.2 = f32[32,128]{1,0:T(8,128)S(1)} collective-permute-done((f32[32,128]{1,0:T(8,128)S(1)}, f32[32,128]{1,0:T(8,128)S(1)}, u32[]{:S(2)}, u32[]{:S(2)}) %collective-permute-start.2) | collective-permute-done | bytes 16416 | tf_op jit(solution)/shard_map/ppermute | solution.py:468
  116.4 0.1 broadcast_in_dim.3
  116.4 17.3 %all_to_all.16 = f32[32,32,128]{2,1,0:T(8,128)S(1)} all-to-all(f32[32,32,128]{2,1,0:T(8,128)S(1)} %broadcast_in_dim.3), channel_id=1, replica_groups=mesh['tx'=4,'ty'=8,'pos'=8] {'tx','ty'}, dimensions={0} | all-to-all | bytes 1048576 | tf_op jit(solution)/shard_map/all_to_all | solution.py:470
  133.8 0.8 broadcast_multiply_fusion
  134.6 5.9 %reduce-scatter.2.cloned.1.call-done = f32[2,96,768]{2,1,0:T(8,128)} async-done(((f32[2,768,768]{2,1,0:T(8,128)}), f32[2,96,768]{2,1,0:T(8,128)}) %reduce-scatter.2.cloned.1.call-update) | async-done | bytes 589840 | tf_op jit(solution)/shard_map/reduce_scatter | solution.py:453
  (3 shorter events, 0.0 us)
Async XLA Ops:
  7.2 11.3 %copy-start.4 = (s32[4096,1]{0,1:T(1,128)S(1)}, s32[4096,1]{0,1:T(1,128)}, u32[]{:S(2)}) copy-start(s32[4096,1]{0,1:T(1,128)} %param.10) | copy-start | bytes 49156
  7.2 11.2 %copy-start.5 = (s32[4096,2]{0,1:T(2,128)S(1)}, s32[4096,2]{0,1:T(2,128)}, u32[]{:S(2)}) copy-start(s32[4096,2]{0,1:T(2,128)} %param.11) | copy-start | bytes 98308
  9.8 36.9 %all-to-all-start = ((bf16[32,2,128,128]{3,2,1,0:T(8,128)(2,1)}), bf16[32,2,128,128]{3,2,1,0:T(8,128)(2,1)S(1)}, u32[]{:S(2)}, u32[]{:S(2)}) async-start(bf16[32,2,128,128]{3,2,1,0:T(8,128)(2,1)} %bitcast.7), calls=%async_computation | async-start | bytes 4194304 | tf_op jit(solution)/shard_map/all_to_all | solution.py:444
  18.4 122.1 %reduce-scatter.2.cloned.1.call-start = ((), (), s32[]{:S(2)}) async-start(), calls=%async_computation.4 | async-start | bytes 5308416 | tf_op jit(solution)/shard_map/reduce_scatter | solution.py:453
  19.1 27.6 %copy-start = (f32[4,2,128,128]{3,2,1,0:T(8,128)S(1)}, f32[4,2,128,128]{3,2,1,0:T(8,128)}, u32[]{:S(2)}) copy-start(f32[4,2,128,128]{3,2,1,0:T(8,128)} %refs_2_.3) | copy-start | bytes 1572868
  19.1 27.6 %copy-start.1 = (bf16[256,256]{1,0:T(8,128)(2,1)S(1)}, bf16[256,256]{1,0:T(8,128)(2,1)}, u32[]{:S(2)}) copy-start(bf16[256,256]{1,0:T(8,128)(2,1)} %constant.11.clone.refs_3_.refs_5_) | copy-start | bytes 393220
  19.1 27.6 %copy-start.2 = (bf16[256,256]{1,0:T(8,128)(2,1)S(1)}, bf16[256,256]{1,0:T(8,128)(2,1)}, u32[]{:S(2)}) copy-start(bf16[256,256]{1,0:T(8,128)(2,1)} %constant.10.clone.refs_4_) | copy-start | bytes 393220
  46.7 0.7 copy-start.3
  98.8 4.1 %collective-permute-start = (f32[32,128]{1,0:T(8,128)}, f32[32,128]{1,0:T(8,128)S(1)}, u32[]{:S(2)}, u32[]{:S(2)}) collective-permute-start(f32[32,128]{1,0:T(8,128)} %get-tuple-element.17), channel_id=1, source_target_pairs={{0,1},{1,0},{2,3},{3,2},{4,5},{5,4},{6,7},{7,6},{8,9},{9,8},{10,11... | collective-permute-start | bytes 49160 | tf_op jit(solution)/shard_map/ppermute | solution.py:468
  103.6 5.1 %collective-permute-start.1 = (f32[32,128]{1,0:T(8,128)S(1)}, f32[32,128]{1,0:T(8,128)S(1)}, u32[]{:S(2)}, u32[]{:S(2)}) collective-permute-start(f32[32,128]{1,0:T(8,128)S(1)} %add.11), channel_id=1, source_target_pairs={{0,2},{1,3},{2,0},{3,1},{4,6},{5,7},{6,4},{7,5},{8,10},{9,11},{10,... | collective-permute-start | bytes 49160 | tf_op jit(solution)/shard_map/ppermute | solution.py:468
  108.8 7.6 %collective-permute-start.2 = (f32[32,128]{1,0:T(8,128)S(1)}, f32[32,128]{1,0:T(8,128)S(1)}, u32[]{:S(2)}, u32[]{:S(2)}) collective-permute-start(f32[32,128]{1,0:T(8,128)S(1)} %add.12), channel_id=1, source_target_pairs={{0,4},{1,5},{2,6},{3,7},{4,0},{5,1},{6,2},{7,3},{8,12},{9,13},{10,... | collective-permute-start | bytes 49160 | tf_op jit(solution)/shard_map/ppermute | solution.py:468
Sparse Core Ops, SparseCore 0:
  55.8 84.6 reduce-scatter.1

commit v9 on v5

--- a/solution.py
+++ b/solution.py
@@ -49,18 +49,20 @@
 
     def one_group(group, count):
         base = (group * depth + plane) * per_device
-        rank = jnp.int32(0)
+        values = [packed_ref[base + i] for i in range(per_device)]
+        hits = [lax.shift_right_logical(value, TILE_SHIFT) == tile for value in values]
+        first = last = jnp.int32(0)
+        found = jnp.int32(0)
         for i in range(per_device):
-            value = packed_ref[base + i]
-            hit = (lax.shift_right_logical(value, TILE_SHIFT) == tile).astype(jnp.int32)
-            slot = group * CAP + rank
-            list_ref[count] = (slot << TILE_SHIFT) | (value & ((1 << TILE_SHIFT) - 1))
-            count = count + hit
-            rank = rank + hit
-        return count
+            last = jnp.where(hits[i], values[i], last)
+            first = jnp.where(hits[per_device - 1 - i], values[per_device - 1 - i], first)
+            found = found + hits[i].astype(jnp.int32)
+        for rank, value in enumerate((first, last)):
+            list_ref[count + rank] = ((group * CAP + rank) << TILE_SHIFT) | (value & ((1 << TILE_SHIFT) - 1))
+        return count + found
 
     count = lax.fori_loop(0, groups, one_group, jnp.int32(0))
-    for u in range(UNROLL - 1):
+    for u in range(UNROLL):
         list_ref[count + u] = jnp.int32((groups * CAP) << TILE_SHIFT)
     list_ref[groups * CAP + UNROLL] = (count + UNROLL - 1) // UNROLL
 
@@ -312,12 +314,12 @@
         copy.wait()
 
 
-def receive_kernel(scale, pixels, slot_ref, sums_ref, probe_ref, misfit_ref):
+def receive_kernel(pixels, slot_ref, sums_ref, probe_ref, misfit_ref):
     groups, rows = sums_ref.shape[0], probe_ref.shape[0]
     total = jnp.zeros((rows, LANES), jnp.float32)
     for g in range(groups):
         total = total + sums_ref[g, pl.ds(0, rows), :]
-    probe_ref[...] = total * scale
+    probe_ref[...] = total
     for i in range(slot_ref.shape[0]):
         slot = slot_ref[i]
         picked = sums_ref[lax.shift_right_logical(slot, 1), pl.ds(rows + (slot & 1), 1), :]
@@ -334,8 +336,10 @@
     blocks = tile_width // LANES
     rows = modes * 2 * width // groups
     flops = slots // 2 * modes * 2 * (2 * width) ** 2 * width * 2
+    far_buffers = [
+        pltpu.VMEM((turns, UNROLL, 2 * width + 2 * PACK, modes * width), jnp.float32) for turns in (2, 3)
+    ]
     staging = [
-        pltpu.VMEM((2, UNROLL, 2 * width + 2 * PACK, modes * width), jnp.float32),
         pltpu.VMEM((UNROLL, modes * width, 2 * width), jnp.bfloat16),
         pltpu.VMEM((UNROLL, 2 * width, modes * width), jnp.bfloat16),
     ]
@@ -349,11 +353,12 @@
         out_specs=(ANY, SMEM),
         scratch_shapes=[
             pltpu.VMEM((2, blocks, tile_width, LANES), jnp.float32),
+            far_buffers[0],
             *staging,
             pltpu.SemaphoreType.DMA((2 * blocks,)),
             pltpu.SemaphoreType.DMA((2,)),
         ],
-        compiler_params=pltpu.CompilerParams(vmem_limit_bytes=48 << 20),
+        compiler_params=pltpu.CompilerParams(vmem_limit_bytes=55 << 20),
         cost_estimate=pl.CostEstimate(flops=flops, bytes_accessed=40_000_000, transcendentals=0),
         name="forward_windows",
     )
@@ -369,10 +374,11 @@
             pltpu.VMEM((2, blocks, tile_width, LANES), jnp.float32),
             pltpu.VMEM((modes, 2, width, LANES), jnp.float32),
             pltpu.VMEM((slots + 1, 1, LANES), jnp.float32),
+            far_buffers[1],
             *staging,
             pltpu.VMEM((UNROLL, 2 * width, modes * width), jnp.float32),
             pltpu.SemaphoreType.DMA((2 * blocks,)),
-            pltpu.SemaphoreType.DMA((2,)),
+            pltpu.SemaphoreType.DMA((3,)),
         ],
         compiler_params=pltpu.CompilerParams(vmem_limit_bytes=48 << 20),
         cost_estimate=pl.CostEstimate(flops=flops, bytes_accessed=40_000_000, transcendentals=0),
@@ -412,7 +418,7 @@
     shares = lax.psum_scatter(tile_grad, "pos", scatter_dimension=1, tiled=True)
     sums = lax.all_to_all(sums, plane, split_axis=0, concat_axis=0, tiled=True)
     probe_part, misfit = pl.pallas_call(
-        lambda *refs: receive_kernel(1.0 / positions, width * width, *refs),
+        lambda *refs: receive_kernel(width * width, *refs),
         out_shape=(
             jax.ShapeDtypeStruct((rows, LANES), jnp.float32),
             jax.ShapeDtypeStruct((per_device,), jnp.float32),
@@ -429,7 +435,7 @@
     probe_total = lax.all_to_all(
         jnp.broadcast_to(probe_part, (groups, rows, LANES)), plane, split_axis=0, concat_axis=0, tiled=True
     )
-    return (shares, probe_total.reshape(modes, 2, width, width), misfit)
+    return (shares, probe_total.reshape(modes, 2, width, width) * (1.0 / positions), misfit)
 
 
 def solution(mesh):

time: 150 us -> 149 us (level); the launches traced: 150 us -> 147 us
  blocking collectives: 59.9 us -> 56.9 us
  local copies, waits for them, and re-layouts: 3.2 us -> 0.72 us
    all_to_all x1, blocking collectives: 42.6 us -> 39.6 us  [local(): sums = lax.all_to_all(sums, plane, split_axis=0, concat_axis=0, tiled=True)]
    unnamed x13 -> x12, local copies, waits for them, and re-layouts: 3.15 us -> 0.67 us
    all_to_all x1, waiting for transfers between devices: 16.6 us -> 18.1 us  [local(): lax.all_to_all(outgoing.reshape(groups, CAP, width, width), plane, split_...]
  transfers between devices with their start and end apart: 5 -> 5, of which waited for: 5 -> 5; matrix products, arithmetic and copies ran while one was open for 1% -> 2% of each run, Pallas kernels for 7% -> 8%
where the time goes in v9:
time: 149 us; the launch traced here: 147 us
  blocking collectives  56.9 us (38%)
  waiting for transfers between devices  30.2 us (20%)
  Pallas kernels  23.6 us (16%)
  starting transfers between devices  19.4 us (13%)
  between operations  14.1 us (9%)
  other arithmetic  2.2 us (1%)
    all_to_all x1, blocking collectives, local(): sums = lax.all_to_all(sums, plane, split_axis=0, concat_axis=0, tiled=True)  39.6 us
    all_to_all x1, waiting for transfers between devices, local(): lax.all_to_all(outgoing.reshape(groups, CAP, width, width), plane, split_...  18.1 us
    all_to_all x1, blocking collectives, local(): lax.all_to_all(jnp.broadcast_to(probe_part, (groups, rows, LANES)), plane...  17.3 us
    ppermute x3, starting transfers between devices, local(): probe_part = probe_part + lax.ppermute(probe_part, 'pos', partner)  10.8 us
    pallas_call x1, Pallas kernels, local(): tile_grad, sums = backward(listed, far, probe, arrived, *tables)  9.75 us
    pallas_call x1, Pallas kernels, local(): far, listed = forward(packed, obj, probe, *tables)  9.42 us
    all_to_all x1, starting transfers between devices, local(): lax.all_to_all(outgoing.reshape(groups, CAP, width, width), plane, split_...  8.6 us
    ppermute x3, waiting for transfers between devices, local(): probe_part = probe_part + lax.ppermute(probe_part, 'pos', partner)  6.21 us
  transfers between devices with their start and end apart: 5, of which 5 were waited for; matrix products, arithmetic and copies ran while one was open for 2% of the time, Pallas kernels for 8%

profile of v9, /device:TPU:1, one launch (start us, length us, event | category | flops | bytes accessed | tf_op | source)
XLA Modules:
  0.0 147.2 jit_solution(11804674516776094498)
XLA Ops:
  7.2 0.0 copy-start.4
  7.2 0.0 copy-start.5
  7.2 2.6 %send_slots.1 = (bf16[64,128,128]{2,1,0:T(8,128)(2,1)}, s32[16]{0:T(128)}) custom-call(s32[4096]{0:T(1024)} %bitcast.9, bf16[16,128,128]{2,1,0:T(8,128)(2,1)} %refs_1_.3), custom_call_target="tpu_custom_call" | custom-call | tf_op jit(solution)/shard_map/send_slots/pallas_call | solution.py:399
  9.8 8.6 %all-to-all-start = ((bf16[32,2,128,128]{3,2,1,0:T(8,128)(2,1)}), bf16[32,2,128,128]{3,2,1,0:T(8,128)(2,1)S(1)}, u32[]{:S(2)}, u32[]{:S(2)}) async-start(bf16[32,2,128,128]{3,2,1,0:T(8,128)(2,1)} %bitcast.7), calls=%async_computation | async-start | bytes 4194304 | tf_op jit(solution)/shard_map/all_to_all | solution.py:409
  18.4 0.0 reduce-scatter.2.cloned.1.call-start
  18.5 0.0 copy-done.5
  18.5 0.0 copy-done.4
  18.5 0.6 or_or_fusion.refs_0_
  19.1 0.0 copy-start
  19.1 0.0 copy-start.1
  19.1 0.0 copy-start.2
  19.1 9.4 %forward_windows.1 = (f32[68,320,512]{2,1,0:T(8,128)}, s32[76]{0:T(128)}) custom-call(s32[4096]{0:T(1024)} %or_or_fusion.refs_0_, f32[2,768,768]{2,1,0:T(8,128)} %refs_1_.2, f32[4,2,128,128]{3,2,1,0:T(8,128)} %refs_2_.3, bf16[256,256]{1,0:T(8,128)(2,1)} %constant.10.clone.refs_3_.refs_4_, bf16[256,256]{1,0:T(8,128)(2,1)} %constant.11.clone.refs_4_.refs_5_), custom_call_target="tpu_custom_call" | custom-call | flops 4294967296 | bytes 40000000 | tf_op jit(solution)/shard_map/forward_windows/pallas_call | solution.py:416
  28.6 18.1 %all-to-all-done = bf16[32,2,128,128]{3,2,1,0:T(8,128)(2,1)S(1)} async-done(((bf16[32,2,128,128]{3,2,1,0:T(8,128)(2,1)}), bf16[32,2,128,128]{3,2,1,0:T(8,128)(2,1)S(1)}, u32[]{:S(2)}, u32[]{:S(2)}) %all-to-all-start) | async-done | bytes 2097184 | tf_op jit(solution)/shard_map/all_to_all | solution.py:409
  46.7 0.0 copy-done
  46.7 0.0 copy-done.1
  46.7 0.0 copy-done.2
  46.7 0.0 copy-start.3
  46.7 0.6 copy-done.3
  47.4 9.8 %backward_windows.1 = (f32[2,768,768]{2,1,0:T(8,128)}, f32[32,40,128]{2,1,0:T(8,128)S(1)}) custom-call(s32[76]{0:T(128)S(1)} %copy-done.3, f32[68,320,512]{2,1,0:T(8,128)} %get-tuple-element.12.refs_1_, f32[4,2,128,128]{3,2,1,0:T(8,128)S(1)} %copy-done, bf16[64,128,128]{2,1,0:T(8,128)(2,1)S(1)} %bitcast.6, bf16[256,256]{1,0:T(8,128)(2,1)S(1)} %copy-done.2, ...), custom_call_target="tpu_custom_call" | custom-call | flops 4294967296 | bytes 40000000 | tf_op jit(solution)/shard_map/backward_windows/pallas_call | solution.py:417
  57.2 0.0 reduce-scatter.2.cloned.1.call-update
  57.2 39.6 %all_to_all.15.refs_1_ = f32[32,40,128]{2,1,0:T(8,128)} all-to-all(f32[32,40,128]{2,1,0:T(8,128)S(1)} %get-tuple-element.16), channel_id=1, replica_groups=mesh['tx'=4,'ty'=8,'pos'=8] {'tx','ty'}, dimensions={0} | all-to-all | bytes 1310720 | tf_op jit(solution)/shard_map/all_to_all | solution.py:419
  96.8 1.8 %receive_sums.1 = (f32[32,128]{1,0:T(8,128)}, f32[16]{0:T(128)}) custom-call(s32[16]{0:T(128)} %get-tuple-element.15.refs_0_, f32[32,40,128]{2,1,0:T(8,128)} %all_to_all.15.refs_1_), custom_call_target="tpu_custom_call" | custom-call | tf_op jit(solution)/shard_map/receive_sums/pallas_call | solution.py:420
  98.5 1.7 %collective-permute-start = (f32[32,128]{1,0:T(8,128)}, f32[32,128]{1,0:T(8,128)S(1)}, u32[]{:S(2)}, u32[]{:S(2)}) collective-permute-start(f32[32,128]{1,0:T(8,128)} %get-tuple-element.17), channel_id=1, source_target_pairs={{0,1},{1,0},{2,3},{3,2},{4,5},{5,4},{6,7},{7,6},{8,9},{9,8},{10,11... | collective-permute-start | bytes 49160 | tf_op jit(solution)/shard_map/ppermute | solution.py:433
  100.3 2.4 %collective-permute-done = f32[32,128]{1,0:T(8,128)S(1)} collective-permute-done((f32[32,128]{1,0:T(8,128)}, f32[32,128]{1,0:T(8,128)S(1)}, u32[]{:S(2)}, u32[]{:S(2)}) %collective-permute-start) | collective-permute-done | bytes 16416 | tf_op jit(solution)/shard_map/ppermute | solution.py:433
  102.7 0.7 add.11
  103.4 3.0 %collective-permute-start.1 = (f32[32,128]{1,0:T(8,128)S(1)}, f32[32,128]{1,0:T(8,128)S(1)}, u32[]{:S(2)}, u32[]{:S(2)}) collective-permute-start(f32[32,128]{1,0:T(8,128)S(1)} %add.11), channel_id=1, source_target_pairs={{0,2},{1,3},{2,0},{3,1},{4,6},{5,7},{6,4},{7,5},{8,10},{9,11},{10,... | collective-permute-start | bytes 49160 | tf_op jit(solution)/shard_map/ppermute | solution.py:433
  106.4 2.1 %collective-permute-done.1 = f32[32,128]{1,0:T(8,128)S(1)} collective-permute-done((f32[32,128]{1,0:T(8,128)S(1)}, f32[32,128]{1,0:T(8,128)S(1)}, u32[]{:S(2)}, u32[]{:S(2)}) %collective-permute-start.1) | collective-permute-done | bytes 16416 | tf_op jit(solution)/shard_map/ppermute | solution.py:433
  108.5 6.1 %collective-permute-start.2 = (f32[32,128]{1,0:T(8,128)S(1)}, f32[32,128]{1,0:T(8,128)S(1)}, u32[]{:S(2)}, u32[]{:S(2)}) collective-permute-start(f32[32,128]{1,0:T(8,128)S(1)} %add.12), channel_id=1, source_target_pairs={{0,4},{1,5},{2,6},{3,7},{4,0},{5,1},{6,2},{7,3},{8,12},{9,13},{10,... | collective-permute-start | bytes 49160 | tf_op jit(solution)/shard_map/ppermute | solution.py:433
  114.6 1.7 %collective-permute-done.2 = f32[32,128]{1,0:T(8,128)S(1)} collective-permute-done((f32[32,128]{1,0:T(8,128)S(1)}, f32[32,128]{1,0:T(8,128)S(1)}, u32[]{:S(2)}, u32[]{:S(2)}) %collective-permute-start.2) | collective-permute-done | bytes 16416 | tf_op jit(solution)/shard_map/ppermute | solution.py:433
  116.3 0.1 broadcast_in_dim.3
  116.3 17.3 %all_to_all.16 = f32[32,32,128]{2,1,0:T(8,128)S(1)} all-to-all(f32[32,32,128]{2,1,0:T(8,128)S(1)} %broadcast_in_dim.3), channel_id=1, replica_groups=mesh['tx'=4,'ty'=8,'pos'=8] {'tx','ty'}, dimensions={0} | all-to-all | bytes 1048576 | tf_op jit(solution)/shard_map/all_to_all | solution.py:435
  133.7 0.8 broadcast_multiply_fusion
  134.5 5.9 %reduce-scatter.2.cloned.1.call-done = f32[2,96,768]{2,1,0:T(8,128)} async-done(((f32[2,768,768]{2,1,0:T(8,128)}), f32[2,96,768]{2,1,0:T(8,128)}) %reduce-scatter.2.cloned.1.call-update) | async-done | bytes 589840 | tf_op jit(solution)/shard_map/reduce_scatter | solution.py:418
  (3 shorter events, 0.0 us)
Async XLA Ops:
  7.2 11.4 %copy-start.4 = (s32[4096,1]{0,1:T(1,128)S(1)}, s32[4096,1]{0,1:T(1,128)}, u32[]{:S(2)}) copy-start(s32[4096,1]{0,1:T(1,128)} %param.10) | copy-start | bytes 49156
  7.2 11.3 %copy-start.5 = (s32[4096,2]{0,1:T(2,128)S(1)}, s32[4096,2]{0,1:T(2,128)}, u32[]{:S(2)}) copy-start(s32[4096,2]{0,1:T(2,128)} %param.11) | copy-start | bytes 98308
  9.8 36.9 %all-to-all-start = ((bf16[32,2,128,128]{3,2,1,0:T(8,128)(2,1)}), bf16[32,2,128,128]{3,2,1,0:T(8,128)(2,1)S(1)}, u32[]{:S(2)}, u32[]{:S(2)}) async-start(bf16[32,2,128,128]{3,2,1,0:T(8,128)(2,1)} %bitcast.7), calls=%async_computation | async-start | bytes 4194304 | tf_op jit(solution)/shard_map/all_to_all | solution.py:409
  18.4 121.9 %reduce-scatter.2.cloned.1.call-start = ((), (), s32[]{:S(2)}) async-start(), calls=%async_computation.4 | async-start | bytes 5308416 | tf_op jit(solution)/shard_map/reduce_scatter | solution.py:418
  19.1 27.6 %copy-start = (f32[4,2,128,128]{3,2,1,0:T(8,128)S(1)}, f32[4,2,128,128]{3,2,1,0:T(8,128)}, u32[]{:S(2)}) copy-start(f32[4,2,128,128]{3,2,1,0:T(8,128)} %refs_2_.3) | copy-start | bytes 1572868
  19.1 27.6 %copy-start.1 = (bf16[256,256]{1,0:T(8,128)(2,1)S(1)}, bf16[256,256]{1,0:T(8,128)(2,1)}, u32[]{:S(2)}) copy-start(bf16[256,256]{1,0:T(8,128)(2,1)} %constant.11.clone.refs_4_.refs_5_) | copy-start | bytes 393220
  19.1 27.6 %copy-start.2 = (bf16[256,256]{1,0:T(8,128)(2,1)S(1)}, bf16[256,256]{1,0:T(8,128)(2,1)}, u32[]{:S(2)}) copy-start(bf16[256,256]{1,0:T(8,128)(2,1)} %constant.10.clone.refs_3_.refs_4_) | copy-start | bytes 393220
  46.7 0.7 copy-start.3
  98.5 4.1 %collective-permute-start = (f32[32,128]{1,0:T(8,128)}, f32[32,128]{1,0:T(8,128)S(1)}, u32[]{:S(2)}, u32[]{:S(2)}) collective-permute-start(f32[32,128]{1,0:T(8,128)} %get-tuple-element.17), channel_id=1, source_target_pairs={{0,1},{1,0},{2,3},{3,2},{4,5},{5,4},{6,7},{7,6},{8,9},{9,8},{10,11... | collective-permute-start | bytes 49160 | tf_op jit(solution)/shard_map/ppermute | solution.py:433
  103.4 5.1 %collective-permute-start.1 = (f32[32,128]{1,0:T(8,128)S(1)}, f32[32,128]{1,0:T(8,128)S(1)}, u32[]{:S(2)}, u32[]{:S(2)}) collective-permute-start(f32[32,128]{1,0:T(8,128)S(1)} %add.11), channel_id=1, source_target_pairs={{0,2},{1,3},{2,0},{3,1},{4,6},{5,7},{6,4},{7,5},{8,10},{9,11},{10,... | collective-permute-start | bytes 49160 | tf_op jit(solution)/shard_map/ppermute | solution.py:433
  108.5 7.7 %collective-permute-start.2 = (f32[32,128]{1,0:T(8,128)S(1)}, f32[32,128]{1,0:T(8,128)S(1)}, u32[]{:S(2)}, u32[]{:S(2)}) collective-permute-start(f32[32,128]{1,0:T(8,128)S(1)} %add.12), channel_id=1, source_target_pairs={{0,4},{1,5},{2,6},{3,7},{4,0},{5,1},{6,2},{7,3},{8,12},{9,13},{10,... | collective-permute-start | bytes 49160 | tf_op jit(solution)/shard_map/ppermute | solution.py:433
Sparse Core Ops, SparseCore 0:
  57.3 83.0 reduce-scatter.1
